TPU v7x, 256 devices: a whole 4x4x8 slice. The times are simulated.
256 devices in a mesh: front: 8 (over z), lat: 32 (over y, x, core).
Axes of the slice: x: 4, y: 4, z: 8, core: 2. Of those that a mesh axis runs over, the one named last changes fastest.
Arguments:
- samples: float32 [128, 512, 128], P('front', 'lat'), may hold values from -6 to 6
- reaction: float32 [128, 512], P('front', 'lat'), may hold values from 0.5 to 2
- weight_x: float32 [128, 512], P('front', 'lat'), may hold values from 0.2 to 1
- weight_y: float32 [128, 512], P('front', 'lat'), may hold values from 0.2 to 1
- inverses: float32 [8, 64, 128, 128], P('front', 'lat'), may hold values from -0.3 to 0.4
- couplings: float32 [8, 64, 128, 128], P('front', 'lat'), may hold values from -12 to 12
Outputs:
- whitened: float32 [128, 512, 128], P('front', 'lat')
- gradients: float32 [3, 128, 512], P(None, 'front', 'lat')
All inputs are finite; a program needn't handle non-finite values.
Results may differ from a plain program's by a relative error of at most 0.0003.
Values sent between devices are 32-bit elements; how exact they have to be, the bound alone decides.
No kernel may reach another device: no remote copies, remote signals or barrier semaphores. Data moves between devices by JAX's collectives and lax.ppermute only.
A program may use at most 192 MiB of HBM per device.

v0:
```python
import jax
import jax.numpy as jnp
from jax import lax
from jax.experimental import pallas as pl
from jax.experimental.pallas import tpu as pltpu
from jax.sharding import PartitionSpec as P

F32 = jnp.float32
BF16 = jnp.bfloat16
W = 128


def exchange(array, axis, mask):
    return lax.ppermute(array, axis, [(i, i ^ mask) for i in range(lax.axis_size(axis))])


def call(kernel, outs, *operands, flops=4e7):
    vmem = pl.BlockSpec(memory_space=pltpu.VMEM)
    traffic = sum(a.size * 4 for a in operands) + sum(a.size * 4 for a in outs)
    return pl.pallas_call(
        kernel,
        out_shape=outs,
        in_specs=[vmem] * len(operands),
        out_specs=[vmem] * len(outs),
        compiler_params=pltpu.CompilerParams(vmem_limit_bytes=16 << 20),
        cost_estimate=pl.CostEstimate(flops=int(flops), bytes_accessed=int(traffic), transcendentals=0),
    )(*operands)


def shaped(*dims):
    return jax.ShapeDtypeStruct(dims, F32)


def two(value):
    high = value.astype(BF16)
    return high, (value - high.astype(F32)).astype(BF16)


def three(value):
    high = value.astype(BF16)
    rest = value - high.astype(F32)
    middle = rest.astype(BF16)
    return high, middle, (rest - middle.astype(F32)).astype(BF16)


def product(left, right, contract=1):
    def one(a, b):
        return lax.dot_general(a, b, (((contract,), (0,)), ((), ())), preferred_element_type=F32)

    (ah, al), (bh, bl) = (two(left), two(right))
    return one(ah, bh) + (one(ah, bl) + one(al, bh))


def exact(left, right, contract=1):
    def one(a, b):
        return lax.dot_general(a, b, (((contract,), (0,)), ((), ())), preferred_element_type=F32)

    (ah, am, al), (bh, bm, bl) = (three(left), three(right))
    return one(ah, bh) + ((one(ah, bm) + one(am, bh)) + (one(am, bm) + (one(ah, bl) + one(al, bh))))


def compose(first, second):
    (xa, za), (xb, zb) = (first, second)
    upper = product(jnp.concatenate([xb[:, :W], zb[:, :W]], axis=0), xa)
    tail = jnp.concatenate([xb[:, W:], zb[:, W:]], axis=0)
    upper = jnp.concatenate([upper[:, :W], upper[:, W:] + tail], axis=1)
    return (upper[:W], za + product(xa[:, :W], upper[W:], 0))


def forward(first, xb):
    out = product(xb[:, :W], first)
    return jnp.concatenate([out[:, :W], out[:, W:] + xb[:, W:]], axis=1)


def choose(flag, one, other):
    return tuple(jnp.where(flag, a, b) for a, b in zip(one, other))


def ordered(late, partner, own):
    return (choose(late, partner, own), choose(late, own, partner))


def bit(axis, mask):
    return (lax.axis_index(axis) & mask) != 0


def edges(samples):
    def kernel(s, x_one, x_two, y_one, y_two):
        up = bit("front", 1)
        x_one[...] = jnp.where(up, s[0:1], s[15:16])
        x_two[...] = jnp.where(up, s[15:16], s[0:1])
        right = bit("lat", 1)
        y_one[...] = jnp.where(right, s[:, 0:1], s[:, 15:16])
        y_two[...] = jnp.where(right, s[:, 15:16], s[:, 0:1])

    x, y = (shaped(1, 16, W), shaped(16, 1, W))
    return call(kernel, [x, x, y, y], samples, flops=1)


def inside(axis, before, after):
    at, size = (lax.axis_index(axis), lax.axis_size(axis))
    return (jnp.where(at == 0, 0.0, before), jnp.where(at == size - 1, 0.0, after))


def matrices(inverses, couplings):
    def kernel(inv, cou, steps, total):
        f1 = -exact(inv[0, 0], cou[0, 0])
        f2 = -exact(inv[0, 1], cou[0, 1])
        steps[0] = f1
        steps[1] = f2
        both = exact(f2, f1)
        total[0] = both
        total[1] = exact(f1, f1 + exact(f2, both, 0), 0)

    return call(kernel, [shaped(2, W, W), shaped(2, W, W)], inverses, couplings, flops=3e7)


def sources(samples, halo, reaction, weight_x, weight_y, inverses, steps, total):
    def kernel(s, x1, x2, y1, y2, re, wx, wy, inv, st, to, lapx, lapy, local, element):
        v = s[...]
        xm, xp = choose(bit("front", 1), (x1[...], x2[...]), (x2[...], x1[...]))
        ym, yp = choose(bit("lat", 1), (y1[...], y2[...]), (y2[...], y1[...]))
        xm, xp = inside("front", xm, xp)
        ym, yp = inside("lat", ym, yp)
        lx = 2.0 * v - jnp.concatenate([xm, v[:-1]], axis=0) - jnp.concatenate([v[1:], xp], axis=0)
        ly = 2.0 * v - jnp.concatenate([ym, v[:, :-1]], axis=1) - jnp.concatenate([v[:, 1:], yp], axis=1)
        lapx[...] = lx
        lapy[...] = ly
        r = re[...][:, :, None] * v + wx[...][:, :, None] * lx + wy[...][:, :, None] * ly
        r = r.reshape(2, W, W)
        b1 = exact(inv[0, 0], r[0])
        b2 = exact(inv[0, 1], r[1])
        f1, f2 = (st[0], st[1])
        v2 = exact(f2, b1) + b2
        local[0] = b1
        local[1] = b2
        element[0] = jnp.concatenate([to[0], v2], axis=1)
        h1 = exact(f1, b1 + exact(f2, v2, 0), 0)
        element[1] = jnp.concatenate([to[1], h1], axis=1)

    tile, pair = (shaped(16, 16, W), shaped(2, W, W))
    outs = [tile, tile, pair, shaped(2, W, 2 * W)]
    return call(kernel, outs, samples, *halo, reaction, weight_x, weight_y, inverses, steps, total)


def pair_up(element, partner):
    def kernel(e, p, out, mine):
        late = bit("lat", 1)
        x, z = compose(*ordered(late, (p[0], p[1]), (e[0], e[1])))
        out[0] = x
        out[1] = z
        mine[...] = jnp.where(late, z, x)

    return call(kernel, [shaped(2, W, 2 * W), shaped(W, 2 * W)], element, partner)


def start_sides(partner):
    def kernel(p, before, after):
        late = bit("lat", 1)
        row = lax.broadcasted_iota(jnp.int32, (W, 2 * W), 0)
        col = lax.broadcasted_iota(jnp.int32, (W, 2 * W), 1)
        eye = jnp.where(row == col, 1.0, 0.0).astype(F32)
        before[...] = jnp.where(late, p[0], eye)
        after[0] = jnp.where(late, eye, p[0])
        after[1] = jnp.where(late, 0.0, p[1])

    return call(kernel, [shaped(W, 2 * W), shaped(2, W, 2 * W)], partner, flops=1)


def whole(got, other):
    return choose(bit("lat", 1), (other[...], got[...]), (got[...], other[...]))


def level(element, axis, mask, final):
    def kernel(e, g, o, earlier_sides, out, mine):
        late = bit(axis, mask)
        x, z = compose(*ordered(late, whole(g, o), (e[0], e[1])))
        out[0] = x
        out[1] = z
        odd = bit("lat", 1)
        if final:
            mine[...] = jnp.where(bit(*final), jnp.where(odd, z[:, W:], z[:, :W]), x[:, W:])
        else:
            mine[...] = jnp.where(odd, z, x)

    sent = shaped(W, W) if final else shaped(W, 2 * W)
    return lambda got, other, done: call(kernel, [shaped(2, W, 2 * W), sent], element, got, other, done)


def sides(before, after, got, other, axis, mask):
    def kernel(b, a, g, o, before_out, after_out):
        late = bit(axis, mask)
        px, pz = whole(g, o)

        @pl.when(late)
        def _():
            before_out[...] = forward(px, b[...])
            after_out[...] = a[...]

        @pl.when(jnp.logical_not(late))
        def _():
            before_out[...] = b[...]
            x, z = compose((a[0], a[1]), (px, pz))
            after_out[0] = x
            after_out[1] = z

    return call(kernel, [shaped(W, 2 * W), shaped(2, W, 2 * W)], before, after, got, other)


def respond(before, after, inverses, couplings, local, steps, axis, mask):
    def kernel(b, a, inv, cou, loc, st, out):
        late = bit(axis, mask)
        tail = jnp.concatenate
        none = jnp.zeros((W, W), F32)
        incoming = tail([jnp.where(late, b[:, :W], 0.0), b[:, W:]], axis=1)
        y1 = tail([none, loc[0]], axis=1) + exact(st[0], incoming)
        y2 = tail([none, loc[1]], axis=1) + exact(st[1], y1)
        back = tail([jnp.where(late, 0.0, a[0, :, :W].T), a[1, :, W:]], axis=1)
        x2 = exact(inv[0, 1], y2 + back + exact(a[1, :, :W], y2), 0)
        out[0] = exact(inv[0, 0], y1 - exact(cou[0, 1], x2, 0), 0)
        out[1] = x2

    return call(kernel, [shaped(2, W, 2 * W)], before, after, inverses, couplings, local, steps, flops=1e8)[0]


def finish(axis, mask, element, got, other, response, samples, lapx, lapy):
    def kernel(e, g, o, resp, s, lx, ly, white, grad):
        late = bit(axis, mask)
        odd = bit("lat", 1)
        matrix, vector = choose(odd, (o[...], g[...]), (g[...], o[...]))
        reach = vector + product(matrix, e[0, :, W:])
        comes = jnp.where(late, g[...], reach)
        r = resp[...].reshape(2 * W, 2 * W)
        w = (r[:, W:] + product(r[:, :W], comes)).reshape(16, 16, W)
        white[...] = w
        grad[0] = jnp.sum(w * s[...], axis=2) * (1.0 / W)
        grad[1] = jnp.sum(w * lx[...], axis=2) * (1.0 / W)
        grad[2] = jnp.sum(w * ly[...], axis=2) * (1.0 / W)

    outs = [shaped(16, 16, W), shaped(3, 16, 16)]
    return call(kernel, outs, element, got, other, response, samples, lapx, lapy)


LEVELS = (
    ("lat", 2, 2),
    ("lat", 4, 6),
    ("lat", 8, 8),
    ("lat", 16, 24),
    ("front", 1, 1),
    ("front", 2, 2),
)
TOP = ("front", 4, 6)


def body(samples, reaction, weight_x, weight_y, inverses, couplings):
    x_one, x_two, y_one, y_two = edges(samples)
    halo = []
    for axis, one, two_ in (("front", x_one, x_two), ("lat", y_one, y_two)):
        size = lax.axis_size(axis)
        odd = [(i, (i + 1) % size) for i in range(1, size, 2)]
        halo += [exchange(one, axis, 1), lax.ppermute(two_, axis, odd + [(j, i) for i, j in odd])]
    steps, total = matrices(inverses, couplings)
    lapx, lapy, local, element = sources(
        samples, halo, reaction, weight_x, weight_y, inverses, steps, total
    )
    partner = exchange(element, "lat", 1)
    element, mine = pair_up(element, partner)
    before, after = start_sides(partner)
    for at, (axis, mask, away) in enumerate(LEVELS):
        got = exchange(mine, axis, away)
        other = exchange(got, "lat", 1)
        final = TOP[:2] if at == len(LEVELS) - 1 else None
        element, mine = level(element, axis, mask, final)(got, other, before)
        before, after = sides(before, after, got, other, axis, mask)
    response = respond(before, after, inverses, couplings, local, steps, *TOP[:2])
    got = exchange(mine, TOP[0], TOP[2])
    other = exchange(got, "lat", 1)
    return tuple(finish(*TOP[:2], element, got, other, response, samples, lapx, lapy))


def solution(mesh):
    placed = (
        P("front", "lat", None),
        P("front", "lat"),
        P("front", "lat"),
        P("front", "lat"),
        P("front", "lat", None, None),
        P("front", "lat", None, None),
    )
    return jax.shard_map(
        body,
        mesh=mesh,
        in_specs=placed,
        out_specs=(P("front", "lat", None), P(None, "front", "lat")),
        check_vma=False,
    )
```

profile of v0, /device:TPU:1, one launch (start us, length us, event | category | flops | bytes accessed | tf_op | source)
XLA Modules:
  0.0 81.9 jit_solution(1183546406381983251)
XLA Ops:
  0.6 0.0 copy-start
  0.6 0.0 copy-start.1
  0.7 0.9 %copy-done.1 = f32[16,16,128]{2,1,0:T(8,128)S(1)} copy-done((f32[16,16,128]{2,1,0:T(8,128)S(1)}, f32[16,16,128]{2,1,0:T(8,128)}, u32[]{:S(2)}) %copy-start.1) | copy-done | bytes 131096
  1.6 2.6 %collective-permute-start = (f32[1,16,128]{2,1,0:T(8,128)S(1)}, f32[1,16,128]{2,1,0:T(8,128)S(1)}, u32[]{:S(2)}, u32[]{:S(2)}) collective-permute-start(f32[1,16,128]{2,1,0:T(8,128)S(1)} %get-tuple-element.40), channel_id=1, source_target_pairs={{0,32},{32,0},{64,96},{96,64},{128,160},{160,128},{192,224},{224,1... | collective-permute-start | bytes 24584 | tf_op jit(solution)/shard_map/ppermute | solution.py:14
  4.2 4.7 %collective-permute-start.1 = (f32[1,16,128]{2,1,0:T(8,128)S(1)}, f32[1,16,128]{2,1,0:T(8,128)S(1)}, u32[]{:S(2)}, u32[]{:S(2)}) collective-permute-start(f32[1,16,128]{2,1,0:T(8,128)S(1)} %get-tuple-element.41), channel_id=1, source_target_pairs={{32,64},{96,128},{160,192},{224,0},{64,32},{128,96},{192,160},{0,2... | collective-permute-start | bytes 24584 | tf_op jit(solution)/shard_map/ppermute | solution.py:261
  8.8 1.2 %collective-permute-start.2 = (f32[16,1,128]{2,1,0:T(1,128)S(1)}, f32[16,1,128]{2,1,0:T(1,128)S(1)}, u32[]{:S(2)}, u32[]{:S(2)}) collective-permute-start(f32[16,1,128]{2,1,0:T(1,128)S(1)} %get-tuple-element.42), channel_id=1, source_target_pairs={{0,1},{1,0},{2,3},{3,2},{4,5},{5,4},{6,7},{7,6},{8,9},{9,8},{10,11... | collective-permute-start | bytes 24584 | tf_op jit(solution)/shard_map/ppermute | solution.py:14
  10.1 1.1 %collective-permute-start.3 = (f32[16,1,128]{2,1,0:T(1,128)S(1)}, f32[16,1,128]{2,1,0:T(1,128)S(1)}, u32[]{:S(2)}, u32[]{:S(2)}) collective-permute-start(f32[16,1,128]{2,1,0:T(1,128)S(1)} %get-tuple-element.43), channel_id=1, source_target_pairs={{1,2},{3,4},{5,6},{7,8},{9,10},{11,12},{13,14},{15,16},{17,18},{19... | collective-permute-start | bytes 24584 | tf_op jit(solution)/shard_map/ppermute | solution.py:261
  11.2 0.0 copy-done
  11.2 0.9 %copy-done.3 = f32[1,2,128,128]{3,2,1,0:T(8,128)S(1)} copy-done((f32[1,2,128,128]{3,2,1,0:T(8,128)S(1)}, f32[1,2,128,128]{3,2,1,0:T(8,128)}, u32[]{:S(2)}) %copy-start.3) | copy-done | bytes 131096
  12.1 0.9 %shard_map.78 = (f32[2,128,128]{2,1,0:T(8,128)S(1)}, f32[2,128,128]{2,1,0:T(8,128)S(1)}) custom-call(f32[1,2,128,128]{3,2,1,0:T(8,128)S(1)} %copy-done, f32[1,2,128,128]{3,2,1,0:T(8,128)S(1)} %copy-done.3), custom_call_target="tpu_custom_call" | custom-call | flops 30000000 | bytes 524288 | tf_op jit(solution)/shard_map/pallas_call | solution.py:20
  13.0 0.0 collective-permute-done.x1
  13.0 0.0 collective-permute-done.1.x2
  13.1 0.0 collective-permute-done.2.y1
  13.1 0.1 collective-permute-done.3.y2
  13.1 0.0 copy-done.5
  13.1 0.0 copy-done.7
  13.1 1.0 %shard_map.79 = (f32[16,16,128]{2,1,0:T(8,128)S(1)}, f32[16,16,128]{2,1,0:T(8,128)S(1)}, f32[2,128,128]{2,1,0:T(8,128)S(1)}, f32[2,128,256]{2,1,0:T(8,128)S(1)}) custom-call(f32[16,16,128]{2,1,0:T(8,128)S(1)} %copy-done.1, f32[1,16,128]{2,1,0:T(8,128)S(1)} %collective-permute-done.x1, f32[1,16,128]{2,1,0:T(8,128)S(1)} %collective-permute-done.1.x2, ...), custom_call_target="tpu_custom_call" | custom-call | flops 40000000 | bytes 1215488 | tf_op jit(solution)/shard_map/pallas_call | solution.py:20
  14.1 4.3 %collective-permute-start.4 = (f32[2,128,256]{2,1,0:T(8,128)S(1)}, f32[2,128,256]{2,1,0:T(8,128)S(1)}, u32[]{:S(2)}, u32[]{:S(2)}) collective-permute-start(f32[2,128,256]{2,1,0:T(8,128)S(1)} %get-tuple-element.46.e), channel_id=1, source_target_pairs={{0,1},{1,0},{2,3},{3,2},{4,5},{5,4},{6,7},{7,6},{8,9},{9,8},{10,11... | collective-permute-start | bytes 786440 | tf_op jit(solution)/shard_map/ppermute | solution.py:14
  18.4 1.2 %collective-permute-done.4.p = f32[2,128,256]{2,1,0:T(8,128)S(1)} collective-permute-done((f32[2,128,256]{2,1,0:T(8,128)S(1)}, f32[2,128,256]{2,1,0:T(8,128)S(1)}, u32[]{:S(2)}, u32[]{:S(2)}) %collective-permute-start.4) | collective-permute-done | bytes 262176 | tf_op jit(solution)/shard_map/ppermute | solution.py:14
  19.6 0.5 shard_map.80
  20.1 0.1 collective-permute-start.5
  20.2 4.7 %collective-permute-done.5.g = f32[128,256]{1,0:T(8,128)S(1)} collective-permute-done((f32[128,256]{1,0:T(8,128)S(1)}, f32[128,256]{1,0:T(8,128)S(1)}, u32[]{:S(2)}, u32[]{:S(2)}) %collective-permute-start.5) | collective-permute-done | bytes 131104 | tf_op jit(solution)/shard_map/ppermute | solution.py:14
  24.9 1.2 %collective-permute-start.6 = (f32[128,256]{1,0:T(8,128)S(1)}, f32[128,256]{1,0:T(8,128)S(1)}, u32[]{:S(2)}, u32[]{:S(2)}) collective-permute-start(f32[128,256]{1,0:T(8,128)S(1)} %collective-permute-done.5.g), channel_id=1, source_target_pairs={{0,1},{1,0},{2,3},{3,2},{4,5},{5,4},{6,7},{7,6},{8,9},{9,8},{10,11... | collective-permute-start | bytes 393224 | tf_op jit(solution)/shard_map/ppermute | solution.py:14
  26.1 0.9 %collective-permute-done.6.o = f32[128,256]{1,0:T(8,128)S(1)} collective-permute-done((f32[128,256]{1,0:T(8,128)S(1)}, f32[128,256]{1,0:T(8,128)S(1)}, u32[]{:S(2)}, u32[]{:S(2)}) %collective-permute-start.6) | collective-permute-done | bytes 131104 | tf_op jit(solution)/shard_map/ppermute | solution.py:14
  27.1 0.5 shard_map.82
  27.6 0.9 %collective-permute-start.7 = (f32[128,256]{1,0:T(8,128)S(1)}, f32[128,256]{1,0:T(8,128)S(1)}, u32[]{:S(2)}, u32[]{:S(2)}) collective-permute-start(f32[128,256]{1,0:T(8,128)S(1)} %get-tuple-element.51), channel_id=1, source_target_pairs={{0,6},{1,7},{2,4},{3,5},{4,2},{5,3},{6,0},{7,1},{8,14},{9,15},{10,... | collective-permute-start | bytes 393224 | tf_op jit(solution)/shard_map/ppermute | solution.py:14
  28.5 5.1 %collective-permute-done.7.g = f32[128,256]{1,0:T(8,128)S(1)} collective-permute-done((f32[128,256]{1,0:T(8,128)S(1)}, f32[128,256]{1,0:T(8,128)S(1)}, u32[]{:S(2)}, u32[]{:S(2)}) %collective-permute-start.7) | collective-permute-done | bytes 131104 | tf_op jit(solution)/shard_map/ppermute | solution.py:14
  33.6 1.2 %collective-permute-start.8 = (f32[128,256]{1,0:T(8,128)S(1)}, f32[128,256]{1,0:T(8,128)S(1)}, u32[]{:S(2)}, u32[]{:S(2)}) collective-permute-start(f32[128,256]{1,0:T(8,128)S(1)} %collective-permute-done.7.g), channel_id=1, source_target_pairs={{0,1},{1,0},{2,3},{3,2},{4,5},{5,4},{6,7},{7,6},{8,9},{9,8},{10,11... | collective-permute-start | bytes 393224 | tf_op jit(solution)/shard_map/ppermute | solution.py:14
  34.8 0.5 shard_map.83
  35.4 0.4 collective-permute-done.8.o
  35.8 0.5 shard_map.84
  36.3 0.1 collective-permute-start.9
  36.4 4.7 %collective-permute-done.9.g = f32[128,256]{1,0:T(8,128)S(1)} collective-permute-done((f32[128,256]{1,0:T(8,128)S(1)}, f32[128,256]{1,0:T(8,128)S(1)}, u32[]{:S(2)}, u32[]{:S(2)}) %collective-permute-start.9) | collective-permute-done | bytes 131104 | tf_op jit(solution)/shard_map/ppermute | solution.py:14
  41.1 1.2 %collective-permute-start.10 = (f32[128,256]{1,0:T(8,128)S(1)}, f32[128,256]{1,0:T(8,128)S(1)}, u32[]{:S(2)}, u32[]{:S(2)}) collective-permute-start(f32[128,256]{1,0:T(8,128)S(1)} %collective-permute-done.9.g), channel_id=1, source_target_pairs={{0,1},{1,0},{2,3},{3,2},{4,5},{5,4},{6,7},{7,6},{8,9},{9,8},{10,11... | collective-permute-start | bytes 393224 | tf_op jit(solution)/shard_map/ppermute | solution.py:14
  42.3 0.5 shard_map.85
  42.9 0.4 collective-permute-done.10.o
  43.3 0.5 shard_map.86
  43.8 2.1 %collective-permute-start.11 = (f32[128,256]{1,0:T(8,128)S(1)}, f32[128,256]{1,0:T(8,128)S(1)}, u32[]{:S(2)}, u32[]{:S(2)}) collective-permute-start(f32[128,256]{1,0:T(8,128)S(1)} %get-tuple-element.59), channel_id=1, source_target_pairs={{0,24},{1,25},{2,26},{3,27},{4,28},{5,29},{6,30},{7,31},{8,16},{9,... | collective-permute-start | bytes 393224 | tf_op jit(solution)/shard_map/ppermute | solution.py:14
  46.0 3.9 %collective-permute-done.11.g = f32[128,256]{1,0:T(8,128)S(1)} collective-permute-done((f32[128,256]{1,0:T(8,128)S(1)}, f32[128,256]{1,0:T(8,128)S(1)}, u32[]{:S(2)}, u32[]{:S(2)}) %collective-permute-start.11) | collective-permute-done | bytes 131104 | tf_op jit(solution)/shard_map/ppermute | solution.py:14
  49.9 1.2 %collective-permute-start.12 = (f32[128,256]{1,0:T(8,128)S(1)}, f32[128,256]{1,0:T(8,128)S(1)}, u32[]{:S(2)}, u32[]{:S(2)}) collective-permute-start(f32[128,256]{1,0:T(8,128)S(1)} %collective-permute-done.11.g), channel_id=1, source_target_pairs={{0,1},{1,0},{2,3},{3,2},{4,5},{5,4},{6,7},{7,6},{8,9},{9,8},{10,11... | collective-permute-start | bytes 393224 | tf_op jit(solution)/shard_map/ppermute | solution.py:14
  51.1 0.5 shard_map.87
  51.6 0.4 collective-permute-done.12.o
  52.0 0.5 shard_map.88
  52.6 0.1 collective-permute-start.13
  52.7 4.7 %collective-permute-done.13.g = f32[128,256]{1,0:T(8,128)S(1)} collective-permute-done((f32[128,256]{1,0:T(8,128)S(1)}, f32[128,256]{1,0:T(8,128)S(1)}, u32[]{:S(2)}, u32[]{:S(2)}) %collective-permute-start.13) | collective-permute-done | bytes 131104 | tf_op jit(solution)/shard_map/ppermute | solution.py:14
  57.4 1.2 %collective-permute-start.14 = (f32[128,256]{1,0:T(8,128)S(1)}, f32[128,256]{1,0:T(8,128)S(1)}, u32[]{:S(2)}, u32[]{:S(2)}) collective-permute-start(f32[128,256]{1,0:T(8,128)S(1)} %collective-permute-done.13.g), channel_id=1, source_target_pairs={{0,1},{1,0},{2,3},{3,2},{4,5},{5,4},{6,7},{7,6},{8,9},{9,8},{10,11... | collective-permute-start | bytes 393224 | tf_op jit(solution)/shard_map/ppermute | solution.py:14
  58.6 0.7 shard_map.89
  59.3 0.3 collective-permute-done.14.o
  59.6 0.5 shard_map.90
  60.1 0.5 collective-permute-start.15
  60.6 8.4 %collective-permute-done.15.g = f32[128,256]{1,0:T(8,128)S(1)} collective-permute-done((f32[128,256]{1,0:T(8,128)S(1)}, f32[128,256]{1,0:T(8,128)S(1)}, u32[]{:S(2)}, u32[]{:S(2)}) %collective-permute-start.15) | collective-permute-done | bytes 131104 | tf_op jit(solution)/shard_map/ppermute | solution.py:14
  69.1 0.5 collective-permute-start.16
  69.5 0.5 shard_map.91
  70.1 0.4 collective-permute-done.16.o
  70.5 0.5 shard_map.92
  71.1 0.1 collective-permute-start.17
  71.2 5.2 %collective-permute-done.17.g = f32[128,128]{1,0:T(8,128)S(1)} collective-permute-done((f32[128,128]{1,0:T(8,128)S(1)}, f32[128,128]{1,0:T(8,128)S(1)}, u32[]{:S(2)}, u32[]{:S(2)}) %collective-permute-start.17) | collective-permute-done | bytes 65568 | tf_op jit(solution)/shard_map/ppermute | solution.py:14
  76.4 1.5 %collective-permute-start.18 = (f32[128,128]{1,0:T(8,128)S(1)}, f32[128,128]{1,0:T(8,128)S(1)}, u32[]{:S(2)}, u32[]{:S(2)}) collective-permute-start(f32[128,128]{1,0:T(8,128)S(1)} %collective-permute-done.17.g), channel_id=1, source_target_pairs={{0,1},{1,0},{2,3},{3,2},{4,5},{5,4},{6,7},{7,6},{8,9},{9,8},{10,11... | collective-permute-start | bytes 196616 | tf_op jit(solution)/shard_map/ppermute | solution.py:14
  77.9 0.5 shard_map.93
  78.4 0.4 copy-done.4
  78.8 1.9 %shard_map.94.resp = f32[2,128,256]{2,1,0:T(8,128)S(1)} custom-call(f32[128,256]{1,0:T(8,128)S(1)} %get-tuple-element.73.b, f32[2,128,256]{2,1,0:T(8,128)S(1)} %get-tuple-element.74.a, f32[1,2,128,128]{3,2,1,0:T(8,128)S(1)} %copy-done, f32[1,2,128,128]{3,2,1,0:T(8,128)S(1)} %copy-done.4, f32[2,128,128]{2,1,0:T(8,128)S(1)} %get-tuple-element.75.loc, ...), custom_call_target="tpu_custom_call" | custom-call | flops 100000000 | bytes 1179648 | tf_op jit(solution)/shard_map/pallas_call | solution.py:20
  80.7 0.0 collective-permute-done.18.o
  80.7 0.0 copy-done.2
  80.8 1.1 %shard_map.95 = (f32[16,16,128]{2,1,0:T(8,128)}, f32[3,16,16]{2,1,0:T(8,128)}) custom-call(f32[2,128,256]{2,1,0:T(8,128)S(1)} %get-tuple-element.70.e, f32[128,128]{1,0:T(8,128)S(1)} %collective-permute-done.17.g, f32[128,128]{1,0:T(8,128)S(1)} %collective-permute-done.18.o, f32[2,128,256]{2,1,0:T(8,128)S(1)} %shard_map.94.resp, ...), custom_call_target="tpu_custom_call" | custom-call | flops 40000000 | bytes 1182720 | tf_op jit(solution)/shard_map/pallas_call | solution.py:20
  (9 shorter events, 0.1 us)
Async XLA Ops:
  0.6 10.5 %copy-start = (f32[1,2,128,128]{3,2,1,0:T(8,128)S(1)}, f32[1,2,128,128]{3,2,1,0:T(8,128)}, u32[]{:S(2)}) copy-start(f32[1,2,128,128]{3,2,1,0:T(8,128)} %inv.5) | copy-start | bytes 393220
  0.6 0.9 %copy-start.1 = (f32[16,16,128]{2,1,0:T(8,128)S(1)}, f32[16,16,128]{2,1,0:T(8,128)}, u32[]{:S(2)}) copy-start(f32[16,16,128]{2,1,0:T(8,128)} %s.5) | copy-start | bytes 393220
  1.6 11.4 %collective-permute-start = (f32[1,16,128]{2,1,0:T(8,128)S(1)}, f32[1,16,128]{2,1,0:T(8,128)S(1)}, u32[]{:S(2)}, u32[]{:S(2)}) collective-permute-start(f32[1,16,128]{2,1,0:T(8,128)S(1)} %get-tuple-element.40), channel_id=1, source_target_pairs={{0,32},{32,0},{64,96},{96,64},{128,160},{160,128},{192,224},{224,1... | collective-permute-start | bytes 24584 | tf_op jit(solution)/shard_map/ppermute | solution.py:14
  4.2 8.9 %collective-permute-start.1 = (f32[1,16,128]{2,1,0:T(8,128)S(1)}, f32[1,16,128]{2,1,0:T(8,128)S(1)}, u32[]{:S(2)}, u32[]{:S(2)}) collective-permute-start(f32[1,16,128]{2,1,0:T(8,128)S(1)} %get-tuple-element.41), channel_id=1, source_target_pairs={{32,64},{96,128},{160,192},{224,0},{64,32},{128,96},{192,160},{0,2... | collective-permute-start | bytes 24584 | tf_op jit(solution)/shard_map/ppermute | solution.py:261
  8.8 4.2 %collective-permute-start.2 = (f32[16,1,128]{2,1,0:T(1,128)S(1)}, f32[16,1,128]{2,1,0:T(1,128)S(1)}, u32[]{:S(2)}, u32[]{:S(2)}) collective-permute-start(f32[16,1,128]{2,1,0:T(1,128)S(1)} %get-tuple-element.42), channel_id=1, source_target_pairs={{0,1},{1,0},{2,3},{3,2},{4,5},{5,4},{6,7},{7,6},{8,9},{9,8},{10,11... | collective-permute-start | bytes 24584 | tf_op jit(solution)/shard_map/ppermute | solution.py:14
  10.1 3.1 %collective-permute-start.3 = (f32[16,1,128]{2,1,0:T(1,128)S(1)}, f32[16,1,128]{2,1,0:T(1,128)S(1)}, u32[]{:S(2)}, u32[]{:S(2)}) collective-permute-start(f32[16,1,128]{2,1,0:T(1,128)S(1)} %get-tuple-element.43), channel_id=1, source_target_pairs={{1,2},{3,4},{5,6},{7,8},{9,10},{11,12},{13,14},{15,16},{17,18},{19... | collective-permute-start | bytes 24584 | tf_op jit(solution)/shard_map/ppermute | solution.py:261
  11.2 0.9 %copy-start.3 = (f32[1,2,128,128]{3,2,1,0:T(8,128)S(1)}, f32[1,2,128,128]{3,2,1,0:T(8,128)}, u32[]{:S(2)}) copy-start(f32[1,2,128,128]{3,2,1,0:T(8,128)} %cou.3) | copy-start | bytes 393220
  12.1 1.1 %copy-start.5 = (f32[16,16]{1,0:T(8,128)S(1)}, f32[16,16]{1,0:T(8,128)}, u32[]{:S(2)}) copy-start(f32[16,16]{1,0:T(8,128)} %re.1) | copy-start | bytes 3076
  12.1 1.1 %copy-start.6 = (f32[16,16]{1,0:T(8,128)S(1)}, f32[16,16]{1,0:T(8,128)}, u32[]{:S(2)}) copy-start(f32[16,16]{1,0:T(8,128)} %wx.1) | copy-start | bytes 3076
  12.1 1.1 %copy-start.7 = (f32[16,16]{1,0:T(8,128)S(1)}, f32[16,16]{1,0:T(8,128)}, u32[]{:S(2)}) copy-start(f32[16,16]{1,0:T(8,128)} %wy.1) | copy-start | bytes 3076
  14.1 5.4 %collective-permute-start.4 = (f32[2,128,256]{2,1,0:T(8,128)S(1)}, f32[2,128,256]{2,1,0:T(8,128)S(1)}, u32[]{:S(2)}, u32[]{:S(2)}) collective-permute-start(f32[2,128,256]{2,1,0:T(8,128)S(1)} %get-tuple-element.46.e), channel_id=1, source_target_pairs={{0,1},{1,0},{2,3},{3,2},{4,5},{5,4},{6,7},{7,6},{8,9},{9,8},{10,11... | collective-permute-start | bytes 786440 | tf_op jit(solution)/shard_map/ppermute | solution.py:14
  20.1 4.8 %collective-permute-start.5 = (f32[128,256]{1,0:T(8,128)S(1)}, f32[128,256]{1,0:T(8,128)S(1)}, u32[]{:S(2)}, u32[]{:S(2)}) collective-permute-start(f32[128,256]{1,0:T(8,128)S(1)} %get-tuple-element.48), channel_id=1, source_target_pairs={{0,2},{1,3},{2,0},{3,1},{4,6},{5,7},{6,4},{7,5},{8,10},{9,11},{10,... | collective-permute-start | bytes 393224 | tf_op jit(solution)/shard_map/ppermute | solution.py:14
  24.9 2.2 %collective-permute-start.6 = (f32[128,256]{1,0:T(8,128)S(1)}, f32[128,256]{1,0:T(8,128)S(1)}, u32[]{:S(2)}, u32[]{:S(2)}) collective-permute-start(f32[128,256]{1,0:T(8,128)S(1)} %collective-permute-done.5.g), channel_id=1, source_target_pairs={{0,1},{1,0},{2,3},{3,2},{4,5},{5,4},{6,7},{7,6},{8,9},{9,8},{10,11... | collective-permute-start | bytes 393224 | tf_op jit(solution)/shard_map/ppermute | solution.py:14
  27.6 6.0 %collective-permute-start.7 = (f32[128,256]{1,0:T(8,128)S(1)}, f32[128,256]{1,0:T(8,128)S(1)}, u32[]{:S(2)}, u32[]{:S(2)}) collective-permute-start(f32[128,256]{1,0:T(8,128)S(1)} %get-tuple-element.51), channel_id=1, source_target_pairs={{0,6},{1,7},{2,4},{3,5},{4,2},{5,3},{6,0},{7,1},{8,14},{9,15},{10,... | collective-permute-start | bytes 393224 | tf_op jit(solution)/shard_map/ppermute | solution.py:14
  33.6 2.2 %collective-permute-start.8 = (f32[128,256]{1,0:T(8,128)S(1)}, f32[128,256]{1,0:T(8,128)S(1)}, u32[]{:S(2)}, u32[]{:S(2)}) collective-permute-start(f32[128,256]{1,0:T(8,128)S(1)} %collective-permute-done.7.g), channel_id=1, source_target_pairs={{0,1},{1,0},{2,3},{3,2},{4,5},{5,4},{6,7},{7,6},{8,9},{9,8},{10,11... | collective-permute-start | bytes 393224 | tf_op jit(solution)/shard_map/ppermute | solution.py:14
  36.3 4.8 %collective-permute-start.9 = (f32[128,256]{1,0:T(8,128)S(1)}, f32[128,256]{1,0:T(8,128)S(1)}, u32[]{:S(2)}, u32[]{:S(2)}) collective-permute-start(f32[128,256]{1,0:T(8,128)S(1)} %get-tuple-element.55), channel_id=1, source_target_pairs={{0,8},{1,9},{2,10},{3,11},{4,12},{5,13},{6,14},{7,15},{8,0},{9,1},... | collective-permute-start | bytes 393224 | tf_op jit(solution)/shard_map/ppermute | solution.py:14
  41.1 2.2 %collective-permute-start.10 = (f32[128,256]{1,0:T(8,128)S(1)}, f32[128,256]{1,0:T(8,128)S(1)}, u32[]{:S(2)}, u32[]{:S(2)}) collective-permute-start(f32[128,256]{1,0:T(8,128)S(1)} %collective-permute-done.9.g), channel_id=1, source_target_pairs={{0,1},{1,0},{2,3},{3,2},{4,5},{5,4},{6,7},{7,6},{8,9},{9,8},{10,11... | collective-permute-start | bytes 393224 | tf_op jit(solution)/shard_map/ppermute | solution.py:14
  43.8 6.0 %collective-permute-start.11 = (f32[128,256]{1,0:T(8,128)S(1)}, f32[128,256]{1,0:T(8,128)S(1)}, u32[]{:S(2)}, u32[]{:S(2)}) collective-permute-start(f32[128,256]{1,0:T(8,128)S(1)} %get-tuple-element.59), channel_id=1, source_target_pairs={{0,24},{1,25},{2,26},{3,27},{4,28},{5,29},{6,30},{7,31},{8,16},{9,... | collective-permute-start | bytes 393224 | tf_op jit(solution)/shard_map/ppermute | solution.py:14
  49.9 2.2 %collective-permute-start.12 = (f32[128,256]{1,0:T(8,128)S(1)}, f32[128,256]{1,0:T(8,128)S(1)}, u32[]{:S(2)}, u32[]{:S(2)}) collective-permute-start(f32[128,256]{1,0:T(8,128)S(1)} %collective-permute-done.11.g), channel_id=1, source_target_pairs={{0,1},{1,0},{2,3},{3,2},{4,5},{5,4},{6,7},{7,6},{8,9},{9,8},{10,11... | collective-permute-start | bytes 393224 | tf_op jit(solution)/shard_map/ppermute | solution.py:14
  52.6 4.8 %collective-permute-start.13 = (f32[128,256]{1,0:T(8,128)S(1)}, f32[128,256]{1,0:T(8,128)S(1)}, u32[]{:S(2)}, u32[]{:S(2)}) collective-permute-start(f32[128,256]{1,0:T(8,128)S(1)} %get-tuple-element.63), channel_id=1, source_target_pairs={{0,32},{32,0},{64,96},{96,64},{128,160},{160,128},{192,224},{224,1... | collective-permute-start | bytes 393224 | tf_op jit(solution)/shard_map/ppermute | solution.py:14
  57.4 2.2 %collective-permute-start.14 = (f32[128,256]{1,0:T(8,128)S(1)}, f32[128,256]{1,0:T(8,128)S(1)}, u32[]{:S(2)}, u32[]{:S(2)}) collective-permute-start(f32[128,256]{1,0:T(8,128)S(1)} %collective-permute-done.13.g), channel_id=1, source_target_pairs={{0,1},{1,0},{2,3},{3,2},{4,5},{5,4},{6,7},{7,6},{8,9},{9,8},{10,11... | collective-permute-start | bytes 393224 | tf_op jit(solution)/shard_map/ppermute | solution.py:14
  60.1 9.0 %collective-permute-start.15 = (f32[128,256]{1,0:T(8,128)S(1)}, f32[128,256]{1,0:T(8,128)S(1)}, u32[]{:S(2)}, u32[]{:S(2)}) collective-permute-start(f32[128,256]{1,0:T(8,128)S(1)} %get-tuple-element.67), channel_id=1, source_target_pairs={{0,64},{32,96},{64,0},{96,32},{128,192},{160,224},{192,128},{224,1... | collective-permute-start | bytes 393224 | tf_op jit(solution)/shard_map/ppermute | solution.py:14
  69.1 1.5 %collective-permute-start.16 = (f32[128,256]{1,0:T(8,128)S(1)}, f32[128,256]{1,0:T(8,128)S(1)}, u32[]{:S(2)}, u32[]{:S(2)}) collective-permute-start(f32[128,256]{1,0:T(8,128)S(1)} %collective-permute-done.15.g), channel_id=1, source_target_pairs={{0,1},{1,0},{2,3},{3,2},{4,5},{5,4},{6,7},{7,6},{8,9},{9,8},{10,11... | collective-permute-start | bytes 393224 | tf_op jit(solution)/shard_map/ppermute | solution.py:14
  71.1 5.3 %collective-permute-start.17 = (f32[128,128]{1,0:T(8,128)S(1)}, f32[128,128]{1,0:T(8,128)S(1)}, u32[]{:S(2)}, u32[]{:S(2)}) collective-permute-start(f32[128,128]{1,0:T(8,128)S(1)} %get-tuple-element.71), channel_id=1, source_target_pairs={{0,192},{32,224},{64,128},{96,160},{128,64},{160,96},{192,0},{224,... | collective-permute-start | bytes 196616 | tf_op jit(solution)/shard_map/ppermute | solution.py:14
  76.4 4.4 %collective-permute-start.18 = (f32[128,128]{1,0:T(8,128)S(1)}, f32[128,128]{1,0:T(8,128)S(1)}, u32[]{:S(2)}, u32[]{:S(2)}) collective-permute-start(f32[128,128]{1,0:T(8,128)S(1)} %collective-permute-done.17.g), channel_id=1, source_target_pairs={{0,1},{1,0},{2,3},{3,2},{4,5},{5,4},{6,7},{7,6},{8,9},{9,8},{10,11... | collective-permute-start | bytes 196616 | tf_op jit(solution)/shard_map/ppermute | solution.py:14
  77.9 0.9 %copy-start.4 = (f32[1,2,128,128]{3,2,1,0:T(8,128)S(1)}, f32[1,2,128,128]{3,2,1,0:T(8,128)}, u32[]{:S(2)}) copy-start(f32[1,2,128,128]{3,2,1,0:T(8,128)} %cou.3) | copy-start | bytes 393220
  78.8 2.0 %copy-start.2 = (f32[16,16,128]{2,1,0:T(8,128)S(1)}, f32[16,16,128]{2,1,0:T(8,128)}, u32[]{:S(2)}) copy-start(f32[16,16,128]{2,1,0:T(8,128)} %s.5) | copy-start | bytes 393220
where the time goes:
time: 82 us; the launch traced here: 81.9 us
  waiting for transfers between devices  41 us (50%)
  starting transfers between devices  25.7 us (31%)
  Pallas kernels  12.1 us (15%)
  local copies, waits for them, and re-layouts  2.22 us (3%)
  between operations  0.88 us (1%)
    ppermute x17, waiting for transfers between devices, exchange(): lax.ppermute(array, axis, [(i, i ^ mask) for i in range(lax.axis_size(axi...  40.9 us
    ppermute x17, starting transfers between devices, exchange(): lax.ppermute(array, axis, [(i, i ^ mask) for i in range(lax.axis_size(axi...  19.9 us
    pallas_call x19, Pallas kernels, call(): pl.pallas_call(kernel, out_shape=outs, in_specs=[vmem] * len(operands), o...  12.1 us
    ppermute x2, starting transfers between devices, body(): lax.ppermute(two_, axis, odd + [(j, i) for i, j in odd])  5.77 us
    unnamed x16, local copies, waits for them, and re-layouts  2.22 us
  transfers between devices with their start and end apart: 19, of which 15 were waited for; matrix products, arithmetic and copies ran while one was open for 0% of the time, Pallas kernels for 8%

commit v1 on v0

v1 whole, which is shorter than its diff:
```python
import jax
import jax.numpy as jnp
from jax import lax
from jax.experimental import pallas as pl
from jax.experimental.pallas import tpu as pltpu
from jax.sharding import PartitionSpec as P

F32 = jnp.float32
BF16 = jnp.bfloat16
W = 128


EVERY = ("front", "lat")


def count():
    return lax.axis_size("front") * lax.axis_size("lat")


def send(array, pairs):
    return lax.ppermute(array, EVERY, pairs)


def swap(array):
    return send(array, [(i, i ^ 1) for i in range(count())])


def call(kernel, outs, *operands, flops=4e7, same=None):
    vmem = pl.BlockSpec(memory_space=pltpu.VMEM)
    traffic = sum(a.size * 4 for a in operands) + sum(a.size * 4 for a in outs)
    return pl.pallas_call(
        kernel,
        out_shape=outs,
        in_specs=[vmem] * len(operands),
        out_specs=[vmem] * len(outs),
        input_output_aliases=same or {},
        compiler_params=pltpu.CompilerParams(vmem_limit_bytes=16 << 20),
        cost_estimate=pl.CostEstimate(flops=int(flops), bytes_accessed=int(traffic), transcendentals=0),
    )(*operands)


def shaped(*dims):
    return jax.ShapeDtypeStruct(dims, F32)


def two(value):
    high = value.astype(BF16)
    return high, (value - high.astype(F32)).astype(BF16)


def three(value):
    high = value.astype(BF16)
    rest = value - high.astype(F32)
    middle = rest.astype(BF16)
    return high, middle, (rest - middle.astype(F32)).astype(BF16)


def product(left, right, contract=1):
    def one(a, b):
        return lax.dot_general(a, b, (((contract,), (0,)), ((), ())), preferred_element_type=F32)

    (ah, al), (bh, bl) = (two(left), two(right))
    return one(ah, bh) + (one(ah, bl) + one(al, bh))


def exact(left, right, contract=1):
    def one(a, b):
        return lax.dot_general(a, b, (((contract,), (0,)), ((), ())), preferred_element_type=F32)

    (ah, am, al), (bh, bm, bl) = (three(left), three(right))
    return one(ah, bh) + ((one(ah, bm) + one(am, bh)) + (one(am, bm) + (one(ah, bl) + one(al, bh))))


def compose(first, second):
    (xa, za), (xb, zb) = (first, second)
    upper = product(jnp.concatenate([xb[:, :W], zb[:, :W]], axis=0), xa)
    tail = jnp.concatenate([xb[:, W:], zb[:, W:]], axis=0)
    upper = jnp.concatenate([upper[:, :W], upper[:, W:] + tail], axis=1)
    return (upper[:W], za + product(xa[:, :W], upper[W:], 0))


def compose_vectors(fa, maps, a, b):
    out = product(maps, a[:W]) + b
    return out[:W], a[W:] + product(fa, out[W:], 0)


def compose_matrices(a, b):
    out = product(b, a[:W])
    return out[:W], a[W:] + product(a[:W], out[W:], 0)


def forward(first, xb):
    out = product(xb[:, :W], first)
    return jnp.concatenate([out[:, :W], out[:, W:] + xb[:, W:]], axis=1)


def choose(flag, one, other):
    return tuple(jnp.where(flag, a, b) for a, b in zip(one, other))


def place():
    return lax.axis_index("front") * lax.axis_size("lat") + lax.axis_index("lat")


def bit(mask):
    return (place() & mask) != 0


def edges(samples, inverses, couplings):
    def kernel(s, inv, cou, x_one, x_two, y_one, y_two, s_out, inv_out, cou_out, sems):
        pairs = ((s, s_out), (inv, inv_out), (cou, cou_out))
        copies = [pltpu.make_async_copy(a, b, sems.at[i]) for i, (a, b) in enumerate(pairs)]
        for copy in copies:
            copy.start()
        copies[0].wait()
        up = bit(UP)
        x_one[...] = jnp.where(up, s_out[0:1], s_out[15:16])
        x_two[...] = jnp.where(up, s_out[15:16], s_out[0:1])
        right = bit(1)
        y_one[...] = jnp.where(right, s_out[:, 0:1], s_out[:, 15:16])
        y_two[...] = jnp.where(right, s_out[:, 15:16], s_out[:, 0:1])
        copies[1].wait()
        copies[2].wait()

    x, y = (shaped(1, 16, W), shaped(16, 1, W))
    outs = [x, x, y, y] + [shaped(*a.shape) for a in (samples, inverses, couplings)]
    return pl.pallas_call(
        kernel,
        out_shape=outs,
        in_specs=[pl.BlockSpec(memory_space=pltpu.HBM)] * 3,
        out_specs=[pl.BlockSpec(memory_space=pltpu.VMEM)] * len(outs),
        scratch_shapes=[pltpu.SemaphoreType.DMA((3,))],
        compiler_params=pltpu.CompilerParams(vmem_limit_bytes=107 << 19),
        cost_estimate=pl.CostEstimate(flops=1, bytes_accessed=800000, transcendentals=0),
    )(samples, inverses, couplings)


def inside(axis, before, after):
    at, size = (lax.axis_index(axis), lax.axis_size(axis))
    return (jnp.where(at == 0, 0.0, before), jnp.where(at == size - 1, 0.0, after))


def matrices(inverses, couplings, *waits):
    def kernel(inv, cou, *refs):
        steps, total = refs[-2:]
        f1 = -exact(inv[0, 0], cou[0, 0])
        f2 = -exact(inv[0, 1], cou[0, 1])
        steps[0] = f1
        steps[1] = f2
        both = exact(f2, f1)
        total[:W] = both
        total[W:] = exact(f1, f1 + exact(f2, both, 0), 0)

    return call(kernel, [shaped(2, W, W), shaped(2 * W, W)], inverses, couplings, *waits, flops=3e7)


def sources(samples, halo, reaction, weight_x, weight_y, inverses, steps, *waits):
    def kernel(s, x1, x2, y1, y2, re, wx, wy, inv, st, *refs):
        lapx, lapy, local, vectors = refs[-4:]
        v = s[...]
        xm, xp = choose(bit(UP), (x1[...], x2[...]), (x2[...], x1[...]))
        ym, yp = choose(bit(1), (y1[...], y2[...]), (y2[...], y1[...]))
        xm, xp = inside("front", xm, xp)
        ym, yp = inside("lat", ym, yp)
        lx = 2.0 * v - jnp.concatenate([xm, v[:-1]], axis=0) - jnp.concatenate([v[1:], xp], axis=0)
        ly = 2.0 * v - jnp.concatenate([ym, v[:, :-1]], axis=1) - jnp.concatenate([v[:, 1:], yp], axis=1)
        lapx[...] = lx
        lapy[...] = ly
        r = re[...][:, :, None] * v + wx[...][:, :, None] * lx + wy[...][:, :, None] * ly
        r = r.reshape(2, W, W)
        b1 = exact(inv[0, 0], r[0])
        b2 = exact(inv[0, 1], r[1])
        f1, f2 = (st[0], st[1])
        v2 = exact(f2, b1) + b2
        local[0] = b1
        local[1] = b2
        vectors[:W] = v2
        vectors[W:] = exact(f1, b1 + exact(f2, v2, 0), 0)

    tile = shaped(16, 16, W)
    outs = [tile, tile, shaped(2, W, W), shaped(2 * W, W)]
    return call(kernel, outs, samples, *halo, reaction, weight_x, weight_y, inverses, steps, *waits)


def in_chip(total, partner, *waits):
    def kernel(t, p, *refs):
        chip = refs[-1]
        a, b = choose(bit(1), (p[...], t[...]), (t[...], p[...]))
        chip[:W], chip[W:] = compose_matrices(a, b)

    return call(kernel, [shaped(2 * W, W)], total, partner, *waits)[0]


def merge(got, bit_even, bit_odd, even, odd, own, theirs, got_odd=None, last=None, waits=()):
    def kernel(g, ev, od, ow, th, *refs):
        state, block = refs[-2:]

        @pl.when(bit(1))
        def _():
            late = bit(bit_odd)
            vectors = g if got_odd is None else refs[0]
            a, b = choose(late, (vectors[...], od[...]), (od[...], vectors[...]))
            maps_a, maps_b = choose(late, (th[...], ow[...]), (ow[...], th[...]))
            tail = jnp.concatenate
            first = (tail([maps_a[:W], a[:W]], axis=1), tail([maps_a[W:], a[W:]], axis=1))
            second = (tail([maps_b[:W], b[:W]], axis=1), tail([maps_b[W:], b[W:]], axis=1))
            x, z = compose(first, second)
            if last is None:
                block[:W] = x[:, :W]
                block[W:] = z[:, :W]
                state[:W] = x[:, W:]
                state[W:] = z[:, W:]
            else:
                block[: 2 * W] = g[...]
                block[2 * W :] = x[:, W:]
                state[...] = jnp.where(bit(last), z[:, W:], x[:, W:])

        @pl.when(jnp.logical_not(bit(1)))
        def _():
            if last is not None:
                state[...] = ev[W:]
            else:
                late = bit(bit_even)
                a, b = choose(late, (g[...], ev[...]), (ev[...], g[...]))
                state[:W], state[W:] = compose_matrices(a, b)

    outs = [shaped(2 * W, W)] * 3 if last is None else [shaped(2 * W, W), shaped(W, W), shaped(3 * W, W)]
    operands = (got, even, odd, own, theirs) + (() if got_odd is None else (got_odd,)) + tuple(waits)
    return call(kernel, outs, *operands, same={0: 0})


def arrived(array):
    def kernel(a, out):
        pass

    return call(kernel, [shaped(*array.shape)], array, flops=1e10, same={0: 0})[0]


def start_sides(matrices, vectors):
    def kernel(m, v, out):
        odd = bit(1)
        row = lax.broadcasted_iota(jnp.int32, (W, 2 * W), 0)
        col = lax.broadcasted_iota(jnp.int32, (W, 2 * W), 1)
        eye = jnp.where(row == col, 1.0, 0.0).astype(F32)
        x = jnp.concatenate([m[:W], v[:W]], axis=1)
        out[0] = jnp.where(odd, x, eye)
        out[1] = jnp.where(odd, eye, x)
        out[2] = jnp.where(odd, 0.0, jnp.concatenate([m[W:], v[W:]], axis=1))

    return call(kernel, [shaped(3, W, 2 * W)], matrices, vectors, flops=1)[0]


def widen(around, theirs, theirs_swapped, got, got_swapped, mask):
    def kernel(s, te, to, go, ge, out):
        odd = bit(1)
        late = bit(mask)
        m = jnp.where(odd, to[...], te[...])
        v = jnp.where(odd, go[...], ge[: 2 * W])

        @pl.when(late)
        def _():
            out[0] = forward(jnp.concatenate([m[:W], v[:W]], axis=1), s[0])
            out[1:] = s[1:]

        @pl.when(jnp.logical_not(late))
        def _():
            out[0] = s[0]
            later = (jnp.concatenate([m[:W], v[:W]], axis=1), jnp.concatenate([m[W:], v[W:]], axis=1))
            out[1], out[2] = compose((s[1], s[2]), later)

    operands = (around, theirs, theirs_swapped, got, got_swapped)
    return call(kernel, [shaped(3, W, 2 * W)], *operands)[0]


def respond(around, inverses, couplings, local, steps, mask):
    def kernel(ar, inv, cou, loc, st, out):
        late = bit(mask)
        tail = jnp.concatenate
        none = jnp.zeros((W, W), F32)
        incoming = tail([jnp.where(late, ar[0, :, :W], 0.0), ar[0, :, W:]], axis=1)
        y1 = tail([none, loc[0]], axis=1) + product(st[0], incoming)
        y2 = tail([none, loc[1]], axis=1) + product(st[1], y1)
        back = tail([jnp.where(late, 0.0, ar[1, :, :W].T), ar[2, :, W:]], axis=1)
        x2 = product(inv[0, 1], y2 + back + product(ar[2, :, :W], y2), 0)
        out[0] = product(inv[0, 0], y1 - product(cou[0, 1], x2, 0), 0)
        out[1] = x2

    return call(kernel, [shaped(2, W, 2 * W)], around, inverses, couplings, local, steps, flops=1e8)[0]


def arrive(got, swapped, mask, *waits):
    def kernel(g, sw, *refs):
        out = refs[-1]

        @pl.when(bit(1))
        def _():
            out[...] = g[...]

        @pl.when(jnp.logical_not(bit(1)))
        def _():
            out[...] = jnp.where(bit(mask), 0.0, product(g[...], sw[2 * W :]))

    return call(kernel, [shaped(W, W)], got, swapped, *waits)[0]


def finish(comes, sent, response, samples, lapx, lapy):
    def kernel(c, se, resp, s, lx, ly, white, grad):
        v = c[...] + se[...]
        r = resp[...].reshape(2 * W, 2 * W)
        w = (r[:, W:] + product(r[:, :W], v)).reshape(16, 16, W)
        white[...] = w
        grad[0] = jnp.sum(w * s[...], axis=2) * (1.0 / W)
        grad[1] = jnp.sum(w * lx[...], axis=2) * (1.0 / W)
        grad[2] = jnp.sum(w * ly[...], axis=2) * (1.0 / W)

    return call(kernel, [shaped(16, 16, W), shaped(3, 16, 16)], comes, sent, response, samples, lapx, lapy)


LEVELS = ((1, 1), (2, 2), (4, 6), (8, 8), (16, 24), (32, 32), (64, 64), (128, 192))
UP = 32


def body(samples, reaction, weight_x, weight_y, inverses, couplings):
    top = len(LEVELS) - 1
    evens = range(0, count(), 2)
    odds = range(1, count(), 2)
    x_one, x_two, y_one, y_two, samples, inverses, couplings = edges(samples, inverses, couplings)
    halo = []
    for axis, one, other in (("front", x_one, x_two), ("lat", y_one, y_two)):
        size = lax.axis_size(axis)
        pairs = [(i, (i + 1) % size) for i in range(1, size, 2)]
        halo.append(lax.ppermute(one, axis, [(i, i ^ 1) for i in range(size)]))
        halo.append(lax.ppermute(other, axis, pairs + [(j, i) for i, j in pairs]))
    steps, total = matrices(inverses, couplings, x_one)
    other_total = swap(total)
    chip = in_chip(total, other_total, *halo)
    got = arrived(send(chip, [(i, i ^ LEVELS[1][1]) for i in evens]))
    lapx, lapy, local, vectors = sources(
        samples, halo, reaction, weight_x, weight_y, inverses, steps, chip
    )
    other_vectors = swap(vectors)
    got, state, own = merge(
        got, LEVELS[1][0], LEVELS[0][0], chip, vectors, total, other_total, got_odd=other_vectors
    )
    swapped = swap(got)
    around = start_sides(other_total, other_vectors)
    waits = ()
    for at in range(1, top):
        pairs = [(i, i ^ LEVELS[at][1]) for i in odds]
        pairs += [(i, i ^ LEVELS[at + 1][1]) for i in evens if at + 1 < top]
        theirs, theirs_swapped, before = (got, swapped, state)
        got = send(before, pairs)
        last = LEVELS[top][0] if at + 1 == top else None
        got, state, own = merge(
            got, LEVELS[at + 1][0], LEVELS[at][0], before, before, own, theirs_swapped, last=last, waits=waits
        )
        swapped = swap(got if last is None else own)
        waits = (around,)
        around = widen(around, theirs, theirs_swapped, got, swapped, LEVELS[at][0])
    pairs = [(i, i ^ LEVELS[top][1]) for i in range(count()) if i & 1 or i & LEVELS[top][0]]
    got = send(state, pairs)
    response = respond(around, inverses, couplings, local, steps, LEVELS[top][0])
    comes = arrive(got, swapped, LEVELS[top][0], response)
    return tuple(finish(comes, swap(comes), response, samples, lapx, lapy))


def solution(mesh):
    placed = (
        P("front", "lat", None),
        P("front", "lat"),
        P("front", "lat"),
        P("front", "lat"),
        P("front", "lat", None, None),
        P("front", "lat", None, None),
    )
    return jax.shard_map(
        body,
        mesh=mesh,
        in_specs=placed,
        out_specs=(P("front", "lat", None), P(None, "front", "lat")),
        check_vma=False,
    )
```

time: 82 us -> 71.9 us (0.88)
  waiting for transfers between devices: 41 us -> 9.9 us
  starting transfers between devices: 25.7 us -> 48.2 us
  local copies, waits for them, and re-layouts: 2.22 us -> 0.01 us
    ppermute x19 -> x22, waiting for transfers between devices: 41 us -> 9.9 us  [the longest x18 7.41 us: send(): return lax.ppermute(array, EVERY, pairs)]
    ppermute x19 -> x22, starting transfers between devices: 25.7 us -> 48.2 us  [the longest x18 42.7 us: send(): return lax.ppermute(array, EVERY, pairs)]
    unnamed x16 -> x6, local copies, waits for them, and re-layouts: 2.22 us -> 0.01 us
    pallas_call x0 -> x1, Pallas kernels: none -> 1.06 us  [edges(): pl.pallas_call(kernel, out_shape=outs, in_specs=[pl.BlockSpec(memory_spac...]
    pallas_call x19 -> x21, Pallas kernels: 12.1 us -> 11.7 us  [call(): pl.pallas_call(kernel, out_shape=outs, in_specs=[vmem] * len(operands), o...]
  transfers between devices with their start and end apart: 19 -> 22, of which waited for: 15 -> 14; matrix products, arithmetic and copies ran while one was open for 0% -> 0% of each run, Pallas kernels for 8% -> 8%
where the time goes in v1:
time: 71.9 us; the launch traced here: 71.7 us
  starting transfers between devices  48.2 us (67%)
  Pallas kernels  12.7 us (18%)
  waiting for transfers between devices  9.9 us (14%)
  between operations  0.89 us (1%)
    ppermute x18, starting transfers between devices, send(): return lax.ppermute(array, EVERY, pairs)  42.7 us
    pallas_call x21, Pallas kernels, call(): pl.pallas_call(kernel, out_shape=outs, in_specs=[vmem] * len(operands), o...  11.7 us
    ppermute x18, waiting for transfers between devices, send(): return lax.ppermute(array, EVERY, pairs)  7.41 us
    ppermute x2, starting transfers between devices, body(): halo.append(lax.ppermute(other, axis, pairs + [(j, i) for i, j in pairs]))  5.11 us
    ppermute x2, waiting for transfers between devices, body(): halo.append(lax.ppermute(other, axis, pairs + [(j, i) for i, j in pairs]))  1.82 us
  transfers between devices with their start and end apart: 22, of which 14 were waited for; matrix products, arithmetic and copies ran while one was open for 0% of the time, Pallas kernels for 8%

profile of v1, /device:TPU:1, one launch (start us, length us, event | category | flops | bytes accessed | tf_op | source)
XLA Modules:
  0.0 71.7 jit_solution(15186743995818843458)
XLA Ops:
  0.6 1.1 %shard_map.77 = (f32[1,16,128]{2,1,0:T(8,128)S(1)}, f32[1,16,128]{2,1,0:T(8,128)S(1)}, f32[16,1,128]{2,1,0:T(1,128)S(1)}, f32[16,1,128]{2,1,0:T(1,128)S(1)}, f32...) custom-call(f32[16,16,128]{2,1,0:T(8,128)} %s.1, f32[1,2,128,128]{3,2,1,0:T(8,128)} %inv.1, ...), custom_call_target="tpu_custom_call" | custom-call | flops 1 | bytes 800000 | tf_op jit(solution)/shard_map/pallas_call | solution.py:127
  1.7 1.0 %shard_map.78 = (f32[2,128,128]{2,1,0:T(8,128)S(1)}, f32[256,128]{1,0:T(8,128)S(1)}) custom-call(f32[1,2,128,128]{3,2,1,0:T(8,128)S(1)} %get-tuple-element.36.inv, f32[1,2,128,128]{3,2,1,0:T(8,128)S(1)} %get-tuple-element.37.cou, f32[1,16,128]{2,1,0:T(8,128)S(1)} %get-tuple-element.38.refs_0_), custom_call_target="tpu_custom_call" | custom-call | flops 30000000 | bytes 532480 | tf_op jit(solution)/shard_map/pallas_call | solution.py:31
  2.7 3.3 %collective-permute-start = (f32[256,128]{1,0:T(8,128)S(1)}, f32[256,128]{1,0:T(8,128)S(1)}, u32[]{:S(2)}, u32[]{:S(2)}) collective-permute-start(f32[256,128]{1,0:T(8,128)S(1)} %get-tuple-element.39.t.ow), channel_id=1, source_target_pairs={{0,1},{1,0},{2,3},{3,2},{4,5},{5,4},{6,7},{7,6},{8,9},{9,8},{10,11... | collective-permute-start | bytes 393224 | tf_op jit(solution)/shard_map/ppermute | solution.py:21
  6.0 3.9 %collective-permute-start.2 = (f32[1,16,128]{2,1,0:T(8,128)S(1)}, f32[1,16,128]{2,1,0:T(8,128)S(1)}, u32[]{:S(2)}, u32[]{:S(2)}) collective-permute-start(f32[1,16,128]{2,1,0:T(8,128)S(1)} %get-tuple-element.40), channel_id=1, source_target_pairs={{32,64},{96,128},{160,192},{224,0},{64,32},{128,96},{192,160},{0,2... | collective-permute-start | bytes 24584 | tf_op jit(solution)/shard_map/ppermute | solution.py:333
  9.8 0.4 collective-permute-start.3
  10.2 1.2 %collective-permute-start.4 = (f32[16,1,128]{2,1,0:T(1,128)S(1)}, f32[16,1,128]{2,1,0:T(1,128)S(1)}, u32[]{:S(2)}, u32[]{:S(2)}) collective-permute-start(f32[16,1,128]{2,1,0:T(1,128)S(1)} %get-tuple-element.42), channel_id=1, source_target_pairs={{1,2},{3,4},{5,6},{7,8},{9,10},{11,12},{13,14},{15,16},{17,18},{19... | collective-permute-start | bytes 24584 | tf_op jit(solution)/shard_map/ppermute | solution.py:333
  11.4 0.0 collective-permute-start.1
  11.5 0.0 collective-permute-done.2.refs_1_.x2
  11.5 0.0 collective-permute-done.3.refs_2_.y1
  11.5 1.8 %collective-permute-done.4.refs_3_.y2 = f32[16,1,128]{2,1,0:T(1,128)S(1)} collective-permute-done((f32[16,1,128]{2,1,0:T(1,128)S(1)}, f32[16,1,128]{2,1,0:T(1,128)S(1)}, u32[]{:S(2)}, u32[]{:S(2)}) %collective-permute-start.4) | collective-permute-done | bytes 8224 | tf_op jit(solution)/shard_map/ppermute | solution.py:333
  13.3 0.7 collective-permute-done.1.refs_0_.x1
  14.0 0.0 collective-permute-done.p.th.m
  14.0 0.4 shard_map.79.refs_0_.ev
  14.4 0.7 collective-permute-start.5
  15.0 0.0 copy-done
  15.1 1.0 %shard_map.81 = (f32[16,16,128]{2,1,0:T(8,128)S(1)}, f32[16,16,128]{2,1,0:T(8,128)S(1)}, f32[2,128,128]{2,1,0:T(8,128)S(1)}, f32[256,128]{1,0:T(8,128)S(1)}) custom-call(f32[16,16,128]{2,1,0:T(8,128)S(1)} %get-tuple-element.43.s, f32[1,16,128]{2,1,0:T(8,128)S(1)} %collective-permute-done.1.refs_0_.x1, f32[1,16,128]{2,1,0:T(8,128)S(1)} %collective-permute-done.2.refs_1_.x2, ...), custom_call_target="tpu_custom_call" | custom-call | flops 40000000 | bytes 1084416 | tf_op jit(solution)/shard_map/pallas_call | solution.py:31
  16.1 6.6 %collective-permute-start.6 = (f32[256,128]{1,0:T(8,128)S(1)}, f32[256,128]{1,0:T(8,128)S(1)}, u32[]{:S(2)}, u32[]{:S(2)}) collective-permute-start(f32[256,128]{1,0:T(8,128)S(1)} %get-tuple-element.45.od), channel_id=1, source_target_pairs={{0,1},{1,0},{2,3},{3,2},{4,5},{5,4},{6,7},{7,6},{8,9},{9,8},{10,11... | collective-permute-start | bytes 393224 | tf_op jit(solution)/shard_map/ppermute | solution.py:21
  22.6 0.0 collective-permute-done.5.a
  22.6 1.0 %collective-permute-done.6.refs_0_.v = f32[256,128]{1,0:T(8,128)S(1)} collective-permute-done((f32[256,128]{1,0:T(8,128)S(1)}, f32[256,128]{1,0:T(8,128)S(1)}, u32[]{:S(2)}, u32[]{:S(2)}) %collective-permute-start.6) | collective-permute-done | bytes 131104 | tf_op jit(solution)/shard_map/ppermute | solution.py:21
  23.6 0.5 shard_map.82
  24.1 1.8 %collective-permute-start.7 = (f32[256,128]{1,0:T(8,128)S(1)}, f32[256,128]{1,0:T(8,128)S(1)}, u32[]{:S(2)}, u32[]{:S(2)}) collective-permute-start(f32[256,128]{1,0:T(8,128)S(1)} %get-tuple-element.46.ev.od), channel_id=1, source_target_pairs={{1,3},{3,1},{5,7},{7,5},{9,11},{11,9},{13,15},{15,13},{17,19},{19,... | collective-permute-start | bytes 393224 | tf_op jit(solution)/shard_map/ppermute | solution.py:21
  25.9 1.1 %collective-permute-start.8 = (f32[256,128]{1,0:T(8,128)S(1)}, f32[256,128]{1,0:T(8,128)S(1)}, u32[]{:S(2)}, u32[]{:S(2)}) collective-permute-start(f32[256,128]{1,0:T(8,128)S(1)} %get-tuple-element.48.te), channel_id=1, source_target_pairs={{0,1},{1,0},{2,3},{3,2},{4,5},{5,4},{6,7},{7,6},{8,9},{9,8},{10,11... | collective-permute-start | bytes 393224 | tf_op jit(solution)/shard_map/ppermute | solution.py:21
  27.0 1.3 %collective-permute-done.7.g = f32[256,128]{1,0:T(8,128)S(1)} collective-permute-done((f32[256,128]{1,0:T(8,128)S(1)}, f32[256,128]{1,0:T(8,128)S(1)}, u32[]{:S(2)}, u32[]{:S(2)}) %collective-permute-start.7) | collective-permute-done | bytes 131104 | tf_op jit(solution)/shard_map/ppermute | solution.py:21
  28.3 0.0 collective-permute-done.8.th.to
  28.3 0.5 shard_map.83
  28.8 2.7 %collective-permute-start.9 = (f32[256,128]{1,0:T(8,128)S(1)}, f32[256,128]{1,0:T(8,128)S(1)}, u32[]{:S(2)}, u32[]{:S(2)}) collective-permute-start(f32[256,128]{1,0:T(8,128)S(1)} %get-tuple-element.49.ev.od), channel_id=1, source_target_pairs={{1,7},{3,5},{5,3},{7,1},{9,15},{11,13},{13,11},{15,9},{17,23},{19,... | collective-permute-start | bytes 393224 | tf_op jit(solution)/shard_map/ppermute | solution.py:21
  31.5 2.2 %collective-permute-start.10 = (f32[256,128]{1,0:T(8,128)S(1)}, f32[256,128]{1,0:T(8,128)S(1)}, u32[]{:S(2)}, u32[]{:S(2)}) collective-permute-start(f32[256,128]{1,0:T(8,128)S(1)} %get-tuple-element.51.go.te), channel_id=1, source_target_pairs={{0,1},{1,0},{2,3},{3,2},{4,5},{5,4},{6,7},{7,6},{8,9},{9,8},{10,11... | collective-permute-start | bytes 393224 | tf_op jit(solution)/shard_map/ppermute | solution.py:21
  33.7 0.2 collective-permute-done.9.g
  33.9 0.7 %collective-permute-done.10.th.ge.to = f32[256,128]{1,0:T(8,128)S(1)} collective-permute-done((f32[256,128]{1,0:T(8,128)S(1)}, f32[256,128]{1,0:T(8,128)S(1)}, u32[]{:S(2)}, u32[]{:S(2)}) %collective-permute-start.10) | collective-permute-done | bytes 131104 | tf_op jit(solution)/shard_map/ppermute | solution.py:21
  34.7 0.5 shard_map.85
  35.2 1.7 %collective-permute-start.11 = (f32[256,128]{1,0:T(8,128)S(1)}, f32[256,128]{1,0:T(8,128)S(1)}, u32[]{:S(2)}, u32[]{:S(2)}) collective-permute-start(f32[256,128]{1,0:T(8,128)S(1)} %get-tuple-element.52.ev.od), channel_id=1, source_target_pairs={{1,9},{3,11},{5,13},{7,15},{9,1},{11,3},{13,5},{15,7},{17,25},{19,... | collective-permute-start | bytes 393224 | tf_op jit(solution)/shard_map/ppermute | solution.py:21
  36.9 2.8 %collective-permute-start.12 = (f32[256,128]{1,0:T(8,128)S(1)}, f32[256,128]{1,0:T(8,128)S(1)}, u32[]{:S(2)}, u32[]{:S(2)}) collective-permute-start(f32[256,128]{1,0:T(8,128)S(1)} %get-tuple-element.54.go.te), channel_id=1, source_target_pairs={{0,1},{1,0},{2,3},{3,2},{4,5},{5,4},{6,7},{7,6},{8,9},{9,8},{10,11... | collective-permute-start | bytes 393224 | tf_op jit(solution)/shard_map/ppermute | solution.py:21
  39.8 0.5 shard_map.86.refs_0_.s
  40.3 0.0 collective-permute-done.11.g
  40.3 0.4 collective-permute-done.12.th.ge.to
  40.8 0.5 shard_map.87
  41.3 2.3 %collective-permute-start.13 = (f32[256,128]{1,0:T(8,128)S(1)}, f32[256,128]{1,0:T(8,128)S(1)}, u32[]{:S(2)}, u32[]{:S(2)}) collective-permute-start(f32[256,128]{1,0:T(8,128)S(1)} %get-tuple-element.55.ev.od), channel_id=1, source_target_pairs={{1,25},{3,27},{5,29},{7,31},{9,17},{11,19},{13,21},{15,23},{17,9},... | collective-permute-start | bytes 393224 | tf_op jit(solution)/shard_map/ppermute | solution.py:21
  43.6 2.2 %collective-permute-start.14 = (f32[256,128]{1,0:T(8,128)S(1)}, f32[256,128]{1,0:T(8,128)S(1)}, u32[]{:S(2)}, u32[]{:S(2)}) collective-permute-start(f32[256,128]{1,0:T(8,128)S(1)} %get-tuple-element.57.go.te), channel_id=1, source_target_pairs={{0,1},{1,0},{2,3},{3,2},{4,5},{5,4},{6,7},{7,6},{8,9},{9,8},{10,11... | collective-permute-start | bytes 393224 | tf_op jit(solution)/shard_map/ppermute | solution.py:21
  45.8 0.5 shard_map.88.refs_0_.s
  46.4 0.1 collective-permute-done.13.g
  46.4 0.4 collective-permute-done.14.th.ge.to
  46.8 0.7 shard_map.89
  47.5 1.7 %collective-permute-start.15 = (f32[256,128]{1,0:T(8,128)S(1)}, f32[256,128]{1,0:T(8,128)S(1)}, u32[]{:S(2)}, u32[]{:S(2)}) collective-permute-start(f32[256,128]{1,0:T(8,128)S(1)} %get-tuple-element.58.ev.od), channel_id=1, source_target_pairs={{1,33},{3,35},{5,37},{7,39},{9,41},{11,43},{13,45},{15,47},{17,49}... | collective-permute-start | bytes 393224 | tf_op jit(solution)/shard_map/ppermute | solution.py:21
  49.2 2.5 %collective-permute-start.16 = (f32[256,128]{1,0:T(8,128)S(1)}, f32[256,128]{1,0:T(8,128)S(1)}, u32[]{:S(2)}, u32[]{:S(2)}) collective-permute-start(f32[256,128]{1,0:T(8,128)S(1)} %get-tuple-element.60.go.te), channel_id=1, source_target_pairs={{0,1},{1,0},{2,3},{3,2},{4,5},{5,4},{6,7},{7,6},{8,9},{9,8},{10,11... | collective-permute-start | bytes 393224 | tf_op jit(solution)/shard_map/ppermute | solution.py:21
  51.8 0.5 shard_map.90.refs_0_.s
  52.3 0.0 collective-permute-done.15.g
  52.3 0.4 collective-permute-done.16.th.ge.to
  52.8 0.5 shard_map.91
  53.3 4.1 %collective-permute-start.17 = (f32[256,128]{1,0:T(8,128)S(1)}, f32[256,128]{1,0:T(8,128)S(1)}, u32[]{:S(2)}, u32[]{:S(2)}) collective-permute-start(f32[256,128]{1,0:T(8,128)S(1)} %get-tuple-element.61.ev.od), channel_id=1, source_target_pairs={{1,65},{3,67},{5,69},{7,71},{9,73},{11,75},{13,77},{15,79},{17,81}... | collective-permute-start | bytes 393224 | tf_op jit(solution)/shard_map/ppermute | solution.py:21
  57.4 1.8 %collective-permute-start.18 = (f32[256,128]{1,0:T(8,128)S(1)}, f32[256,128]{1,0:T(8,128)S(1)}, u32[]{:S(2)}, u32[]{:S(2)}) collective-permute-start(f32[256,128]{1,0:T(8,128)S(1)} %get-tuple-element.63.go.te), channel_id=1, source_target_pairs={{0,1},{1,0},{2,3},{3,2},{4,5},{5,4},{6,7},{7,6},{8,9},{9,8},{10,11... | collective-permute-start | bytes 393224 | tf_op jit(solution)/shard_map/ppermute | solution.py:21
  59.2 0.5 shard_map.92.refs_0_.s
  59.8 0.1 collective-permute-done.17.g
  59.9 0.3 collective-permute-done.18.th.ge.to
  60.2 0.5 shard_map.93
  60.7 0.1 collective-permute-start.20
  60.8 3.1 %collective-permute-start.19 = (f32[128,128]{1,0:T(8,128)S(1)}, f32[128,128]{1,0:T(8,128)S(1)}, u32[]{:S(2)}, u32[]{:S(2)}) collective-permute-start(f32[128,128]{1,0:T(8,128)S(1)} %get-tuple-element.64), channel_id=1, source_target_pairs={{1,193},{3,195},{5,197},{7,199},{9,201},{11,203},{13,205},{15,207}... | collective-permute-start | bytes 196616 | tf_op jit(solution)/shard_map/ppermute | solution.py:21
  64.0 0.5 shard_map.94.s
  64.5 0.0 collective-permute-done.20.ge.sw
  64.5 0.5 shard_map.95.ar
  65.1 1.3 %shard_map.96.refs_0_.resp = f32[2,128,256]{2,1,0:T(8,128)S(1)} custom-call(f32[3,128,256]{2,1,0:T(8,128)S(1)} %shard_map.95.ar, f32[1,2,128,128]{3,2,1,0:T(8,128)S(1)} %get-tuple-element.36.inv, f32[1,2,128,128]{3,2,1,0:T(8,128)S(1)} %get-tuple-element.37.cou, f32[2,128,128]{2,1,0:T(8,128)S(1)} %get-tuple-element.67.loc, ...), custom_call_target="tpu_custom_call" | custom-call | flops 100000000 | bytes 1179648 | tf_op jit(solution)/shard_map/pallas_call | solution.py:31
  66.4 1.6 %collective-permute-done.19.g = f32[128,128]{1,0:T(8,128)S(1)} collective-permute-done((f32[128,128]{1,0:T(8,128)S(1)}, f32[128,128]{1,0:T(8,128)S(1)}, u32[]{:S(2)}, u32[]{:S(2)}) %collective-permute-start.19) | collective-permute-done | bytes 65568 | tf_op jit(solution)/shard_map/ppermute | solution.py:21
  68.0 1.9 %collective-permute-start.21 = (f32[128,128]{1,0:T(8,128)S(1)}, f32[128,128]{1,0:T(8,128)S(1)}, u32[]{:S(2)}, u32[]{:S(2)}) collective-permute-start(f32[128,128]{1,0:T(8,128)S(1)} %shard_map.97.c), channel_id=1, source_target_pairs={{0,1},{1,0},{2,3},{3,2},{4,5},{5,4},{6,7},{7,6},{8,9},{9,8},{10,11... | collective-permute-start | bytes 196616 | tf_op jit(solution)/shard_map/ppermute | solution.py:21
  69.8 0.9 %collective-permute-done.21.se = f32[128,128]{1,0:T(8,128)S(1)} collective-permute-done((f32[128,128]{1,0:T(8,128)S(1)}, f32[128,128]{1,0:T(8,128)S(1)}, u32[]{:S(2)}, u32[]{:S(2)}) %collective-permute-start.21) | collective-permute-done | bytes 65568 | tf_op jit(solution)/shard_map/ppermute | solution.py:21
  70.7 1.0 %shard_map.98 = (f32[16,16,128]{2,1,0:T(8,128)}, f32[3,16,16]{2,1,0:T(8,128)}) custom-call(f32[128,128]{1,0:T(8,128)S(1)} %shard_map.97.c, f32[128,128]{1,0:T(8,128)S(1)} %collective-permute-done.21.se, f32[2,128,256]{2,1,0:T(8,128)S(1)} %shard_map.96.refs_0_.resp, f32[16,16,128]{2,1,0:T(8,128)S(1)} %get-tuple-element.43.s, ...), custom_call_target="tpu_custom_call" | custom-call | flops 40000000 | bytes 920576 | tf_op jit(solution)/shard_map/pallas_call | solution.py:31
  (8 shorter events, 0.1 us)
Async XLA Ops:
  2.7 11.3 %collective-permute-start = (f32[256,128]{1,0:T(8,128)S(1)}, f32[256,128]{1,0:T(8,128)S(1)}, u32[]{:S(2)}, u32[]{:S(2)}) collective-permute-start(f32[256,128]{1,0:T(8,128)S(1)} %get-tuple-element.39.t.ow), channel_id=1, source_target_pairs={{0,1},{1,0},{2,3},{3,2},{4,5},{5,4},{6,7},{7,6},{8,9},{9,8},{10,11... | collective-permute-start | bytes 393224 | tf_op jit(solution)/shard_map/ppermute | solution.py:21
  6.0 5.5 %collective-permute-start.2 = (f32[1,16,128]{2,1,0:T(8,128)S(1)}, f32[1,16,128]{2,1,0:T(8,128)S(1)}, u32[]{:S(2)}, u32[]{:S(2)}) collective-permute-start(f32[1,16,128]{2,1,0:T(8,128)S(1)} %get-tuple-element.40), channel_id=1, source_target_pairs={{32,64},{96,128},{160,192},{224,0},{64,32},{128,96},{192,160},{0,2... | collective-permute-start | bytes 24584 | tf_op jit(solution)/shard_map/ppermute | solution.py:333
  9.8 1.6 %collective-permute-start.3 = (f32[16,1,128]{2,1,0:T(1,128)S(1)}, f32[16,1,128]{2,1,0:T(1,128)S(1)}, u32[]{:S(2)}, u32[]{:S(2)}) collective-permute-start(f32[16,1,128]{2,1,0:T(1,128)S(1)} %get-tuple-element.41), channel_id=1, source_target_pairs={{0,1},{1,0},{2,3},{3,2},{4,5},{5,4},{6,7},{7,6},{8,9},{9,8},{10,11... | collective-permute-start | bytes 24584 | tf_op jit(solution)/shard_map/ppermute | solution.py:332
  10.2 3.1 %collective-permute-start.4 = (f32[16,1,128]{2,1,0:T(1,128)S(1)}, f32[16,1,128]{2,1,0:T(1,128)S(1)}, u32[]{:S(2)}, u32[]{:S(2)}) collective-permute-start(f32[16,1,128]{2,1,0:T(1,128)S(1)} %get-tuple-element.42), channel_id=1, source_target_pairs={{1,2},{3,4},{5,6},{7,8},{9,10},{11,12},{13,14},{15,16},{17,18},{19... | collective-permute-start | bytes 24584 | tf_op jit(solution)/shard_map/ppermute | solution.py:333
  11.4 2.5 %collective-permute-start.1 = (f32[1,16,128]{2,1,0:T(8,128)S(1)}, f32[1,16,128]{2,1,0:T(8,128)S(1)}, u32[]{:S(2)}, u32[]{:S(2)}) collective-permute-start(f32[1,16,128]{2,1,0:T(8,128)S(1)} %get-tuple-element.38.refs_0_), channel_id=1, source_target_pairs={{0,32},{32,0},{64,96},{96,64},{128,160},{160,128},{192,224},{224,1... | collective-permute-start | bytes 24584 | tf_op jit(solution)/shard_map/ppermute | solution.py:332
  14.0 1.1 %copy-start = (f32[16,16]{1,0:T(8,128)S(1)}, f32[16,16]{1,0:T(8,128)}, u32[]{:S(2)}) copy-start(f32[16,16]{1,0:T(8,128)} %re.1) | copy-start | bytes 3076
  14.0 1.1 %copy-start.1 = (f32[16,16]{1,0:T(8,128)S(1)}, f32[16,16]{1,0:T(8,128)}, u32[]{:S(2)}) copy-start(f32[16,16]{1,0:T(8,128)} %wx.1) | copy-start | bytes 3076
  14.0 1.1 %copy-start.2 = (f32[16,16]{1,0:T(8,128)S(1)}, f32[16,16]{1,0:T(8,128)}, u32[]{:S(2)}) copy-start(f32[16,16]{1,0:T(8,128)} %wy.1) | copy-start | bytes 3076
  14.4 8.3 %collective-permute-start.5 = (f32[256,128]{1,0:T(8,128)S(1)}, f32[256,128]{1,0:T(8,128)S(1)}, u32[]{:S(2)}, u32[]{:S(2)}) collective-permute-start(f32[256,128]{1,0:T(8,128)S(1)} %shard_map.79.refs_0_.ev), channel_id=1, source_target_pairs={{0,2},{2,0},{4,6},{6,4},{8,10},{10,8},{12,14},{14,12},{16,18},{18,... | collective-permute-start | bytes 393224 | tf_op jit(solution)/shard_map/ppermute | solution.py:21
  16.1 7.5 %collective-permute-start.6 = (f32[256,128]{1,0:T(8,128)S(1)}, f32[256,128]{1,0:T(8,128)S(1)}, u32[]{:S(2)}, u32[]{:S(2)}) collective-permute-start(f32[256,128]{1,0:T(8,128)S(1)} %get-tuple-element.45.od), channel_id=1, source_target_pairs={{0,1},{1,0},{2,3},{3,2},{4,5},{5,4},{6,7},{7,6},{8,9},{9,8},{10,11... | collective-permute-start | bytes 393224 | tf_op jit(solution)/shard_map/ppermute | solution.py:21
  24.1 4.2 %collective-permute-start.7 = (f32[256,128]{1,0:T(8,128)S(1)}, f32[256,128]{1,0:T(8,128)S(1)}, u32[]{:S(2)}, u32[]{:S(2)}) collective-permute-start(f32[256,128]{1,0:T(8,128)S(1)} %get-tuple-element.46.ev.od), channel_id=1, source_target_pairs={{1,3},{3,1},{5,7},{7,5},{9,11},{11,9},{13,15},{15,13},{17,19},{19,... | collective-permute-start | bytes 393224 | tf_op jit(solution)/shard_map/ppermute | solution.py:21
  25.9 2.4 %collective-permute-start.8 = (f32[256,128]{1,0:T(8,128)S(1)}, f32[256,128]{1,0:T(8,128)S(1)}, u32[]{:S(2)}, u32[]{:S(2)}) collective-permute-start(f32[256,128]{1,0:T(8,128)S(1)} %get-tuple-element.48.te), channel_id=1, source_target_pairs={{0,1},{1,0},{2,3},{3,2},{4,5},{5,4},{6,7},{7,6},{8,9},{9,8},{10,11... | collective-permute-start | bytes 393224 | tf_op jit(solution)/shard_map/ppermute | solution.py:21
  28.8 5.1 %collective-permute-start.9 = (f32[256,128]{1,0:T(8,128)S(1)}, f32[256,128]{1,0:T(8,128)S(1)}, u32[]{:S(2)}, u32[]{:S(2)}) collective-permute-start(f32[256,128]{1,0:T(8,128)S(1)} %get-tuple-element.49.ev.od), channel_id=1, source_target_pairs={{1,7},{3,5},{5,3},{7,1},{9,15},{11,13},{13,11},{15,9},{17,23},{19,... | collective-permute-start | bytes 393224 | tf_op jit(solution)/shard_map/ppermute | solution.py:21
  31.5 3.2 %collective-permute-start.10 = (f32[256,128]{1,0:T(8,128)S(1)}, f32[256,128]{1,0:T(8,128)S(1)}, u32[]{:S(2)}, u32[]{:S(2)}) collective-permute-start(f32[256,128]{1,0:T(8,128)S(1)} %get-tuple-element.51.go.te), channel_id=1, source_target_pairs={{0,1},{1,0},{2,3},{3,2},{4,5},{5,4},{6,7},{7,6},{8,9},{9,8},{10,11... | collective-permute-start | bytes 393224 | tf_op jit(solution)/shard_map/ppermute | solution.py:21
  35.2 5.1 %collective-permute-start.11 = (f32[256,128]{1,0:T(8,128)S(1)}, f32[256,128]{1,0:T(8,128)S(1)}, u32[]{:S(2)}, u32[]{:S(2)}) collective-permute-start(f32[256,128]{1,0:T(8,128)S(1)} %get-tuple-element.52.ev.od), channel_id=1, source_target_pairs={{1,9},{3,11},{5,13},{7,15},{9,1},{11,3},{13,5},{15,7},{17,25},{19,... | collective-permute-start | bytes 393224 | tf_op jit(solution)/shard_map/ppermute | solution.py:21
  36.9 3.8 %collective-permute-start.12 = (f32[256,128]{1,0:T(8,128)S(1)}, f32[256,128]{1,0:T(8,128)S(1)}, u32[]{:S(2)}, u32[]{:S(2)}) collective-permute-start(f32[256,128]{1,0:T(8,128)S(1)} %get-tuple-element.54.go.te), channel_id=1, source_target_pairs={{0,1},{1,0},{2,3},{3,2},{4,5},{5,4},{6,7},{7,6},{8,9},{9,8},{10,11... | collective-permute-start | bytes 393224 | tf_op jit(solution)/shard_map/ppermute | solution.py:21
  41.3 5.1 %collective-permute-start.13 = (f32[256,128]{1,0:T(8,128)S(1)}, f32[256,128]{1,0:T(8,128)S(1)}, u32[]{:S(2)}, u32[]{:S(2)}) collective-permute-start(f32[256,128]{1,0:T(8,128)S(1)} %get-tuple-element.55.ev.od), channel_id=1, source_target_pairs={{1,25},{3,27},{5,29},{7,31},{9,17},{11,19},{13,21},{15,23},{17,9},... | collective-permute-start | bytes 393224 | tf_op jit(solution)/shard_map/ppermute | solution.py:21
  43.6 3.2 %collective-permute-start.14 = (f32[256,128]{1,0:T(8,128)S(1)}, f32[256,128]{1,0:T(8,128)S(1)}, u32[]{:S(2)}, u32[]{:S(2)}) collective-permute-start(f32[256,128]{1,0:T(8,128)S(1)} %get-tuple-element.57.go.te), channel_id=1, source_target_pairs={{0,1},{1,0},{2,3},{3,2},{4,5},{5,4},{6,7},{7,6},{8,9},{9,8},{10,11... | collective-permute-start | bytes 393224 | tf_op jit(solution)/shard_map/ppermute | solution.py:21
  47.5 4.8 %collective-permute-start.15 = (f32[256,128]{1,0:T(8,128)S(1)}, f32[256,128]{1,0:T(8,128)S(1)}, u32[]{:S(2)}, u32[]{:S(2)}) collective-permute-start(f32[256,128]{1,0:T(8,128)S(1)} %get-tuple-element.58.ev.od), channel_id=1, source_target_pairs={{1,33},{3,35},{5,37},{7,39},{9,41},{11,43},{13,45},{15,47},{17,49}... | collective-permute-start | bytes 393224 | tf_op jit(solution)/shard_map/ppermute | solution.py:21
  49.2 3.5 %collective-permute-start.16 = (f32[256,128]{1,0:T(8,128)S(1)}, f32[256,128]{1,0:T(8,128)S(1)}, u32[]{:S(2)}, u32[]{:S(2)}) collective-permute-start(f32[256,128]{1,0:T(8,128)S(1)} %get-tuple-element.60.go.te), channel_id=1, source_target_pairs={{0,1},{1,0},{2,3},{3,2},{4,5},{5,4},{6,7},{7,6},{8,9},{9,8},{10,11... | collective-permute-start | bytes 393224 | tf_op jit(solution)/shard_map/ppermute | solution.py:21
  53.3 6.6 %collective-permute-start.17 = (f32[256,128]{1,0:T(8,128)S(1)}, f32[256,128]{1,0:T(8,128)S(1)}, u32[]{:S(2)}, u32[]{:S(2)}) collective-permute-start(f32[256,128]{1,0:T(8,128)S(1)} %get-tuple-element.61.ev.od), channel_id=1, source_target_pairs={{1,65},{3,67},{5,69},{7,71},{9,73},{11,75},{13,77},{15,79},{17,81}... | collective-permute-start | bytes 393224 | tf_op jit(solution)/shard_map/ppermute | solution.py:21
  57.4 2.8 %collective-permute-start.18 = (f32[256,128]{1,0:T(8,128)S(1)}, f32[256,128]{1,0:T(8,128)S(1)}, u32[]{:S(2)}, u32[]{:S(2)}) collective-permute-start(f32[256,128]{1,0:T(8,128)S(1)} %get-tuple-element.63.go.te), channel_id=1, source_target_pairs={{0,1},{1,0},{2,3},{3,2},{4,5},{5,4},{6,7},{7,6},{8,9},{9,8},{10,11... | collective-permute-start | bytes 393224 | tf_op jit(solution)/shard_map/ppermute | solution.py:21
  60.7 3.8 %collective-permute-start.20 = (f32[384,128]{1,0:T(8,128)S(1)}, f32[384,128]{1,0:T(8,128)S(1)}, u32[]{:S(2)}, u32[]{:S(2)}) collective-permute-start(f32[384,128]{1,0:T(8,128)S(1)} %get-tuple-element.65), channel_id=1, source_target_pairs={{0,1},{1,0},{2,3},{3,2},{4,5},{5,4},{6,7},{7,6},{8,9},{9,8},{10,11... | collective-permute-start | bytes 589832 | tf_op jit(solution)/shard_map/ppermute | solution.py:21
  60.8 7.2 %collective-permute-start.19 = (f32[128,128]{1,0:T(8,128)S(1)}, f32[128,128]{1,0:T(8,128)S(1)}, u32[]{:S(2)}, u32[]{:S(2)}) collective-permute-start(f32[128,128]{1,0:T(8,128)S(1)} %get-tuple-element.64), channel_id=1, source_target_pairs={{1,193},{3,195},{5,197},{7,199},{9,201},{11,203},{13,205},{15,207}... | collective-permute-start | bytes 196616 | tf_op jit(solution)/shard_map/ppermute | solution.py:21
  68.0 2.8 %collective-permute-start.21 = (f32[128,128]{1,0:T(8,128)S(1)}, f32[128,128]{1,0:T(8,128)S(1)}, u32[]{:S(2)}, u32[]{:S(2)}) collective-permute-start(f32[128,128]{1,0:T(8,128)S(1)} %shard_map.97.c), channel_id=1, source_target_pairs={{0,1},{1,0},{2,3},{3,2},{4,5},{5,4},{6,7},{7,6},{8,9},{9,8},{10,11... | collective-permute-start | bytes 196616 | tf_op jit(solution)/shard_map/ppermute | solution.py:21

commit v2 on v1

--- a/solution.py
+++ b/solution.py
@@ -106,24 +106,16 @@
     return (place() & mask) != 0
 
 
-def edges(samples, inverses, couplings):
-    def kernel(s, inv, cou, x_one, x_two, y_one, y_two, s_out, inv_out, cou_out, sems):
+def load(samples, inverses, couplings):
+    def kernel(s, inv, cou, s_out, inv_out, cou_out, sems):
         pairs = ((s, s_out), (inv, inv_out), (cou, cou_out))
         copies = [pltpu.make_async_copy(a, b, sems.at[i]) for i, (a, b) in enumerate(pairs)]
         for copy in copies:
             copy.start()
-        copies[0].wait()
-        up = bit(UP)
-        x_one[...] = jnp.where(up, s_out[0:1], s_out[15:16])
-        x_two[...] = jnp.where(up, s_out[15:16], s_out[0:1])
-        right = bit(1)
-        y_one[...] = jnp.where(right, s_out[:, 0:1], s_out[:, 15:16])
-        y_two[...] = jnp.where(right, s_out[:, 15:16], s_out[:, 0:1])
-        copies[1].wait()
-        copies[2].wait()
-
-    x, y = (shaped(1, 16, W), shaped(16, 1, W))
-    outs = [x, x, y, y] + [shaped(*a.shape) for a in (samples, inverses, couplings)]
+        for copy in copies:
+            copy.wait()
+
+    outs = [shaped(*a.shape) for a in (samples, inverses, couplings)]
     return pl.pallas_call(
         kernel,
         out_shape=outs,
@@ -135,9 +127,27 @@
     )(samples, inverses, couplings)
 
 
-def inside(axis, before, after):
-    at, size = (lax.axis_index(axis), lax.axis_size(axis))
-    return (jnp.where(at == 0, 0.0, before), jnp.where(at == size - 1, 0.0, after))
+def pack(*fields):
+    def kernel(re, wx, wy, out):
+        out[0] = re[...]
+        out[1] = wx[...]
+        out[2] = wy[...]
+
+    return call(kernel, [shaped(3, *fields[0].shape)], *fields, flops=1)[0]
+
+
+def edges(samples, other):
+    def kernel(odd, even, x_one, x_two, y_one, y_two):
+        up = bit(UP)
+        for at, tile in enumerate((even, odd)):
+            x_one[at] = jnp.where(up, tile[0], tile[15])
+            x_two[at] = jnp.where(up, tile[15], tile[0])
+        right = bit(2)
+        y_one[...] = jnp.where(right, even[:, 0:1], odd[:, 15:16])
+        y_two[...] = jnp.where(right, odd[:, 15:16], even[:, 0:1])
+
+    x, y = (shaped(2, 16, W), shaped(16, 1, W))
+    return call(kernel, [x, x, y, y], samples, other, flops=1)
 
 
 def matrices(inverses, couplings, *waits):
@@ -154,32 +164,47 @@
     return call(kernel, [shaped(2, W, W), shaped(2 * W, W)], inverses, couplings, *waits, flops=3e7)
 
 
-def sources(samples, halo, reaction, weight_x, weight_y, inverses, steps, *waits):
-    def kernel(s, x1, x2, y1, y2, re, wx, wy, inv, st, *refs):
-        lapx, lapy, local, vectors = refs[-4:]
-        v = s[...]
-        xm, xp = choose(bit(UP), (x1[...], x2[...]), (x2[...], x1[...]))
-        ym, yp = choose(bit(1), (y1[...], y2[...]), (y2[...], y1[...]))
-        xm, xp = inside("front", xm, xp)
-        ym, yp = inside("lat", ym, yp)
-        lx = 2.0 * v - jnp.concatenate([xm, v[:-1]], axis=0) - jnp.concatenate([v[1:], xp], axis=0)
-        ly = 2.0 * v - jnp.concatenate([ym, v[:, :-1]], axis=1) - jnp.concatenate([v[:, 1:], yp], axis=1)
-        lapx[...] = lx
-        lapy[...] = ly
-        r = re[...][:, :, None] * v + wx[...][:, :, None] * lx + wy[...][:, :, None] * ly
-        r = r.reshape(2, W, W)
-        b1 = exact(inv[0, 0], r[0])
-        b2 = exact(inv[0, 1], r[1])
-        f1, f2 = (st[0], st[1])
-        v2 = exact(f2, b1) + b2
-        local[0] = b1
-        local[1] = b2
-        vectors[:W] = v2
-        vectors[W:] = exact(f1, b1 + exact(f2, v2, 0), 0)
-
-    tile = shaped(16, 16, W)
-    outs = [tile, tile, shaped(2, W, W), shaped(2 * W, W)]
-    return call(kernel, outs, samples, *halo, reaction, weight_x, weight_y, inverses, steps, *waits)
+def sources(samples, samples_other, halo, fields, fields_other, inv, inv_other, steps, steps_other, total, total_other, wait):
+    def kernel(so, se, x1, x2, y1, y2, *refs):
+        fo, fe, io, ie, sto, ste, to, te, _, theirs, mine, chip = refs
+
+        @pl.when(bit(1))
+        def _():
+            tail = jnp.concatenate
+            first, last = (lax.axis_index("front") == 0, lax.axis_index("front") == lax.axis_size("front") - 1)
+            left, right = (lax.axis_index("lat") == 1, lax.axis_index("lat") == lax.axis_size("lat") - 1)
+            xm, xp = choose(bit(UP), (x1[...], x2[...]), (x2[...], x1[...]))
+            xm, xp = (jnp.where(first, 0.0, xm), jnp.where(last, 0.0, xp))
+            ym, yp = choose(bit(2), (y1[...], y2[...]), (y2[...], y1[...]))
+            ym, yp = (jnp.where(left, 0.0, ym), jnp.where(right, 0.0, yp))
+            even, odd = (se[...], so[...])
+            sides_y = ((ym, odd[:, 0:1]), (even[:, 15:16], yp))
+            sets = ((even, fe, ie, ste, theirs), (odd, fo, io, sto, mine))
+            both = []
+            for at, (v, fields, inv, st, out) in enumerate(sets):
+                before, after = sides_y[at]
+                lx = 2.0 * v - tail([xm[at : at + 1], v[:-1]], axis=0) - tail([v[1:], xp[at : at + 1]], axis=0)
+                ly = 2.0 * v - tail([before, v[:, :-1]], axis=1) - tail([v[:, 1:], after], axis=1)
+                out[: 2 * W] = lx.reshape(2 * W, W)
+                out[2 * W : 4 * W] = ly.reshape(2 * W, W)
+                r = fields[0][:, :, None] * v + fields[1][:, :, None] * lx + fields[2][:, :, None] * ly
+                r = r.reshape(2, W, W)
+                b1 = exact(inv[0, 0], r[0])
+                b2 = exact(inv[0, 1], r[1])
+                f = exact(st[1], b1) + b2
+                h = exact(st[0], b1 + exact(st[1], f, 0), 0)
+                out[4 * W : 5 * W] = b1
+                out[5 * W : 6 * W] = b2
+                both.append((f, h))
+            for out, (f, h) in ((theirs, both[1]), (mine, both[0])):
+                out[6 * W : 7 * W] = f
+                out[7 * W :] = h
+            chip[:W], chip[W:] = compose_vectors(te[:W], to[...], tail(both[0], axis=0), tail(both[1], axis=0))
+
+    outs = [shaped(8 * W, W), shaped(8 * W, W), shaped(2 * W, W)]
+    operands = (samples, samples_other, *halo, fields, fields_other)
+    operands += (inv, inv_other, steps, steps_other, total, total_other, wait)
+    return call(kernel, outs, *operands, flops=6e9)
 
 
 def in_chip(total, partner, *waits):
@@ -191,15 +216,28 @@
     return call(kernel, [shaped(2 * W, W)], total, partner, *waits)[0]
 
 
-def merge(got, bit_even, bit_odd, even, odd, own, theirs, got_odd=None, last=None, waits=()):
+def begin(got, mask, chip, vectors):
+    def kernel(g, ev, od, _, state):
+        @pl.when(bit(1))
+        def _():
+            state[...] = od[...]
+
+        @pl.when(jnp.logical_not(bit(1)))
+        def _():
+            a, b = choose(bit(mask), (g[...], ev[...]), (ev[...], g[...]))
+            state[:W], state[W:] = compose_matrices(a, b)
+
+    return call(kernel, [shaped(2 * W, W)] * 2, got, chip, vectors, same={0: 0})
+
+
+def merge(got, bit_even, bit_odd, even, odd, own, theirs, last=None, waits=()):
     def kernel(g, ev, od, ow, th, *refs):
         state, block = refs[-2:]
 
         @pl.when(bit(1))
         def _():
             late = bit(bit_odd)
-            vectors = g if got_odd is None else refs[0]
-            a, b = choose(late, (vectors[...], od[...]), (od[...], vectors[...]))
+            a, b = choose(late, (g[...], od[...]), (od[...], g[...]))
             maps_a, maps_b = choose(late, (th[...], ow[...]), (ow[...], th[...]))
             tail = jnp.concatenate
             first = (tail([maps_a[:W], a[:W]], axis=1), tail([maps_a[W:], a[W:]], axis=1))
@@ -225,7 +263,7 @@
                 state[:W], state[W:] = compose_matrices(a, b)
 
     outs = [shaped(2 * W, W)] * 3 if last is None else [shaped(2 * W, W), shaped(W, W), shaped(3 * W, W)]
-    operands = (got, even, odd, own, theirs) + (() if got_odd is None else (got_odd,)) + tuple(waits)
+    operands = (got, even, odd, own, theirs) + tuple(waits)
     return call(kernel, outs, *operands, same={0: 0})
 
 
@@ -236,9 +274,10 @@
     return call(kernel, [shaped(*array.shape)], array, flops=1e10, same={0: 0})[0]
 
 
-def start_sides(matrices, vectors):
-    def kernel(m, v, out):
+def start_sides(matrices, mine, sent):
+    def kernel(m, mi, se, out):
         odd = bit(1)
+        v = jnp.where(odd, mi[6 * W :], se[6 * W :])
         row = lax.broadcasted_iota(jnp.int32, (W, 2 * W), 0)
         col = lax.broadcasted_iota(jnp.int32, (W, 2 * W), 1)
         eye = jnp.where(row == col, 1.0, 0.0).astype(F32)
@@ -247,7 +286,7 @@
         out[1] = jnp.where(odd, eye, x)
         out[2] = jnp.where(odd, 0.0, jnp.concatenate([m[W:], v[W:]], axis=1))
 
-    return call(kernel, [shaped(3, W, 2 * W)], matrices, vectors, flops=1)[0]
+    return call(kernel, [shaped(3, W, 2 * W)], matrices, mine, sent, flops=1)[0]
 
 
 def widen(around, theirs, theirs_swapped, got, got_swapped, mask):
@@ -272,20 +311,21 @@
     return call(kernel, [shaped(3, W, 2 * W)], *operands)[0]
 
 
-def respond(around, inverses, couplings, local, steps, mask):
-    def kernel(ar, inv, cou, loc, st, out):
+def respond(around, inverses, couplings, mine, sent, steps, mask):
+    def kernel(ar, inv, cou, mi, se, st, out):
         late = bit(mask)
+        loc = jnp.where(bit(1), mi[4 * W : 6 * W], se[4 * W : 6 * W])
         tail = jnp.concatenate
         none = jnp.zeros((W, W), F32)
         incoming = tail([jnp.where(late, ar[0, :, :W], 0.0), ar[0, :, W:]], axis=1)
-        y1 = tail([none, loc[0]], axis=1) + product(st[0], incoming)
-        y2 = tail([none, loc[1]], axis=1) + product(st[1], y1)
+        y1 = tail([none, loc[:W]], axis=1) + product(st[0], incoming)
+        y2 = tail([none, loc[W:]], axis=1) + product(st[1], y1)
         back = tail([jnp.where(late, 0.0, ar[1, :, :W].T), ar[2, :, W:]], axis=1)
         x2 = product(inv[0, 1], y2 + back + product(ar[2, :, :W], y2), 0)
         out[0] = product(inv[0, 0], y1 - product(cou[0, 1], x2, 0), 0)
         out[1] = x2
 
-    return call(kernel, [shaped(2, W, 2 * W)], around, inverses, couplings, local, steps, flops=1e8)[0]
+    return call(kernel, [shaped(2, W, 2 * W)], around, inverses, couplings, mine, sent, steps, flops=1e8)[0]
 
 
 def arrive(got, swapped, mask, *waits):
@@ -303,47 +343,71 @@
     return call(kernel, [shaped(W, W)], got, swapped, *waits)[0]
 
 
-def finish(comes, sent, response, samples, lapx, lapy):
-    def kernel(c, se, resp, s, lx, ly, white, grad):
-        v = c[...] + se[...]
+def finish(comes, swapped, response, samples, mine, sent):
+    def kernel(c, sw, resp, s, mi, se, white, grad):
+        v = c[...] + sw[...]
         r = resp[...].reshape(2 * W, 2 * W)
-        w = (r[:, W:] + product(r[:, :W], v)).reshape(16, 16, W)
-        white[...] = w
-        grad[0] = jnp.sum(w * s[...], axis=2) * (1.0 / W)
-        grad[1] = jnp.sum(w * lx[...], axis=2) * (1.0 / W)
-        grad[2] = jnp.sum(w * ly[...], axis=2) * (1.0 / W)
-
-    return call(kernel, [shaped(16, 16, W), shaped(3, 16, 16)], comes, sent, response, samples, lapx, lapy)
+        w = r[:, W:] + product(r[:, :W], v)
+        white[...] = w.reshape(16, 16, W)
+        lap = jnp.where(bit(1), mi[: 4 * W], se[: 4 * W])
+        for at, factor in enumerate((s[...].reshape(2 * W, W), lap[: 2 * W], lap[2 * W :])):
+            grad[at] = jnp.sum((w * factor).reshape(16, 16, W), axis=2) * (1.0 / W)
+
+    outs = [shaped(16, 16, W), shaped(3, 16, 16)]
+    return call(kernel, outs, comes, swapped, response, samples, mine, sent)
 
 
 LEVELS = ((1, 1), (2, 2), (4, 6), (8, 8), (16, 24), (32, 32), (64, 64), (128, 192))
 UP = 32
+IDLE = 32
 
 
 def body(samples, reaction, weight_x, weight_y, inverses, couplings):
     top = len(LEVELS) - 1
     evens = range(0, count(), 2)
     odds = range(1, count(), 2)
-    x_one, x_two, y_one, y_two, samples, inverses, couplings = edges(samples, inverses, couplings)
-    halo = []
-    for axis, one, other in (("front", x_one, x_two), ("lat", y_one, y_two)):
-        size = lax.axis_size(axis)
-        pairs = [(i, (i + 1) % size) for i in range(1, size, 2)]
-        halo.append(lax.ppermute(one, axis, [(i, i ^ 1) for i in range(size)]))
-        halo.append(lax.ppermute(other, axis, pairs + [(j, i) for i, j in pairs]))
-    steps, total = matrices(inverses, couplings, x_one)
+    samples, inverses, couplings = load(samples, inverses, couplings)
+    fields = pack(reaction, weight_x, weight_y)
+    samples_other = swap(samples)
+    inverses_other = swap(inverses)
+    fields_other = swap(fields)
+    steps, total = matrices(inverses, couplings)
     other_total = swap(total)
-    chip = in_chip(total, other_total, *halo)
-    got = arrived(send(chip, [(i, i ^ LEVELS[1][1]) for i in evens]))
-    lapx, lapy, local, vectors = sources(
-        samples, halo, reaction, weight_x, weight_y, inverses, steps, chip
+    steps_other = swap(steps)
+    x_one, x_two, y_one, y_two = edges(samples, other=samples_other)
+    chips = count() // 2
+    width = lax.axis_size("lat") // 2
+    step = [(i, i - i % width + (i + 1) % width) for i in range(1, chips, 2)]
+    step += [(j, i) for i, j in step]
+    climb = [(i, (i + UP) % count()) for i in range(count()) if i & UP]
+    climb += [(j, i) for i, j in climb]
+    halo = [
+        send(x_one, [(i, i ^ UP) for i in range(count())]),
+        send(x_two, climb),
+        send(y_one, [(i, i ^ 2) for i in range(count())]),
+        send(y_two, [(2 * i + core, 2 * j + core) for i, j in step for core in range(2)]),
+    ]
+    chip = in_chip(total, other_total, x_one)
+    got = arrived(send(chip, [(i, i ^ LEVELS[1][1]) for i in evens] + [(i, i ^ IDLE) for i in odds]))
+    parcel, mine, vectors = sources(
+        samples,
+        samples_other,
+        halo,
+        fields,
+        fields_other,
+        inverses,
+        inverses_other,
+        steps,
+        steps_other,
+        total,
+        other_total,
+        chip,
     )
-    other_vectors = swap(vectors)
-    got, state, own = merge(
-        got, LEVELS[1][0], LEVELS[0][0], chip, vectors, total, other_total, got_odd=other_vectors
-    )
+    got, state = begin(got, LEVELS[1][0], chip, vectors)
+    own = chip
     swapped = swap(got)
-    around = start_sides(other_total, other_vectors)
+    sent = swap(parcel)
+    around = start_sides(other_total, mine, sent)
     waits = ()
     for at in range(1, top):
         pairs = [(i, i ^ LEVELS[at][1]) for i in odds]
@@ -352,16 +416,16 @@
         got = send(before, pairs)
         last = LEVELS[top][0] if at + 1 == top else None
         got, state, own = merge(
-            got, LEVELS[at + 1][0], LEVELS[at][0], before, before, own, theirs_swapped, last=last, waits=waits
+            got, LEVELS[at + 1][0], LEVELS[at][0], before, before, own, theirs_swapped, last, waits
         )
         swapped = swap(got if last is None else own)
         waits = (around,)
         around = widen(around, theirs, theirs_swapped, got, swapped, LEVELS[at][0])
-    pairs = [(i, i ^ LEVELS[top][1]) for i in range(count()) if i & 1 or i & LEVELS[top][0]]
+    pairs = [(i, i ^ LEVELS[top][1]) for i in range(count())]
     got = send(state, pairs)
-    response = respond(around, inverses, couplings, local, steps, LEVELS[top][0])
+    response = respond(around, inverses, couplings, mine, sent, steps, LEVELS[top][0])
     comes = arrive(got, swapped, LEVELS[top][0], response)
-    return tuple(finish(comes, swap(comes), response, samples, lapx, lapy))
+    return tuple(finish(comes, swap(comes), response, samples, mine, sent))
 
 
 def solution(mesh):

time: 71.9 us -> 69 us (0.960)
  starting transfers between devices: 48.2 us -> 43.3 us
  waiting for transfers between devices: 9.9 us -> 11.8 us
    ppermute x4 -> x0, starting transfers between devices: 5.47 us -> none  [the longest x2 5.11 us: body(): halo.append(lax.ppermute(other, axis, pairs + [(j, i) for i, j in pairs]))]
    ppermute x18 -> x26, waiting for transfers between devices: 7.41 us -> 11.8 us  [send(): return lax.ppermute(array, EVERY, pairs)]
    ppermute x4 -> x0, waiting for transfers between devices: 2.49 us -> none  [the longest x2 1.82 us: body(): halo.append(lax.ppermute(other, axis, pairs + [(j, i) for i, j in pairs]))]
    ppermute x18 -> x26, starting transfers between devices: 42.7 us -> 43.3 us  [send(): return lax.ppermute(array, EVERY, pairs)]
    pallas_call x21 -> x23, Pallas kernels: 11.7 us -> 11.8 us  [call(): pl.pallas_call(kernel, out_shape=outs, in_specs=[vmem] * len(operands), o...]
  transfers between devices with their start and end apart: 22 -> 26, of which waited for: 14 -> 11; matrix products, arithmetic and copies ran while one was open for 0% -> 0% of each run, Pallas kernels for 8% -> 12%
where the time goes in v2:
time: 69 us; the launch traced here: 68.9 us
  starting transfers between devices  43.3 us (63%)
  Pallas kernels  12.9 us (19%)
  waiting for transfers between devices  11.8 us (17%)
  between operations  0.9 us (1%)
    ppermute x26, starting transfers between devices, send(): return lax.ppermute(array, EVERY, pairs)  43.3 us
    ppermute x26, waiting for transfers between devices, send(): return lax.ppermute(array, EVERY, pairs)  11.8 us
    pallas_call x23, Pallas kernels, call(): pl.pallas_call(kernel, out_shape=outs, in_specs=[vmem] * len(operands), o...  11.8 us
  transfers between devices with their start and end apart: 26, of which 11 were waited for; matrix products, arithmetic and copies ran while one was open for 0% of the time, Pallas kernels for 12%

profile of v2, /device:TPU:1, one launch (start us, length us, event | category | flops | bytes accessed | tf_op | source)
XLA Modules:
  0.0 68.9 jit_solution(7499346032253056317)
XLA Ops:
  0.6 1.1 %shard_map.77 = (f32[16,16,128]{2,1,0:T(8,128)S(1)}, f32[1,2,128,128]{3,2,1,0:T(8,128)S(1)}, f32[1,2,128,128]{3,2,1,0:T(8,128)S(1)}) custom-call(f32[16,16,128]{2,1,0:T(8,128)} %s.1, f32[1,2,128,128]{3,2,1,0:T(8,128)} %inv.1, f32[1,2,128,128]{3,2,1,0:T(8,128)} %cou.1), custom_call_target="tpu_custom_call" | custom-call | flops 1 | bytes 800000 | tf_op jit(solution)/shard_map/pallas_call | solution.py:119
  1.7 3.3 %collective-permute-start.1 = (f32[16,16,128]{2,1,0:T(8,128)S(1)}, f32[16,16,128]{2,1,0:T(8,128)S(1)}, u32[]{:S(2)}, u32[]{:S(2)}) collective-permute-start(f32[16,16,128]{2,1,0:T(8,128)S(1)} %get-tuple-element.37.odd.so.s), channel_id=1, source_target_pairs={{0,1},{1,0},{2,3},{3,2},{4,5},{5,4},{6,7},{7,6},{8,9},{9,8},{10,11... | collective-permute-start | bytes 393224 | tf_op jit(solution)/shard_map/ppermute | solution.py:21
  5.0 0.1 collective-permute-start.8
  5.1 0.9 %shard_map.78 = (f32[2,128,128]{2,1,0:T(8,128)S(1)}, f32[256,128]{1,0:T(8,128)S(1)}) custom-call(f32[1,2,128,128]{3,2,1,0:T(8,128)S(1)} %get-tuple-element.34.inv.refs_2_, f32[1,2,128,128]{3,2,1,0:T(8,128)S(1)} %get-tuple-element.35.cou), custom_call_target="tpu_custom_call" | custom-call | flops 30000000 | bytes 524288 | tf_op jit(solution)/shard_map/pallas_call | solution.py:31
  6.1 0.5 collective-permute-start
  6.6 0.1 collective-permute-start.9
  6.7 0.5 collective-permute-start.7
  7.2 0.0 collective-permute-done.1.even.se
  7.2 3.9 %collective-permute-start.4 = (f32[2,16,128]{2,1,0:T(8,128)S(1)}, f32[2,16,128]{2,1,0:T(8,128)S(1)}, u32[]{:S(2)}, u32[]{:S(2)}) collective-permute-start(f32[2,16,128]{2,1,0:T(8,128)S(1)} %get-tuple-element.39), channel_id=1, source_target_pairs={{32,64},{33,65},{34,66},{35,67},{36,68},{37,69},{38,70},{39,71},{4... | collective-permute-start | bytes 49160 | tf_op jit(solution)/shard_map/ppermute | solution.py:21
  11.2 0.0 collective-permute-done.7.refs_1_
  11.2 0.0 collective-permute-start.3
  11.2 0.0 collective-permute-done.8.refs_3_
  11.2 1.3 %collective-permute-start.5 = (f32[16,1,128]{2,1,0:T(1,128)S(1)}, f32[16,1,128]{2,1,0:T(1,128)S(1)}, u32[]{:S(2)}, u32[]{:S(2)}) collective-permute-start(f32[16,1,128]{2,1,0:T(1,128)S(1)} %get-tuple-element.40), channel_id=1, source_target_pairs={{0,2},{1,3},{2,0},{3,1},{4,6},{5,7},{6,4},{7,5},{8,10},{9,11},{10,... | collective-permute-start | bytes 24584 | tf_op jit(solution)/shard_map/ppermute | solution.py:21
  12.5 0.0 collective-permute-done.p.refs_7_.m
  12.5 4.3 %collective-permute-start.6 = (f32[16,1,128]{2,1,0:T(1,128)S(1)}, f32[16,1,128]{2,1,0:T(1,128)S(1)}, u32[]{:S(2)}, u32[]{:S(2)}) collective-permute-start(f32[16,1,128]{2,1,0:T(1,128)S(1)} %get-tuple-element.41), channel_id=1, source_target_pairs={{2,4},{3,5},{6,8},{7,9},{10,12},{11,13},{14,16},{15,17},{18,20},{1... | collective-permute-start | bytes 24584 | tf_op jit(solution)/shard_map/ppermute | solution.py:21
  16.8 0.4 shard_map.80.refs_8_.ev.ow
  17.1 0.0 collective-permute-done.9.refs_5_
  17.2 1.5 %collective-permute-start.2 = (f32[256,128]{1,0:T(8,128)S(1)}, f32[256,128]{1,0:T(8,128)S(1)}, u32[]{:S(2)}, u32[]{:S(2)}) collective-permute-start(f32[256,128]{1,0:T(8,128)S(1)} %shard_map.80.refs_8_.ev.ow), channel_id=1, source_target_pairs={{0,2},{2,0},{4,6},{6,4},{8,10},{10,8},{12,14},{14,12},{16,18},{18,... | collective-permute-start | bytes 393224 | tf_op jit(solution)/shard_map/ppermute | solution.py:21
  18.6 0.0 collective-permute-done.5.y1
  18.6 0.0 collective-permute-done.6.y2
  18.6 0.0 collective-permute-done.3.x1
  18.6 1.8 %shard_map.83 = (f32[1024,128]{1,0:T(8,128)S(1)}, f32[1024,128]{1,0:T(8,128)S(1)}, f32[256,128]{1,0:T(8,128)S(1)}) custom-call(f32[16,16,128]{2,1,0:T(8,128)S(1)} %get-tuple-element.37.odd.so.s, f32[16,16,128]{2,1,0:T(8,128)S(1)} %collective-permute-done.1.even.se, f32[2,16,128]{2,1,0:T(8,128)S(1)} %collective-permute-done.3.x1, ...), custom_call_target="tpu_custom_call" | custom-call | flops 6000000000 | bytes 2414592 | tf_op jit(solution)/shard_map/pallas_call | solution.py:31
  20.4 0.1 collective-permute-start.14
  20.5 0.8 %collective-permute-done.2.a = f32[256,128]{1,0:T(8,128)S(1)} collective-permute-done((f32[256,128]{1,0:T(8,128)S(1)}, f32[256,128]{1,0:T(8,128)S(1)}, u32[]{:S(2)}, u32[]{:S(2)}) %collective-permute-start.2) | collective-permute-done | bytes 131104 | tf_op jit(solution)/shard_map/ppermute | solution.py:21
  21.4 0.1 collective-permute-start.10
  21.5 2.2 %collective-permute-start.11 = (f32[256,128]{1,0:T(8,128)S(1)}, f32[256,128]{1,0:T(8,128)S(1)}, u32[]{:S(2)}, u32[]{:S(2)}) collective-permute-start(f32[256,128]{1,0:T(8,128)S(1)} %get-tuple-element.45.te), channel_id=1, source_target_pairs={{0,1},{1,0},{2,3},{3,2},{4,5},{5,4},{6,7},{7,6},{8,9},{9,8},{10,11... | collective-permute-start | bytes 393224 | tf_op jit(solution)/shard_map/ppermute | solution.py:21
  23.7 1.6 %collective-permute-done.10.g = f32[256,128]{1,0:T(8,128)S(1)} collective-permute-done((f32[256,128]{1,0:T(8,128)S(1)}, f32[256,128]{1,0:T(8,128)S(1)}, u32[]{:S(2)}, u32[]{:S(2)}) %collective-permute-start.10) | collective-permute-done | bytes 131104 | tf_op jit(solution)/shard_map/ppermute | solution.py:21
  25.3 0.5 shard_map.85
  25.8 2.4 %collective-permute-start.12 = (f32[256,128]{1,0:T(8,128)S(1)}, f32[256,128]{1,0:T(8,128)S(1)}, u32[]{:S(2)}, u32[]{:S(2)}) collective-permute-start(f32[256,128]{1,0:T(8,128)S(1)} %get-tuple-element.46.ev.od), channel_id=1, source_target_pairs={{1,7},{3,5},{5,3},{7,1},{9,15},{11,13},{13,11},{15,9},{17,23},{19,... | collective-permute-start | bytes 393224 | tf_op jit(solution)/shard_map/ppermute | solution.py:21
  28.2 2.2 %collective-permute-start.13 = (f32[256,128]{1,0:T(8,128)S(1)}, f32[256,128]{1,0:T(8,128)S(1)}, u32[]{:S(2)}, u32[]{:S(2)}) collective-permute-start(f32[256,128]{1,0:T(8,128)S(1)} %get-tuple-element.48.go.te), channel_id=1, source_target_pairs={{0,1},{1,0},{2,3},{3,2},{4,5},{5,4},{6,7},{7,6},{8,9},{9,8},{10,11... | collective-permute-start | bytes 393224 | tf_op jit(solution)/shard_map/ppermute | solution.py:21
  30.4 0.5 collective-permute-done.12.g
  30.9 0.4 collective-permute-done.13.th.ge.to
  31.4 0.5 shard_map.87
  31.9 1.7 %collective-permute-start.15 = (f32[256,128]{1,0:T(8,128)S(1)}, f32[256,128]{1,0:T(8,128)S(1)}, u32[]{:S(2)}, u32[]{:S(2)}) collective-permute-start(f32[256,128]{1,0:T(8,128)S(1)} %get-tuple-element.51.ev.od), channel_id=1, source_target_pairs={{1,9},{3,11},{5,13},{7,15},{9,1},{11,3},{13,5},{15,7},{17,25},{19,... | collective-permute-start | bytes 393224 | tf_op jit(solution)/shard_map/ppermute | solution.py:21
  33.6 2.8 %collective-permute-start.16 = (f32[256,128]{1,0:T(8,128)S(1)}, f32[256,128]{1,0:T(8,128)S(1)}, u32[]{:S(2)}, u32[]{:S(2)}) collective-permute-start(f32[256,128]{1,0:T(8,128)S(1)} %get-tuple-element.53.go.te), channel_id=1, source_target_pairs={{0,1},{1,0},{2,3},{3,2},{4,5},{5,4},{6,7},{7,6},{8,9},{9,8},{10,11... | collective-permute-start | bytes 393224 | tf_op jit(solution)/shard_map/ppermute | solution.py:21
  36.5 0.5 shard_map.88.refs_0_.s
  37.0 0.4 collective-permute-done.16.th.ge.to
  37.4 0.5 shard_map.89
  38.0 2.3 %collective-permute-start.17 = (f32[256,128]{1,0:T(8,128)S(1)}, f32[256,128]{1,0:T(8,128)S(1)}, u32[]{:S(2)}, u32[]{:S(2)}) collective-permute-start(f32[256,128]{1,0:T(8,128)S(1)} %get-tuple-element.54.ev.od), channel_id=1, source_target_pairs={{1,25},{3,27},{5,29},{7,31},{9,17},{11,19},{13,21},{15,23},{17,9},... | collective-permute-start | bytes 393224 | tf_op jit(solution)/shard_map/ppermute | solution.py:21
  40.3 4.0 %collective-permute-start.18 = (f32[256,128]{1,0:T(8,128)S(1)}, f32[256,128]{1,0:T(8,128)S(1)}, u32[]{:S(2)}, u32[]{:S(2)}) collective-permute-start(f32[256,128]{1,0:T(8,128)S(1)} %get-tuple-element.56.go.te), channel_id=1, source_target_pairs={{0,1},{1,0},{2,3},{3,2},{4,5},{5,4},{6,7},{7,6},{8,9},{9,8},{10,11... | collective-permute-start | bytes 393224 | tf_op jit(solution)/shard_map/ppermute | solution.py:21
  44.3 0.5 shard_map.90.refs_0_.s
  44.9 0.0 collective-permute-done.17.g
  44.9 0.4 collective-permute-done.18.th.ge.to
  45.3 0.5 shard_map.91
  45.8 0.1 collective-permute-start.19
  45.9 4.3 %collective-permute-start.20 = (f32[256,128]{1,0:T(8,128)S(1)}, f32[256,128]{1,0:T(8,128)S(1)}, u32[]{:S(2)}, u32[]{:S(2)}) collective-permute-start(f32[256,128]{1,0:T(8,128)S(1)} %get-tuple-element.59.go.te), channel_id=1, source_target_pairs={{0,1},{1,0},{2,3},{3,2},{4,5},{5,4},{6,7},{7,6},{8,9},{9,8},{10,11... | collective-permute-start | bytes 393224 | tf_op jit(solution)/shard_map/ppermute | solution.py:21
  50.2 0.5 shard_map.92.refs_0_.s
  50.8 0.4 collective-permute-done.20.th.ge.to
  51.2 0.5 shard_map.93
  51.7 2.2 %collective-permute-start.21 = (f32[256,128]{1,0:T(8,128)S(1)}, f32[256,128]{1,0:T(8,128)S(1)}, u32[]{:S(2)}, u32[]{:S(2)}) collective-permute-start(f32[256,128]{1,0:T(8,128)S(1)} %get-tuple-element.60.ev.od), channel_id=1, source_target_pairs={{1,65},{3,67},{5,69},{7,71},{9,73},{11,75},{13,77},{15,79},{17,81}... | collective-permute-start | bytes 393224 | tf_op jit(solution)/shard_map/ppermute | solution.py:21
  53.9 1.0 %collective-permute-start.22 = (f32[256,128]{1,0:T(8,128)S(1)}, f32[256,128]{1,0:T(8,128)S(1)}, u32[]{:S(2)}, u32[]{:S(2)}) collective-permute-start(f32[256,128]{1,0:T(8,128)S(1)} %get-tuple-element.62.go.te), channel_id=1, source_target_pairs={{0,1},{1,0},{2,3},{3,2},{4,5},{5,4},{6,7},{7,6},{8,9},{9,8},{10,11... | collective-permute-start | bytes 393224 | tf_op jit(solution)/shard_map/ppermute | solution.py:21
  54.9 0.5 shard_map.94.refs_0_.s
  55.4 3.8 %collective-permute-done.21.g = f32[256,128]{1,0:T(8,128)S(1)} collective-permute-done((f32[256,128]{1,0:T(8,128)S(1)}, f32[256,128]{1,0:T(8,128)S(1)}, u32[]{:S(2)}, u32[]{:S(2)}) %collective-permute-start.21) | collective-permute-done | bytes 131104 | tf_op jit(solution)/shard_map/ppermute | solution.py:21
  59.3 0.5 shard_map.95
  59.8 0.1 collective-permute-start.24
  59.9 0.5 collective-permute-start.23
  60.3 0.5 shard_map.96.s
  60.9 0.4 collective-permute-done.24.ge.sw
  61.3 0.5 shard_map.97.ar
  61.9 1.3 %shard_map.98.refs_0_.resp = f32[2,128,256]{2,1,0:T(8,128)S(1)} custom-call(f32[3,128,256]{2,1,0:T(8,128)S(1)} %shard_map.97.ar, f32[1,2,128,128]{3,2,1,0:T(8,128)S(1)} %get-tuple-element.34.inv.refs_2_, f32[1,2,128,128]{3,2,1,0:T(8,128)S(1)} %get-tuple-element.35.cou, f32[1024,128]{1,0:T(8,128)S(1)} %get-tuple-element.49.mi, ...), custom_call_target="tpu_custom_call" | custom-call | flops 100000000 | bytes 2097152 | tf_op jit(solution)/shard_map/pallas_call | solution.py:31
  63.2 2.0 %collective-permute-done.23.g = f32[128,128]{1,0:T(8,128)S(1)} collective-permute-done((f32[128,128]{1,0:T(8,128)S(1)}, f32[128,128]{1,0:T(8,128)S(1)}, u32[]{:S(2)}, u32[]{:S(2)}) %collective-permute-start.23) | collective-permute-done | bytes 65568 | tf_op jit(solution)/shard_map/ppermute | solution.py:21
  65.2 1.8 %collective-permute-start.25 = (f32[128,128]{1,0:T(8,128)S(1)}, f32[128,128]{1,0:T(8,128)S(1)}, u32[]{:S(2)}, u32[]{:S(2)}) collective-permute-start(f32[128,128]{1,0:T(8,128)S(1)} %shard_map.99.c), channel_id=1, source_target_pairs={{0,1},{1,0},{2,3},{3,2},{4,5},{5,4},{6,7},{7,6},{8,9},{9,8},{10,11... | collective-permute-start | bytes 196616 | tf_op jit(solution)/shard_map/ppermute | solution.py:21
  67.0 0.9 %collective-permute-done.25.sw = f32[128,128]{1,0:T(8,128)S(1)} collective-permute-done((f32[128,128]{1,0:T(8,128)S(1)}, f32[128,128]{1,0:T(8,128)S(1)}, u32[]{:S(2)}, u32[]{:S(2)}) %collective-permute-start.25) | collective-permute-done | bytes 65568 | tf_op jit(solution)/shard_map/ppermute | solution.py:21
  67.9 1.0 %shard_map.100 = (f32[16,16,128]{2,1,0:T(8,128)}, f32[3,16,16]{2,1,0:T(8,128)}) custom-call(f32[128,128]{1,0:T(8,128)S(1)} %shard_map.99.c, f32[128,128]{1,0:T(8,128)S(1)} %collective-permute-done.25.sw, f32[2,128,256]{2,1,0:T(8,128)S(1)} %shard_map.98.refs_0_.resp, f32[16,16,128]{2,1,0:T(8,128)S(1)} %get-tuple-element.37.odd.so.s, ...), custom_call_target="tpu_custom_call" | custom-call | flops 40000000 | bytes 1707008 | tf_op jit(solution)/shard_map/pallas_call | solution.py:31
  (18 shorter events, 0.1 us)
Async XLA Ops:
  1.7 5.5 %collective-permute-start.1 = (f32[16,16,128]{2,1,0:T(8,128)S(1)}, f32[16,16,128]{2,1,0:T(8,128)S(1)}, u32[]{:S(2)}, u32[]{:S(2)}) collective-permute-start(f32[16,16,128]{2,1,0:T(8,128)S(1)} %get-tuple-element.37.odd.so.s), channel_id=1, source_target_pairs={{0,1},{1,0},{2,3},{3,2},{4,5},{5,4},{6,7},{7,6},{8,9},{9,8},{10,11... | collective-permute-start | bytes 393224 | tf_op jit(solution)/shard_map/ppermute | solution.py:21
  5.0 6.2 %collective-permute-start.8 = (f32[1,2,128,128]{3,2,1,0:T(8,128)S(1)}, f32[1,2,128,128]{3,2,1,0:T(8,128)S(1)}, u32[]{:S(2)}, u32[]{:S(2)}) collective-permute-start(f32[1,2,128,128]{3,2,1,0:T(8,128)S(1)} %get-tuple-element.34.inv.refs_2_), channel_id=1, source_target_pairs={{0,1},{1,0},{2,3},{3,2},{4,5},{5,4},{6,7},{7,6},{8,9},{9,8},{10,11... | collective-permute-start | bytes 393224 | tf_op jit(solution)/shard_map/ppermute | solution.py:21
  5.1 1.6 %copy-start = (f32[16,16]{1,0:T(8,128)S(1)}, f32[16,16]{1,0:T(8,128)}, u32[]{:S(2)}) copy-start(f32[16,16]{1,0:T(8,128)} %re.1) | copy-start | bytes 3076
  5.1 1.6 %copy-start.1 = (f32[16,16]{1,0:T(8,128)S(1)}, f32[16,16]{1,0:T(8,128)}, u32[]{:S(2)}) copy-start(f32[16,16]{1,0:T(8,128)} %wx.1) | copy-start | bytes 3076
  5.1 1.6 %copy-start.2 = (f32[16,16]{1,0:T(8,128)S(1)}, f32[16,16]{1,0:T(8,128)}, u32[]{:S(2)}) copy-start(f32[16,16]{1,0:T(8,128)} %wy.1) | copy-start | bytes 3076
  6.1 6.4 %collective-permute-start = (f32[256,128]{1,0:T(8,128)S(1)}, f32[256,128]{1,0:T(8,128)S(1)}, u32[]{:S(2)}, u32[]{:S(2)}) collective-permute-start(f32[256,128]{1,0:T(8,128)S(1)} %get-tuple-element.36.t.refs_6_), channel_id=1, source_target_pairs={{0,1},{1,0},{2,3},{3,2},{4,5},{5,4},{6,7},{7,6},{8,9},{9,8},{10,11... | collective-permute-start | bytes 393224 | tf_op jit(solution)/shard_map/ppermute | solution.py:21
  6.6 10.6 %collective-permute-start.9 = (f32[2,128,128]{2,1,0:T(8,128)S(1)}, f32[2,128,128]{2,1,0:T(8,128)S(1)}, u32[]{:S(2)}, u32[]{:S(2)}) collective-permute-start(f32[2,128,128]{2,1,0:T(8,128)S(1)} %get-tuple-element.42.refs_4_.st), channel_id=1, source_target_pairs={{0,1},{1,0},{2,3},{3,2},{4,5},{5,4},{6,7},{7,6},{8,9},{9,8},{10,11... | collective-permute-start | bytes 393224 | tf_op jit(solution)/shard_map/ppermute | solution.py:21
  6.7 4.5 %collective-permute-start.7 = (f32[3,16,16]{2,1,0:T(8,128)S(1)}, f32[3,16,16]{2,1,0:T(8,128)S(1)}, u32[]{:S(2)}, u32[]{:S(2)}) collective-permute-start(f32[3,16,16]{2,1,0:T(8,128)S(1)} %shard_map.82.refs_0_), channel_id=1, source_target_pairs={{0,1},{1,0},{2,3},{3,2},{4,5},{5,4},{6,7},{7,6},{8,9},{9,8},{10,11... | collective-permute-start | bytes 9224 | tf_op jit(solution)/shard_map/ppermute | solution.py:21
  7.2 11.4 %collective-permute-start.4 = (f32[2,16,128]{2,1,0:T(8,128)S(1)}, f32[2,16,128]{2,1,0:T(8,128)S(1)}, u32[]{:S(2)}, u32[]{:S(2)}) collective-permute-start(f32[2,16,128]{2,1,0:T(8,128)S(1)} %get-tuple-element.39), channel_id=1, source_target_pairs={{32,64},{33,65},{34,66},{35,67},{36,68},{37,69},{38,70},{39,71},{4... | collective-permute-start | bytes 49160 | tf_op jit(solution)/shard_map/ppermute | solution.py:21
  11.2 7.5 %collective-permute-start.3 = (f32[2,16,128]{2,1,0:T(8,128)S(1)}, f32[2,16,128]{2,1,0:T(8,128)S(1)}, u32[]{:S(2)}, u32[]{:S(2)}) collective-permute-start(f32[2,16,128]{2,1,0:T(8,128)S(1)} %get-tuple-element.38.refs_0_), channel_id=1, source_target_pairs={{0,32},{1,33},{2,34},{3,35},{4,36},{5,37},{6,38},{7,39},{8,40},{9,... | collective-permute-start | bytes 49160 | tf_op jit(solution)/shard_map/ppermute | solution.py:21
  11.2 7.4 %collective-permute-start.5 = (f32[16,1,128]{2,1,0:T(1,128)S(1)}, f32[16,1,128]{2,1,0:T(1,128)S(1)}, u32[]{:S(2)}, u32[]{:S(2)}) collective-permute-start(f32[16,1,128]{2,1,0:T(1,128)S(1)} %get-tuple-element.40), channel_id=1, source_target_pairs={{0,2},{1,3},{2,0},{3,1},{4,6},{5,7},{6,4},{7,5},{8,10},{9,11},{10,... | collective-permute-start | bytes 24584 | tf_op jit(solution)/shard_map/ppermute | solution.py:21
  12.5 6.1 %collective-permute-start.6 = (f32[16,1,128]{2,1,0:T(1,128)S(1)}, f32[16,1,128]{2,1,0:T(1,128)S(1)}, u32[]{:S(2)}, u32[]{:S(2)}) collective-permute-start(f32[16,1,128]{2,1,0:T(1,128)S(1)} %get-tuple-element.41), channel_id=1, source_target_pairs={{2,4},{3,5},{6,8},{7,9},{10,12},{11,13},{14,16},{15,17},{18,20},{1... | collective-permute-start | bytes 24584 | tf_op jit(solution)/shard_map/ppermute | solution.py:21
  17.2 4.2 %collective-permute-start.2 = (f32[256,128]{1,0:T(8,128)S(1)}, f32[256,128]{1,0:T(8,128)S(1)}, u32[]{:S(2)}, u32[]{:S(2)}) collective-permute-start(f32[256,128]{1,0:T(8,128)S(1)} %shard_map.80.refs_8_.ev.ow), channel_id=1, source_target_pairs={{0,2},{2,0},{4,6},{6,4},{8,10},{10,8},{12,14},{14,12},{16,18},{18,... | collective-permute-start | bytes 393224 | tf_op jit(solution)/shard_map/ppermute | solution.py:21
  20.4 10.0 %collective-permute-start.14 = (f32[1024,128]{1,0:T(8,128)S(1)}, f32[1024,128]{1,0:T(8,128)S(1)}, u32[]{:S(2)}, u32[]{:S(2)}) collective-permute-start(f32[1024,128]{1,0:T(8,128)S(1)} %get-tuple-element.50), channel_id=1, source_target_pairs={{0,1},{1,0},{2,3},{3,2},{4,5},{5,4},{6,7},{7,6},{8,9},{9,8},{10,11... | collective-permute-start | bytes 1572872 | tf_op jit(solution)/shard_map/ppermute | solution.py:21
  21.4 3.9 %collective-permute-start.10 = (f32[256,128]{1,0:T(8,128)S(1)}, f32[256,128]{1,0:T(8,128)S(1)}, u32[]{:S(2)}, u32[]{:S(2)}) collective-permute-start(f32[256,128]{1,0:T(8,128)S(1)} %get-tuple-element.44.ev.od), channel_id=1, source_target_pairs={{1,3},{3,1},{5,7},{7,5},{9,11},{11,9},{13,15},{15,13},{17,19},{19,... | collective-permute-start | bytes 393224 | tf_op jit(solution)/shard_map/ppermute | solution.py:21
  21.5 3.8 %collective-permute-start.11 = (f32[256,128]{1,0:T(8,128)S(1)}, f32[256,128]{1,0:T(8,128)S(1)}, u32[]{:S(2)}, u32[]{:S(2)}) collective-permute-start(f32[256,128]{1,0:T(8,128)S(1)} %get-tuple-element.45.te), channel_id=1, source_target_pairs={{0,1},{1,0},{2,3},{3,2},{4,5},{5,4},{6,7},{7,6},{8,9},{9,8},{10,11... | collective-permute-start | bytes 393224 | tf_op jit(solution)/shard_map/ppermute | solution.py:21
  25.8 5.1 %collective-permute-start.12 = (f32[256,128]{1,0:T(8,128)S(1)}, f32[256,128]{1,0:T(8,128)S(1)}, u32[]{:S(2)}, u32[]{:S(2)}) collective-permute-start(f32[256,128]{1,0:T(8,128)S(1)} %get-tuple-element.46.ev.od), channel_id=1, source_target_pairs={{1,7},{3,5},{5,3},{7,1},{9,15},{11,13},{13,11},{15,9},{17,23},{19,... | collective-permute-start | bytes 393224 | tf_op jit(solution)/shard_map/ppermute | solution.py:21
  28.2 3.2 %collective-permute-start.13 = (f32[256,128]{1,0:T(8,128)S(1)}, f32[256,128]{1,0:T(8,128)S(1)}, u32[]{:S(2)}, u32[]{:S(2)}) collective-permute-start(f32[256,128]{1,0:T(8,128)S(1)} %get-tuple-element.48.go.te), channel_id=1, source_target_pairs={{0,1},{1,0},{2,3},{3,2},{4,5},{5,4},{6,7},{7,6},{8,9},{9,8},{10,11... | collective-permute-start | bytes 393224 | tf_op jit(solution)/shard_map/ppermute | solution.py:21
  31.9 5.1 %collective-permute-start.15 = (f32[256,128]{1,0:T(8,128)S(1)}, f32[256,128]{1,0:T(8,128)S(1)}, u32[]{:S(2)}, u32[]{:S(2)}) collective-permute-start(f32[256,128]{1,0:T(8,128)S(1)} %get-tuple-element.51.ev.od), channel_id=1, source_target_pairs={{1,9},{3,11},{5,13},{7,15},{9,1},{11,3},{13,5},{15,7},{17,25},{19,... | collective-permute-start | bytes 393224 | tf_op jit(solution)/shard_map/ppermute | solution.py:21
  33.6 3.8 %collective-permute-start.16 = (f32[256,128]{1,0:T(8,128)S(1)}, f32[256,128]{1,0:T(8,128)S(1)}, u32[]{:S(2)}, u32[]{:S(2)}) collective-permute-start(f32[256,128]{1,0:T(8,128)S(1)} %get-tuple-element.53.go.te), channel_id=1, source_target_pairs={{0,1},{1,0},{2,3},{3,2},{4,5},{5,4},{6,7},{7,6},{8,9},{9,8},{10,11... | collective-permute-start | bytes 393224 | tf_op jit(solution)/shard_map/ppermute | solution.py:21
  38.0 6.9 %collective-permute-start.17 = (f32[256,128]{1,0:T(8,128)S(1)}, f32[256,128]{1,0:T(8,128)S(1)}, u32[]{:S(2)}, u32[]{:S(2)}) collective-permute-start(f32[256,128]{1,0:T(8,128)S(1)} %get-tuple-element.54.ev.od), channel_id=1, source_target_pairs={{1,25},{3,27},{5,29},{7,31},{9,17},{11,19},{13,21},{15,23},{17,9},... | collective-permute-start | bytes 393224 | tf_op jit(solution)/shard_map/ppermute | solution.py:21
  40.3 5.0 %collective-permute-start.18 = (f32[256,128]{1,0:T(8,128)S(1)}, f32[256,128]{1,0:T(8,128)S(1)}, u32[]{:S(2)}, u32[]{:S(2)}) collective-permute-start(f32[256,128]{1,0:T(8,128)S(1)} %get-tuple-element.56.go.te), channel_id=1, source_target_pairs={{0,1},{1,0},{2,3},{3,2},{4,5},{5,4},{6,7},{7,6},{8,9},{9,8},{10,11... | collective-permute-start | bytes 393224 | tf_op jit(solution)/shard_map/ppermute | solution.py:21
  45.8 4.9 %collective-permute-start.19 = (f32[256,128]{1,0:T(8,128)S(1)}, f32[256,128]{1,0:T(8,128)S(1)}, u32[]{:S(2)}, u32[]{:S(2)}) collective-permute-start(f32[256,128]{1,0:T(8,128)S(1)} %get-tuple-element.57.ev.od), channel_id=1, source_target_pairs={{1,33},{3,35},{5,37},{7,39},{9,41},{11,43},{13,45},{15,47},{17,49}... | collective-permute-start | bytes 393224 | tf_op jit(solution)/shard_map/ppermute | solution.py:21
  45.9 5.3 %collective-permute-start.20 = (f32[256,128]{1,0:T(8,128)S(1)}, f32[256,128]{1,0:T(8,128)S(1)}, u32[]{:S(2)}, u32[]{:S(2)}) collective-permute-start(f32[256,128]{1,0:T(8,128)S(1)} %get-tuple-element.59.go.te), channel_id=1, source_target_pairs={{0,1},{1,0},{2,3},{3,2},{4,5},{5,4},{6,7},{7,6},{8,9},{9,8},{10,11... | collective-permute-start | bytes 393224 | tf_op jit(solution)/shard_map/ppermute | solution.py:21
  51.7 7.5 %collective-permute-start.21 = (f32[256,128]{1,0:T(8,128)S(1)}, f32[256,128]{1,0:T(8,128)S(1)}, u32[]{:S(2)}, u32[]{:S(2)}) collective-permute-start(f32[256,128]{1,0:T(8,128)S(1)} %get-tuple-element.60.ev.od), channel_id=1, source_target_pairs={{1,65},{3,67},{5,69},{7,71},{9,73},{11,75},{13,77},{15,79},{17,81}... | collective-permute-start | bytes 393224 | tf_op jit(solution)/shard_map/ppermute | solution.py:21
  53.9 5.4 %collective-permute-start.22 = (f32[256,128]{1,0:T(8,128)S(1)}, f32[256,128]{1,0:T(8,128)S(1)}, u32[]{:S(2)}, u32[]{:S(2)}) collective-permute-start(f32[256,128]{1,0:T(8,128)S(1)} %get-tuple-element.62.go.te), channel_id=1, source_target_pairs={{0,1},{1,0},{2,3},{3,2},{4,5},{5,4},{6,7},{7,6},{8,9},{9,8},{10,11... | collective-permute-start | bytes 393224 | tf_op jit(solution)/shard_map/ppermute | solution.py:21
  59.8 1.5 %collective-permute-start.24 = (f32[384,128]{1,0:T(8,128)S(1)}, f32[384,128]{1,0:T(8,128)S(1)}, u32[]{:S(2)}, u32[]{:S(2)}) collective-permute-start(f32[384,128]{1,0:T(8,128)S(1)} %get-tuple-element.64), channel_id=1, source_target_pairs={{0,1},{1,0},{2,3},{3,2},{4,5},{5,4},{6,7},{7,6},{8,9},{9,8},{10,11... | collective-permute-start | bytes 589832 | tf_op jit(solution)/shard_map/ppermute | solution.py:21
  59.9 5.3 %collective-permute-start.23 = (f32[128,128]{1,0:T(8,128)S(1)}, f32[128,128]{1,0:T(8,128)S(1)}, u32[]{:S(2)}, u32[]{:S(2)}) collective-permute-start(f32[128,128]{1,0:T(8,128)S(1)} %get-tuple-element.63), channel_id=1, source_target_pairs={{0,192},{1,193},{2,194},{3,195},{4,196},{5,197},{6,198},{7,199},{8... | collective-permute-start | bytes 196616 | tf_op jit(solution)/shard_map/ppermute | solution.py:21
  65.2 2.7 %collective-permute-start.25 = (f32[128,128]{1,0:T(8,128)S(1)}, f32[128,128]{1,0:T(8,128)S(1)}, u32[]{:S(2)}, u32[]{:S(2)}) collective-permute-start(f32[128,128]{1,0:T(8,128)S(1)} %shard_map.99.c), channel_id=1, source_target_pairs={{0,1},{1,0},{2,3},{3,2},{4,5},{5,4},{6,7},{7,6},{8,9},{9,8},{10,11... | collective-permute-start | bytes 196616 | tf_op jit(solution)/shard_map/ppermute | solution.py:21

commit v3 on v2

--- a/solution.py
+++ b/solution.py
@@ -204,7 +204,7 @@
     outs = [shaped(8 * W, W), shaped(8 * W, W), shaped(2 * W, W)]
     operands = (samples, samples_other, *halo, fields, fields_other)
     operands += (inv, inv_other, steps, steps_other, total, total_other, wait)
-    return call(kernel, outs, *operands, flops=6e9)
+    return call(kernel, outs, *operands, flops=1.3e9)
 
 
 def in_chip(total, partner, *waits):

time: 69 us -> 68.2 us (0.988)
  starting transfers between devices: 43.3 us -> 41 us
  waiting for transfers between devices: 11.8 us -> 13.3 us
    ppermute x26, starting transfers between devices: 43.3 us -> 41 us  [send(): return lax.ppermute(array, EVERY, pairs)]
    ppermute x26, waiting for transfers between devices: 11.8 us -> 13.3 us  [send(): return lax.ppermute(array, EVERY, pairs)]
where the time goes in v3:
time: 68.2 us; the launch traced here: 68.1 us
  starting transfers between devices  41 us (60%)
  waiting for transfers between devices  13.3 us (20%)
  Pallas kernels  12.9 us (19%)
  between operations  0.92 us (1%)
    ppermute x26, starting transfers between devices, send(): return lax.ppermute(array, EVERY, pairs)  41 us
    ppermute x26, waiting for transfers between devices, send(): return lax.ppermute(array, EVERY, pairs)  13.3 us
    pallas_call x23, Pallas kernels, call(): pl.pallas_call(kernel, out_shape=outs, in_specs=[vmem] * len(operands), o...  11.8 us
  transfers between devices with their start and end apart: 26, of which 11 were waited for; matrix products, arithmetic and copies ran while one was open for 0% of the time, Pallas kernels for 12%

profile of v3, /device:TPU:1, one launch (start us, length us, event | category | flops | bytes accessed | tf_op | source)
XLA Modules:
  0.0 68.1 jit_solution(7589427486891107421)
XLA Ops:
  0.6 1.1 %shard_map.77 = (f32[16,16,128]{2,1,0:T(8,128)S(1)}, f32[1,2,128,128]{3,2,1,0:T(8,128)S(1)}, f32[1,2,128,128]{3,2,1,0:T(8,128)S(1)}) custom-call(f32[16,16,128]{2,1,0:T(8,128)} %s.1, f32[1,2,128,128]{3,2,1,0:T(8,128)} %inv.1, f32[1,2,128,128]{3,2,1,0:T(8,128)} %cou.1), custom_call_target="tpu_custom_call" | custom-call | flops 1 | bytes 800000 | tf_op jit(solution)/shard_map/pallas_call | solution.py:119
  1.7 3.3 %collective-permute-start.1 = (f32[16,16,128]{2,1,0:T(8,128)S(1)}, f32[16,16,128]{2,1,0:T(8,128)S(1)}, u32[]{:S(2)}, u32[]{:S(2)}) collective-permute-start(f32[16,16,128]{2,1,0:T(8,128)S(1)} %get-tuple-element.37.odd.so.s), channel_id=1, source_target_pairs={{0,1},{1,0},{2,3},{3,2},{4,5},{5,4},{6,7},{7,6},{8,9},{9,8},{10,11... | collective-permute-start | bytes 393224 | tf_op jit(solution)/shard_map/ppermute | solution.py:21
  5.0 0.9 %shard_map.78 = (f32[2,128,128]{2,1,0:T(8,128)S(1)}, f32[256,128]{1,0:T(8,128)S(1)}) custom-call(f32[1,2,128,128]{3,2,1,0:T(8,128)S(1)} %get-tuple-element.34.inv.refs_2_, f32[1,2,128,128]{3,2,1,0:T(8,128)S(1)} %get-tuple-element.35.cou), custom_call_target="tpu_custom_call" | custom-call | flops 30000000 | bytes 524288 | tf_op jit(solution)/shard_map/pallas_call | solution.py:31
  6.0 0.1 collective-permute-start
  6.1 0.5 collective-permute-start.8
  6.6 0.1 collective-permute-start.9
  6.7 0.0 collective-permute-done.1.even.se
  6.7 3.9 %collective-permute-start.4 = (f32[2,16,128]{2,1,0:T(8,128)S(1)}, f32[2,16,128]{2,1,0:T(8,128)S(1)}, u32[]{:S(2)}, u32[]{:S(2)}) collective-permute-start(f32[2,16,128]{2,1,0:T(8,128)S(1)} %get-tuple-element.39), channel_id=1, source_target_pairs={{32,64},{33,65},{34,66},{35,67},{36,68},{37,69},{38,70},{39,71},{4... | collective-permute-start | bytes 49160 | tf_op jit(solution)/shard_map/ppermute | solution.py:21
  10.7 0.8 %collective-permute-start.7 = (f32[3,16,16]{2,1,0:T(8,128)S(1)}, f32[3,16,16]{2,1,0:T(8,128)S(1)}, u32[]{:S(2)}, u32[]{:S(2)}) collective-permute-start(f32[3,16,16]{2,1,0:T(8,128)S(1)} %shard_map.82.refs_0_), channel_id=1, source_target_pairs={{0,1},{1,0},{2,3},{3,2},{4,5},{5,4},{6,7},{7,6},{8,9},{9,8},{10,11... | collective-permute-start | bytes 9224 | tf_op jit(solution)/shard_map/ppermute | solution.py:21
  11.5 0.4 shard_map.80.refs_8_.ev.ow
  11.9 0.5 collective-permute-done.7.refs_1_
  12.3 1.7 %collective-permute-start.2 = (f32[256,128]{1,0:T(8,128)S(1)}, f32[256,128]{1,0:T(8,128)S(1)}, u32[]{:S(2)}, u32[]{:S(2)}) collective-permute-start(f32[256,128]{1,0:T(8,128)S(1)} %shard_map.80.refs_8_.ev.ow), channel_id=1, source_target_pairs={{0,2},{2,0},{4,6},{6,4},{8,10},{10,8},{12,14},{14,12},{16,18},{18,... | collective-permute-start | bytes 393224 | tf_op jit(solution)/shard_map/ppermute | solution.py:21
  14.0 0.0 collective-permute-done.8.refs_3_
  14.1 1.2 %collective-permute-start.5 = (f32[16,1,128]{2,1,0:T(1,128)S(1)}, f32[16,1,128]{2,1,0:T(1,128)S(1)}, u32[]{:S(2)}, u32[]{:S(2)}) collective-permute-start(f32[16,1,128]{2,1,0:T(1,128)S(1)} %get-tuple-element.40), channel_id=1, source_target_pairs={{0,2},{1,3},{2,0},{3,1},{4,6},{5,7},{6,4},{7,5},{8,10},{9,11},{10,... | collective-permute-start | bytes 24584 | tf_op jit(solution)/shard_map/ppermute | solution.py:21
  15.3 0.0 collective-permute-done.9.refs_5_
  15.3 4.3 %collective-permute-start.6 = (f32[16,1,128]{2,1,0:T(1,128)S(1)}, f32[16,1,128]{2,1,0:T(1,128)S(1)}, u32[]{:S(2)}, u32[]{:S(2)}) collective-permute-start(f32[16,1,128]{2,1,0:T(1,128)S(1)} %get-tuple-element.41), channel_id=1, source_target_pairs={{2,4},{3,5},{6,8},{7,9},{10,12},{11,13},{14,16},{15,17},{18,20},{1... | collective-permute-start | bytes 24584 | tf_op jit(solution)/shard_map/ppermute | solution.py:21
  19.6 0.0 collective-permute-done.5.y1
  19.6 1.7 %collective-permute-done.6.y2 = f32[16,1,128]{2,1,0:T(1,128)S(1)} collective-permute-done((f32[16,1,128]{2,1,0:T(1,128)S(1)}, f32[16,1,128]{2,1,0:T(1,128)S(1)}, u32[]{:S(2)}, u32[]{:S(2)}) %collective-permute-start.6) | collective-permute-done | bytes 8224 | tf_op jit(solution)/shard_map/ppermute | solution.py:21
  21.3 1.8 %shard_map.83 = (f32[1024,128]{1,0:T(8,128)S(1)}, f32[1024,128]{1,0:T(8,128)S(1)}, f32[256,128]{1,0:T(8,128)S(1)}) custom-call(f32[16,16,128]{2,1,0:T(8,128)S(1)} %get-tuple-element.37.odd.so.s, f32[16,16,128]{2,1,0:T(8,128)S(1)} %collective-permute-done.1.even.se, f32[2,16,128]{2,1,0:T(8,128)S(1)} %collective-permute-done.3.x1, ...), custom_call_target="tpu_custom_call" | custom-call | flops 1300000000 | bytes 2414592 | tf_op jit(solution)/shard_map/pallas_call | solution.py:31
  23.0 0.1 collective-permute-start.14
  23.1 0.0 collective-permute-done.2.a
  23.2 0.1 collective-permute-start.10
  23.3 1.5 %collective-permute-start.11 = (f32[256,128]{1,0:T(8,128)S(1)}, f32[256,128]{1,0:T(8,128)S(1)}, u32[]{:S(2)}, u32[]{:S(2)}) collective-permute-start(f32[256,128]{1,0:T(8,128)S(1)} %get-tuple-element.45.te), channel_id=1, source_target_pairs={{0,1},{1,0},{2,3},{3,2},{4,5},{5,4},{6,7},{7,6},{8,9},{9,8},{10,11... | collective-permute-start | bytes 393224 | tf_op jit(solution)/shard_map/ppermute | solution.py:21
  24.8 2.3 %collective-permute-done.10.g = f32[256,128]{1,0:T(8,128)S(1)} collective-permute-done((f32[256,128]{1,0:T(8,128)S(1)}, f32[256,128]{1,0:T(8,128)S(1)}, u32[]{:S(2)}, u32[]{:S(2)}) %collective-permute-start.10) | collective-permute-done | bytes 131104 | tf_op jit(solution)/shard_map/ppermute | solution.py:21
  27.1 0.0 collective-permute-done.11.th.to
  27.1 0.5 shard_map.85
  27.6 1.0 %collective-permute-start.12 = (f32[256,128]{1,0:T(8,128)S(1)}, f32[256,128]{1,0:T(8,128)S(1)}, u32[]{:S(2)}, u32[]{:S(2)}) collective-permute-start(f32[256,128]{1,0:T(8,128)S(1)} %get-tuple-element.46.ev.od), channel_id=1, source_target_pairs={{1,7},{3,5},{5,3},{7,1},{9,15},{11,13},{13,11},{15,9},{17,23},{19,... | collective-permute-start | bytes 393224 | tf_op jit(solution)/shard_map/ppermute | solution.py:21
  28.7 2.5 %collective-permute-start.13 = (f32[256,128]{1,0:T(8,128)S(1)}, f32[256,128]{1,0:T(8,128)S(1)}, u32[]{:S(2)}, u32[]{:S(2)}) collective-permute-start(f32[256,128]{1,0:T(8,128)S(1)} %get-tuple-element.48.go.te), channel_id=1, source_target_pairs={{0,1},{1,0},{2,3},{3,2},{4,5},{5,4},{6,7},{7,6},{8,9},{9,8},{10,11... | collective-permute-start | bytes 393224 | tf_op jit(solution)/shard_map/ppermute | solution.py:21
  31.2 0.0 collective-permute-done.14.se
  31.2 1.6 %collective-permute-done.12.g = f32[256,128]{1,0:T(8,128)S(1)} collective-permute-done((f32[256,128]{1,0:T(8,128)S(1)}, f32[256,128]{1,0:T(8,128)S(1)}, u32[]{:S(2)}, u32[]{:S(2)}) %collective-permute-start.12) | collective-permute-done | bytes 131104 | tf_op jit(solution)/shard_map/ppermute | solution.py:21
  32.8 0.5 shard_map.87
  33.3 0.8 %collective-permute-start.15 = (f32[256,128]{1,0:T(8,128)S(1)}, f32[256,128]{1,0:T(8,128)S(1)}, u32[]{:S(2)}, u32[]{:S(2)}) collective-permute-start(f32[256,128]{1,0:T(8,128)S(1)} %get-tuple-element.51.ev.od), channel_id=1, source_target_pairs={{1,9},{3,11},{5,13},{7,15},{9,1},{11,3},{13,5},{15,7},{17,25},{19,... | collective-permute-start | bytes 393224 | tf_op jit(solution)/shard_map/ppermute | solution.py:21
  34.1 3.9 %collective-permute-start.16 = (f32[256,128]{1,0:T(8,128)S(1)}, f32[256,128]{1,0:T(8,128)S(1)}, u32[]{:S(2)}, u32[]{:S(2)}) collective-permute-start(f32[256,128]{1,0:T(8,128)S(1)} %get-tuple-element.53.go.te), channel_id=1, source_target_pairs={{0,1},{1,0},{2,3},{3,2},{4,5},{5,4},{6,7},{7,6},{8,9},{9,8},{10,11... | collective-permute-start | bytes 393224 | tf_op jit(solution)/shard_map/ppermute | solution.py:21
  38.0 0.5 shard_map.88.refs_0_.s
  38.6 0.0 collective-permute-done.15.g
  38.6 0.4 collective-permute-done.16.th.ge.to
  39.0 0.5 shard_map.89
  39.6 1.2 %collective-permute-start.17 = (f32[256,128]{1,0:T(8,128)S(1)}, f32[256,128]{1,0:T(8,128)S(1)}, u32[]{:S(2)}, u32[]{:S(2)}) collective-permute-start(f32[256,128]{1,0:T(8,128)S(1)} %get-tuple-element.54.ev.od), channel_id=1, source_target_pairs={{1,25},{3,27},{5,29},{7,31},{9,17},{11,19},{13,21},{15,23},{17,9},... | collective-permute-start | bytes 393224 | tf_op jit(solution)/shard_map/ppermute | solution.py:21
  40.8 2.3 %collective-permute-start.18 = (f32[256,128]{1,0:T(8,128)S(1)}, f32[256,128]{1,0:T(8,128)S(1)}, u32[]{:S(2)}, u32[]{:S(2)}) collective-permute-start(f32[256,128]{1,0:T(8,128)S(1)} %get-tuple-element.56.go.te), channel_id=1, source_target_pairs={{0,1},{1,0},{2,3},{3,2},{4,5},{5,4},{6,7},{7,6},{8,9},{9,8},{10,11... | collective-permute-start | bytes 393224 | tf_op jit(solution)/shard_map/ppermute | solution.py:21
  43.1 0.5 shard_map.90.refs_0_.s
  43.6 1.1 %collective-permute-done.17.g = f32[256,128]{1,0:T(8,128)S(1)} collective-permute-done((f32[256,128]{1,0:T(8,128)S(1)}, f32[256,128]{1,0:T(8,128)S(1)}, u32[]{:S(2)}, u32[]{:S(2)}) %collective-permute-start.17) | collective-permute-done | bytes 131104 | tf_op jit(solution)/shard_map/ppermute | solution.py:21
  44.7 0.0 collective-permute-done.18.th.ge.to
  44.7 0.5 shard_map.91
  45.2 1.0 %collective-permute-start.19 = (f32[256,128]{1,0:T(8,128)S(1)}, f32[256,128]{1,0:T(8,128)S(1)}, u32[]{:S(2)}, u32[]{:S(2)}) collective-permute-start(f32[256,128]{1,0:T(8,128)S(1)} %get-tuple-element.57.ev.od), channel_id=1, source_target_pairs={{1,33},{3,35},{5,37},{7,39},{9,41},{11,43},{13,45},{15,47},{17,49}... | collective-permute-start | bytes 393224 | tf_op jit(solution)/shard_map/ppermute | solution.py:21
  46.2 2.7 %collective-permute-start.20 = (f32[256,128]{1,0:T(8,128)S(1)}, f32[256,128]{1,0:T(8,128)S(1)}, u32[]{:S(2)}, u32[]{:S(2)}) collective-permute-start(f32[256,128]{1,0:T(8,128)S(1)} %get-tuple-element.59.go.te), channel_id=1, source_target_pairs={{0,1},{1,0},{2,3},{3,2},{4,5},{5,4},{6,7},{7,6},{8,9},{9,8},{10,11... | collective-permute-start | bytes 393224 | tf_op jit(solution)/shard_map/ppermute | solution.py:21
  49.0 0.5 shard_map.92.refs_0_.s
  49.5 0.0 collective-permute-done.19.g
  49.5 0.4 collective-permute-done.20.th.ge.to
  49.9 0.5 shard_map.93
  50.5 3.9 %collective-permute-start.21 = (f32[256,128]{1,0:T(8,128)S(1)}, f32[256,128]{1,0:T(8,128)S(1)}, u32[]{:S(2)}, u32[]{:S(2)}) collective-permute-start(f32[256,128]{1,0:T(8,128)S(1)} %get-tuple-element.60.ev.od), channel_id=1, source_target_pairs={{1,65},{3,67},{5,69},{7,71},{9,73},{11,75},{13,77},{15,79},{17,81}... | collective-permute-start | bytes 393224 | tf_op jit(solution)/shard_map/ppermute | solution.py:21
  54.4 2.0 %collective-permute-start.22 = (f32[256,128]{1,0:T(8,128)S(1)}, f32[256,128]{1,0:T(8,128)S(1)}, u32[]{:S(2)}, u32[]{:S(2)}) collective-permute-start(f32[256,128]{1,0:T(8,128)S(1)} %get-tuple-element.62.go.te), channel_id=1, source_target_pairs={{0,1},{1,0},{2,3},{3,2},{4,5},{5,4},{6,7},{7,6},{8,9},{9,8},{10,11... | collective-permute-start | bytes 393224 | tf_op jit(solution)/shard_map/ppermute | solution.py:21
  56.4 0.5 shard_map.94.refs_0_.s
  56.9 1.5 %collective-permute-done.21.g = f32[256,128]{1,0:T(8,128)S(1)} collective-permute-done((f32[256,128]{1,0:T(8,128)S(1)}, f32[256,128]{1,0:T(8,128)S(1)}, u32[]{:S(2)}, u32[]{:S(2)}) %collective-permute-start.21) | collective-permute-done | bytes 131104 | tf_op jit(solution)/shard_map/ppermute | solution.py:21
  58.5 0.5 shard_map.95
  59.0 0.1 collective-permute-start.24
  59.1 0.1 collective-permute-start.23
  59.2 0.5 shard_map.96.s
  59.8 0.8 %collective-permute-done.24.ge.sw = f32[384,128]{1,0:T(8,128)S(1)} collective-permute-done((f32[384,128]{1,0:T(8,128)S(1)}, f32[384,128]{1,0:T(8,128)S(1)}, u32[]{:S(2)}, u32[]{:S(2)}) %collective-permute-start.24) | collective-permute-done | bytes 196640 | tf_op jit(solution)/shard_map/ppermute | solution.py:21
  60.5 0.5 shard_map.97.ar
  61.1 1.3 %shard_map.98.refs_0_.resp = f32[2,128,256]{2,1,0:T(8,128)S(1)} custom-call(f32[3,128,256]{2,1,0:T(8,128)S(1)} %shard_map.97.ar, f32[1,2,128,128]{3,2,1,0:T(8,128)S(1)} %get-tuple-element.34.inv.refs_2_, f32[1,2,128,128]{3,2,1,0:T(8,128)S(1)} %get-tuple-element.35.cou, f32[1024,128]{1,0:T(8,128)S(1)} %get-tuple-element.49.mi, ...), custom_call_target="tpu_custom_call" | custom-call | flops 100000000 | bytes 2097152 | tf_op jit(solution)/shard_map/pallas_call | solution.py:31
  62.4 2.1 %collective-permute-done.23.g = f32[128,128]{1,0:T(8,128)S(1)} collective-permute-done((f32[128,128]{1,0:T(8,128)S(1)}, f32[128,128]{1,0:T(8,128)S(1)}, u32[]{:S(2)}, u32[]{:S(2)}) %collective-permute-start.23) | collective-permute-done | bytes 65568 | tf_op jit(solution)/shard_map/ppermute | solution.py:21
  64.5 1.7 %collective-permute-start.25 = (f32[128,128]{1,0:T(8,128)S(1)}, f32[128,128]{1,0:T(8,128)S(1)}, u32[]{:S(2)}, u32[]{:S(2)}) collective-permute-start(f32[128,128]{1,0:T(8,128)S(1)} %shard_map.99.c), channel_id=1, source_target_pairs={{0,1},{1,0},{2,3},{3,2},{4,5},{5,4},{6,7},{7,6},{8,9},{9,8},{10,11... | collective-permute-start | bytes 196616 | tf_op jit(solution)/shard_map/ppermute | solution.py:21
  66.3 0.9 %collective-permute-done.25.sw = f32[128,128]{1,0:T(8,128)S(1)} collective-permute-done((f32[128,128]{1,0:T(8,128)S(1)}, f32[128,128]{1,0:T(8,128)S(1)}, u32[]{:S(2)}, u32[]{:S(2)}) %collective-permute-start.25) | collective-permute-done | bytes 65568 | tf_op jit(solution)/shard_map/ppermute | solution.py:21
  67.2 1.0 %shard_map.100 = (f32[16,16,128]{2,1,0:T(8,128)}, f32[3,16,16]{2,1,0:T(8,128)}) custom-call(f32[128,128]{1,0:T(8,128)S(1)} %shard_map.99.c, f32[128,128]{1,0:T(8,128)S(1)} %collective-permute-done.25.sw, f32[2,128,256]{2,1,0:T(8,128)S(1)} %shard_map.98.refs_0_.resp, f32[16,16,128]{2,1,0:T(8,128)S(1)} %get-tuple-element.37.odd.so.s, ...), custom_call_target="tpu_custom_call" | custom-call | flops 40000000 | bytes 1707008 | tf_op jit(solution)/shard_map/pallas_call | solution.py:31
  (18 shorter events, 0.1 us)
Async XLA Ops:
  1.7 5.0 %collective-permute-start.1 = (f32[16,16,128]{2,1,0:T(8,128)S(1)}, f32[16,16,128]{2,1,0:T(8,128)S(1)}, u32[]{:S(2)}, u32[]{:S(2)}) collective-permute-start(f32[16,16,128]{2,1,0:T(8,128)S(1)} %get-tuple-element.37.odd.so.s), channel_id=1, source_target_pairs={{0,1},{1,0},{2,3},{3,2},{4,5},{5,4},{6,7},{7,6},{8,9},{9,8},{10,11... | collective-permute-start | bytes 393224 | tf_op jit(solution)/shard_map/ppermute | solution.py:21
  6.0 4.7 %collective-permute-start = (f32[256,128]{1,0:T(8,128)S(1)}, f32[256,128]{1,0:T(8,128)S(1)}, u32[]{:S(2)}, u32[]{:S(2)}) collective-permute-start(f32[256,128]{1,0:T(8,128)S(1)} %get-tuple-element.36.t.refs_6_), channel_id=1, source_target_pairs={{0,1},{1,0},{2,3},{3,2},{4,5},{5,4},{6,7},{7,6},{8,9},{9,8},{10,11... | collective-permute-start | bytes 393224 | tf_op jit(solution)/shard_map/ppermute | solution.py:21
  6.1 8.0 %collective-permute-start.8 = (f32[1,2,128,128]{3,2,1,0:T(8,128)S(1)}, f32[1,2,128,128]{3,2,1,0:T(8,128)S(1)}, u32[]{:S(2)}, u32[]{:S(2)}) collective-permute-start(f32[1,2,128,128]{3,2,1,0:T(8,128)S(1)} %get-tuple-element.34.inv.refs_2_), channel_id=1, source_target_pairs={{0,1},{1,0},{2,3},{3,2},{4,5},{5,4},{6,7},{7,6},{8,9},{9,8},{10,11... | collective-permute-start | bytes 393224 | tf_op jit(solution)/shard_map/ppermute | solution.py:21
  6.6 8.7 %collective-permute-start.9 = (f32[2,128,128]{2,1,0:T(8,128)S(1)}, f32[2,128,128]{2,1,0:T(8,128)S(1)}, u32[]{:S(2)}, u32[]{:S(2)}) collective-permute-start(f32[2,128,128]{2,1,0:T(8,128)S(1)} %get-tuple-element.42.refs_4_.st), channel_id=1, source_target_pairs={{0,1},{1,0},{2,3},{3,2},{4,5},{5,4},{6,7},{7,6},{8,9},{9,8},{10,11... | collective-permute-start | bytes 393224 | tf_op jit(solution)/shard_map/ppermute | solution.py:21
  6.7 4.0 %copy-start = (f32[16,16]{1,0:T(8,128)S(1)}, f32[16,16]{1,0:T(8,128)}, u32[]{:S(2)}) copy-start(f32[16,16]{1,0:T(8,128)} %re.1) | copy-start | bytes 3076
  6.7 4.0 %copy-start.1 = (f32[16,16]{1,0:T(8,128)S(1)}, f32[16,16]{1,0:T(8,128)}, u32[]{:S(2)}) copy-start(f32[16,16]{1,0:T(8,128)} %wx.1) | copy-start | bytes 3076
  6.7 4.0 %copy-start.2 = (f32[16,16]{1,0:T(8,128)S(1)}, f32[16,16]{1,0:T(8,128)}, u32[]{:S(2)}) copy-start(f32[16,16]{1,0:T(8,128)} %wy.1) | copy-start | bytes 3076
  6.7 14.6 %collective-permute-start.4 = (f32[2,16,128]{2,1,0:T(8,128)S(1)}, f32[2,16,128]{2,1,0:T(8,128)S(1)}, u32[]{:S(2)}, u32[]{:S(2)}) collective-permute-start(f32[2,16,128]{2,1,0:T(8,128)S(1)} %get-tuple-element.39), channel_id=1, source_target_pairs={{32,64},{33,65},{34,66},{35,67},{36,68},{37,69},{38,70},{39,71},{4... | collective-permute-start | bytes 49160 | tf_op jit(solution)/shard_map/ppermute | solution.py:21
  10.6 10.6 %collective-permute-start.3 = (f32[2,16,128]{2,1,0:T(8,128)S(1)}, f32[2,16,128]{2,1,0:T(8,128)S(1)}, u32[]{:S(2)}, u32[]{:S(2)}) collective-permute-start(f32[2,16,128]{2,1,0:T(8,128)S(1)} %get-tuple-element.38.refs_0_), channel_id=1, source_target_pairs={{0,32},{1,33},{2,34},{3,35},{4,36},{5,37},{6,38},{7,39},{8,40},{9,... | collective-permute-start | bytes 49160 | tf_op jit(solution)/shard_map/ppermute | solution.py:21
  10.7 1.6 %collective-permute-start.7 = (f32[3,16,16]{2,1,0:T(8,128)S(1)}, f32[3,16,16]{2,1,0:T(8,128)S(1)}, u32[]{:S(2)}, u32[]{:S(2)}) collective-permute-start(f32[3,16,16]{2,1,0:T(8,128)S(1)} %shard_map.82.refs_0_), channel_id=1, source_target_pairs={{0,1},{1,0},{2,3},{3,2},{4,5},{5,4},{6,7},{7,6},{8,9},{9,8},{10,11... | collective-permute-start | bytes 9224 | tf_op jit(solution)/shard_map/ppermute | solution.py:21
  12.3 10.8 %collective-permute-start.2 = (f32[256,128]{1,0:T(8,128)S(1)}, f32[256,128]{1,0:T(8,128)S(1)}, u32[]{:S(2)}, u32[]{:S(2)}) collective-permute-start(f32[256,128]{1,0:T(8,128)S(1)} %shard_map.80.refs_8_.ev.ow), channel_id=1, source_target_pairs={{0,2},{2,0},{4,6},{6,4},{8,10},{10,8},{12,14},{14,12},{16,18},{18,... | collective-permute-start | bytes 393224 | tf_op jit(solution)/shard_map/ppermute | solution.py:21
  14.1 5.5 %collective-permute-start.5 = (f32[16,1,128]{2,1,0:T(1,128)S(1)}, f32[16,1,128]{2,1,0:T(1,128)S(1)}, u32[]{:S(2)}, u32[]{:S(2)}) collective-permute-start(f32[16,1,128]{2,1,0:T(1,128)S(1)} %get-tuple-element.40), channel_id=1, source_target_pairs={{0,2},{1,3},{2,0},{3,1},{4,6},{5,7},{6,4},{7,5},{8,10},{9,11},{10,... | collective-permute-start | bytes 24584 | tf_op jit(solution)/shard_map/ppermute | solution.py:21
  15.3 6.0 %collective-permute-start.6 = (f32[16,1,128]{2,1,0:T(1,128)S(1)}, f32[16,1,128]{2,1,0:T(1,128)S(1)}, u32[]{:S(2)}, u32[]{:S(2)}) collective-permute-start(f32[16,1,128]{2,1,0:T(1,128)S(1)} %get-tuple-element.41), channel_id=1, source_target_pairs={{2,4},{3,5},{6,8},{7,9},{10,12},{11,13},{14,16},{15,17},{18,20},{1... | collective-permute-start | bytes 24584 | tf_op jit(solution)/shard_map/ppermute | solution.py:21
  23.0 8.1 %collective-permute-start.14 = (f32[1024,128]{1,0:T(8,128)S(1)}, f32[1024,128]{1,0:T(8,128)S(1)}, u32[]{:S(2)}, u32[]{:S(2)}) collective-permute-start(f32[1024,128]{1,0:T(8,128)S(1)} %get-tuple-element.50), channel_id=1, source_target_pairs={{0,1},{1,0},{2,3},{3,2},{4,5},{5,4},{6,7},{7,6},{8,9},{9,8},{10,11... | collective-permute-start | bytes 1572872 | tf_op jit(solution)/shard_map/ppermute | solution.py:21
  23.2 3.9 %collective-permute-start.10 = (f32[256,128]{1,0:T(8,128)S(1)}, f32[256,128]{1,0:T(8,128)S(1)}, u32[]{:S(2)}, u32[]{:S(2)}) collective-permute-start(f32[256,128]{1,0:T(8,128)S(1)} %get-tuple-element.44.ev.od), channel_id=1, source_target_pairs={{1,3},{3,1},{5,7},{7,5},{9,11},{11,9},{13,15},{15,13},{17,19},{19,... | collective-permute-start | bytes 393224 | tf_op jit(solution)/shard_map/ppermute | solution.py:21
  23.3 3.8 %collective-permute-start.11 = (f32[256,128]{1,0:T(8,128)S(1)}, f32[256,128]{1,0:T(8,128)S(1)}, u32[]{:S(2)}, u32[]{:S(2)}) collective-permute-start(f32[256,128]{1,0:T(8,128)S(1)} %get-tuple-element.45.te), channel_id=1, source_target_pairs={{0,1},{1,0},{2,3},{3,2},{4,5},{5,4},{6,7},{7,6},{8,9},{9,8},{10,11... | collective-permute-start | bytes 393224 | tf_op jit(solution)/shard_map/ppermute | solution.py:21
  27.6 5.1 %collective-permute-start.12 = (f32[256,128]{1,0:T(8,128)S(1)}, f32[256,128]{1,0:T(8,128)S(1)}, u32[]{:S(2)}, u32[]{:S(2)}) collective-permute-start(f32[256,128]{1,0:T(8,128)S(1)} %get-tuple-element.46.ev.od), channel_id=1, source_target_pairs={{1,7},{3,5},{5,3},{7,1},{9,15},{11,13},{13,11},{15,9},{17,23},{19,... | collective-permute-start | bytes 393224 | tf_op jit(solution)/shard_map/ppermute | solution.py:21
  28.7 4.1 %collective-permute-start.13 = (f32[256,128]{1,0:T(8,128)S(1)}, f32[256,128]{1,0:T(8,128)S(1)}, u32[]{:S(2)}, u32[]{:S(2)}) collective-permute-start(f32[256,128]{1,0:T(8,128)S(1)} %get-tuple-element.48.go.te), channel_id=1, source_target_pairs={{0,1},{1,0},{2,3},{3,2},{4,5},{5,4},{6,7},{7,6},{8,9},{9,8},{10,11... | collective-permute-start | bytes 393224 | tf_op jit(solution)/shard_map/ppermute | solution.py:21
  33.3 5.3 %collective-permute-start.15 = (f32[256,128]{1,0:T(8,128)S(1)}, f32[256,128]{1,0:T(8,128)S(1)}, u32[]{:S(2)}, u32[]{:S(2)}) collective-permute-start(f32[256,128]{1,0:T(8,128)S(1)} %get-tuple-element.51.ev.od), channel_id=1, source_target_pairs={{1,9},{3,11},{5,13},{7,15},{9,1},{11,3},{13,5},{15,7},{17,25},{19,... | collective-permute-start | bytes 393224 | tf_op jit(solution)/shard_map/ppermute | solution.py:21
  34.1 4.9 %collective-permute-start.16 = (f32[256,128]{1,0:T(8,128)S(1)}, f32[256,128]{1,0:T(8,128)S(1)}, u32[]{:S(2)}, u32[]{:S(2)}) collective-permute-start(f32[256,128]{1,0:T(8,128)S(1)} %get-tuple-element.53.go.te), channel_id=1, source_target_pairs={{0,1},{1,0},{2,3},{3,2},{4,5},{5,4},{6,7},{7,6},{8,9},{9,8},{10,11... | collective-permute-start | bytes 393224 | tf_op jit(solution)/shard_map/ppermute | solution.py:21
  39.6 5.1 %collective-permute-start.17 = (f32[256,128]{1,0:T(8,128)S(1)}, f32[256,128]{1,0:T(8,128)S(1)}, u32[]{:S(2)}, u32[]{:S(2)}) collective-permute-start(f32[256,128]{1,0:T(8,128)S(1)} %get-tuple-element.54.ev.od), channel_id=1, source_target_pairs={{1,25},{3,27},{5,29},{7,31},{9,17},{11,19},{13,21},{15,23},{17,9},... | collective-permute-start | bytes 393224 | tf_op jit(solution)/shard_map/ppermute | solution.py:21
  40.8 3.9 %collective-permute-start.18 = (f32[256,128]{1,0:T(8,128)S(1)}, f32[256,128]{1,0:T(8,128)S(1)}, u32[]{:S(2)}, u32[]{:S(2)}) collective-permute-start(f32[256,128]{1,0:T(8,128)S(1)} %get-tuple-element.56.go.te), channel_id=1, source_target_pairs={{0,1},{1,0},{2,3},{3,2},{4,5},{5,4},{6,7},{7,6},{8,9},{9,8},{10,11... | collective-permute-start | bytes 393224 | tf_op jit(solution)/shard_map/ppermute | solution.py:21
  45.2 4.3 %collective-permute-start.19 = (f32[256,128]{1,0:T(8,128)S(1)}, f32[256,128]{1,0:T(8,128)S(1)}, u32[]{:S(2)}, u32[]{:S(2)}) collective-permute-start(f32[256,128]{1,0:T(8,128)S(1)} %get-tuple-element.57.ev.od), channel_id=1, source_target_pairs={{1,33},{3,35},{5,37},{7,39},{9,41},{11,43},{13,45},{15,47},{17,49}... | collective-permute-start | bytes 393224 | tf_op jit(solution)/shard_map/ppermute | solution.py:21
  46.2 3.7 %collective-permute-start.20 = (f32[256,128]{1,0:T(8,128)S(1)}, f32[256,128]{1,0:T(8,128)S(1)}, u32[]{:S(2)}, u32[]{:S(2)}) collective-permute-start(f32[256,128]{1,0:T(8,128)S(1)} %get-tuple-element.59.go.te), channel_id=1, source_target_pairs={{0,1},{1,0},{2,3},{3,2},{4,5},{5,4},{6,7},{7,6},{8,9},{9,8},{10,11... | collective-permute-start | bytes 393224 | tf_op jit(solution)/shard_map/ppermute | solution.py:21
  50.5 8.0 %collective-permute-start.21 = (f32[256,128]{1,0:T(8,128)S(1)}, f32[256,128]{1,0:T(8,128)S(1)}, u32[]{:S(2)}, u32[]{:S(2)}) collective-permute-start(f32[256,128]{1,0:T(8,128)S(1)} %get-tuple-element.60.ev.od), channel_id=1, source_target_pairs={{1,65},{3,67},{5,69},{7,71},{9,73},{11,75},{13,77},{15,79},{17,81}... | collective-permute-start | bytes 393224 | tf_op jit(solution)/shard_map/ppermute | solution.py:21
  54.4 4.1 %collective-permute-start.22 = (f32[256,128]{1,0:T(8,128)S(1)}, f32[256,128]{1,0:T(8,128)S(1)}, u32[]{:S(2)}, u32[]{:S(2)}) collective-permute-start(f32[256,128]{1,0:T(8,128)S(1)} %get-tuple-element.62.go.te), channel_id=1, source_target_pairs={{0,1},{1,0},{2,3},{3,2},{4,5},{5,4},{6,7},{7,6},{8,9},{9,8},{10,11... | collective-permute-start | bytes 393224 | tf_op jit(solution)/shard_map/ppermute | solution.py:21
  59.0 1.5 %collective-permute-start.24 = (f32[384,128]{1,0:T(8,128)S(1)}, f32[384,128]{1,0:T(8,128)S(1)}, u32[]{:S(2)}, u32[]{:S(2)}) collective-permute-start(f32[384,128]{1,0:T(8,128)S(1)} %get-tuple-element.64), channel_id=1, source_target_pairs={{0,1},{1,0},{2,3},{3,2},{4,5},{5,4},{6,7},{7,6},{8,9},{9,8},{10,11... | collective-permute-start | bytes 589832 | tf_op jit(solution)/shard_map/ppermute | solution.py:21
  59.1 5.4 %collective-permute-start.23 = (f32[128,128]{1,0:T(8,128)S(1)}, f32[128,128]{1,0:T(8,128)S(1)}, u32[]{:S(2)}, u32[]{:S(2)}) collective-permute-start(f32[128,128]{1,0:T(8,128)S(1)} %get-tuple-element.63), channel_id=1, source_target_pairs={{0,192},{1,193},{2,194},{3,195},{4,196},{5,197},{6,198},{7,199},{8... | collective-permute-start | bytes 196616 | tf_op jit(solution)/shard_map/ppermute | solution.py:21
  64.5 2.6 %collective-permute-start.25 = (f32[128,128]{1,0:T(8,128)S(1)}, f32[128,128]{1,0:T(8,128)S(1)}, u32[]{:S(2)}, u32[]{:S(2)}) collective-permute-start(f32[128,128]{1,0:T(8,128)S(1)} %shard_map.99.c), channel_id=1, source_target_pairs={{0,1},{1,0},{2,3},{3,2},{4,5},{5,4},{6,7},{7,6},{8,9},{9,8},{10,11... | collective-permute-start | bytes 196616 | tf_op jit(solution)/shard_map/ppermute | solution.py:21

commit v4 on v3

--- a/solution.py
+++ b/solution.py
@@ -344,17 +344,28 @@
 
 
 def finish(comes, swapped, response, samples, mine, sent):
-    def kernel(c, sw, resp, s, mi, se, white, grad):
+    def kernel(c, sw, resp, s, mi, se, white, grad, held, sem):
         v = c[...] + sw[...]
         r = resp[...].reshape(2 * W, 2 * W)
         w = r[:, W:] + product(r[:, :W], v)
-        white[...] = w.reshape(16, 16, W)
+        held[...] = w.reshape(16, 16, W)
+        copy = pltpu.make_async_copy(held, white, sem)
+        copy.start()
         lap = jnp.where(bit(1), mi[: 4 * W], se[: 4 * W])
         for at, factor in enumerate((s[...].reshape(2 * W, W), lap[: 2 * W], lap[2 * W :])):
             grad[at] = jnp.sum((w * factor).reshape(16, 16, W), axis=2) * (1.0 / W)
-
-    outs = [shaped(16, 16, W), shaped(3, 16, 16)]
-    return call(kernel, outs, comes, swapped, response, samples, mine, sent)
+        copy.wait()
+
+    vmem = pl.BlockSpec(memory_space=pltpu.VMEM)
+    return pl.pallas_call(
+        kernel,
+        out_shape=[shaped(16, 16, W), shaped(3, 16, 16)],
+        in_specs=[vmem] * 6,
+        out_specs=[pl.BlockSpec(memory_space=pltpu.HBM), vmem],
+        scratch_shapes=[pltpu.VMEM((16, 16, W), F32), pltpu.SemaphoreType.DMA],
+        compiler_params=pltpu.CompilerParams(vmem_limit_bytes=16 << 20),
+        cost_estimate=pl.CostEstimate(flops=40000000, bytes_accessed=1400000, transcendentals=0),
+    )(comes, swapped, response, samples, mine, sent)
 
 
 LEVELS = ((1, 1), (2, 2), (4, 6), (8, 8), (16, 24), (32, 32), (64, 64), (128, 192))

time: 68.2 us -> 69 us (1.012)
    pallas_call x0 -> x1, Pallas kernels: none -> 1.53 us  [finish(): pl.pallas_call(kernel, out_shape=[shaped(16, 16, W), shaped(3, 16, 16)],...]
    pallas_call x23 -> x22, Pallas kernels: 11.8 us -> 10.9 us  [call(): pl.pallas_call(kernel, out_shape=outs, in_specs=[vmem] * len(operands), o...]
where the time goes in v4:
time: 69 us; the launch traced here: 68.8 us
  starting transfers between devices  41 us (59%)
  Pallas kernels  13.5 us (20%)
  waiting for transfers between devices  13.3 us (19%)
  between operations  1.08 us (2%)
    ppermute x26, starting transfers between devices, send(): return lax.ppermute(array, EVERY, pairs)  41 us
    ppermute x26, waiting for transfers between devices, send(): return lax.ppermute(array, EVERY, pairs)  13.3 us
    pallas_call x22, Pallas kernels, call(): pl.pallas_call(kernel, out_shape=outs, in_specs=[vmem] * len(operands), o...  10.9 us
    pallas_call x1, Pallas kernels, finish(): pl.pallas_call(kernel, out_shape=[shaped(16, 16, W), shaped(3, 16, 16)],...  1.53 us
  transfers between devices with their start and end apart: 26, of which 11 were waited for; matrix products, arithmetic and copies ran while one was open for 0% of the time, Pallas kernels for 12%

profile of v4, /device:TPU:1, one launch (start us, length us, event | category | flops | bytes accessed | tf_op | source)
XLA Modules:
  0.0 68.8 jit_solution(5562877311190398647)
XLA Ops:
  0.6 1.1 %shard_map.77 = (f32[16,16,128]{2,1,0:T(8,128)S(1)}, f32[1,2,128,128]{3,2,1,0:T(8,128)S(1)}, f32[1,2,128,128]{3,2,1,0:T(8,128)S(1)}) custom-call(f32[16,16,128]{2,1,0:T(8,128)} %s.1, f32[1,2,128,128]{3,2,1,0:T(8,128)} %inv.1, f32[1,2,128,128]{3,2,1,0:T(8,128)} %cou.1), custom_call_target="tpu_custom_call" | custom-call | flops 1 | bytes 800000 | tf_op jit(solution)/shard_map/pallas_call | solution.py:119
  1.7 3.3 %collective-permute-start.1 = (f32[16,16,128]{2,1,0:T(8,128)S(1)}, f32[16,16,128]{2,1,0:T(8,128)S(1)}, u32[]{:S(2)}, u32[]{:S(2)}) collective-permute-start(f32[16,16,128]{2,1,0:T(8,128)S(1)} %get-tuple-element.37.odd.so.s), channel_id=1, source_target_pairs={{0,1},{1,0},{2,3},{3,2},{4,5},{5,4},{6,7},{7,6},{8,9},{9,8},{10,11... | collective-permute-start | bytes 393224 | tf_op jit(solution)/shard_map/ppermute | solution.py:21
  5.0 0.9 %shard_map.78 = (f32[2,128,128]{2,1,0:T(8,128)S(1)}, f32[256,128]{1,0:T(8,128)S(1)}) custom-call(f32[1,2,128,128]{3,2,1,0:T(8,128)S(1)} %get-tuple-element.34.inv.refs_2_, f32[1,2,128,128]{3,2,1,0:T(8,128)S(1)} %get-tuple-element.35.cou), custom_call_target="tpu_custom_call" | custom-call | flops 30000000 | bytes 524288 | tf_op jit(solution)/shard_map/pallas_call | solution.py:31
  6.0 0.1 collective-permute-start
  6.1 0.5 collective-permute-start.8
  6.6 0.1 collective-permute-start.9
  6.7 0.0 collective-permute-done.1.even.se
  6.7 3.9 %collective-permute-start.4 = (f32[2,16,128]{2,1,0:T(8,128)S(1)}, f32[2,16,128]{2,1,0:T(8,128)S(1)}, u32[]{:S(2)}, u32[]{:S(2)}) collective-permute-start(f32[2,16,128]{2,1,0:T(8,128)S(1)} %get-tuple-element.39), channel_id=1, source_target_pairs={{32,64},{33,65},{34,66},{35,67},{36,68},{37,69},{38,70},{39,71},{4... | collective-permute-start | bytes 49160 | tf_op jit(solution)/shard_map/ppermute | solution.py:21
  10.6 0.0 collective-permute-start.3
  10.7 0.0 collective-permute-done.p.refs_7_.m
  10.7 0.8 %collective-permute-start.7 = (f32[3,16,16]{2,1,0:T(8,128)S(1)}, f32[3,16,16]{2,1,0:T(8,128)S(1)}, u32[]{:S(2)}, u32[]{:S(2)}) collective-permute-start(f32[3,16,16]{2,1,0:T(8,128)S(1)} %shard_map.82.refs_0_), channel_id=1, source_target_pairs={{0,1},{1,0},{2,3},{3,2},{4,5},{5,4},{6,7},{7,6},{8,9},{9,8},{10,11... | collective-permute-start | bytes 9224 | tf_op jit(solution)/shard_map/ppermute | solution.py:21
  11.5 0.4 shard_map.80.refs_8_.ev.ow
  11.9 0.5 collective-permute-done.7.refs_1_
  12.3 1.7 %collective-permute-start.2 = (f32[256,128]{1,0:T(8,128)S(1)}, f32[256,128]{1,0:T(8,128)S(1)}, u32[]{:S(2)}, u32[]{:S(2)}) collective-permute-start(f32[256,128]{1,0:T(8,128)S(1)} %shard_map.80.refs_8_.ev.ow), channel_id=1, source_target_pairs={{0,2},{2,0},{4,6},{6,4},{8,10},{10,8},{12,14},{14,12},{16,18},{18,... | collective-permute-start | bytes 393224 | tf_op jit(solution)/shard_map/ppermute | solution.py:21
  14.0 0.0 collective-permute-done.8.refs_3_
  14.1 1.2 %collective-permute-start.5 = (f32[16,1,128]{2,1,0:T(1,128)S(1)}, f32[16,1,128]{2,1,0:T(1,128)S(1)}, u32[]{:S(2)}, u32[]{:S(2)}) collective-permute-start(f32[16,1,128]{2,1,0:T(1,128)S(1)} %get-tuple-element.40), channel_id=1, source_target_pairs={{0,2},{1,3},{2,0},{3,1},{4,6},{5,7},{6,4},{7,5},{8,10},{9,11},{10,... | collective-permute-start | bytes 24584 | tf_op jit(solution)/shard_map/ppermute | solution.py:21
  15.3 0.0 collective-permute-done.9.refs_5_
  15.3 4.3 %collective-permute-start.6 = (f32[16,1,128]{2,1,0:T(1,128)S(1)}, f32[16,1,128]{2,1,0:T(1,128)S(1)}, u32[]{:S(2)}, u32[]{:S(2)}) collective-permute-start(f32[16,1,128]{2,1,0:T(1,128)S(1)} %get-tuple-element.41), channel_id=1, source_target_pairs={{2,4},{3,5},{6,8},{7,9},{10,12},{11,13},{14,16},{15,17},{18,20},{1... | collective-permute-start | bytes 24584 | tf_op jit(solution)/shard_map/ppermute | solution.py:21
  19.6 1.7 %collective-permute-done.6.y2 = f32[16,1,128]{2,1,0:T(1,128)S(1)} collective-permute-done((f32[16,1,128]{2,1,0:T(1,128)S(1)}, f32[16,1,128]{2,1,0:T(1,128)S(1)}, u32[]{:S(2)}, u32[]{:S(2)}) %collective-permute-start.6) | collective-permute-done | bytes 8224 | tf_op jit(solution)/shard_map/ppermute | solution.py:21
  21.3 0.0 collective-permute-done.4.x2
  21.3 0.0 collective-permute-done.3.x1
  21.3 1.8 %shard_map.83 = (f32[1024,128]{1,0:T(8,128)S(1)}, f32[1024,128]{1,0:T(8,128)S(1)}, f32[256,128]{1,0:T(8,128)S(1)}) custom-call(f32[16,16,128]{2,1,0:T(8,128)S(1)} %get-tuple-element.37.odd.so.s, f32[16,16,128]{2,1,0:T(8,128)S(1)} %collective-permute-done.1.even.se, f32[2,16,128]{2,1,0:T(8,128)S(1)} %collective-permute-done.3.x1, ...), custom_call_target="tpu_custom_call" | custom-call | flops 1300000000 | bytes 2414592 | tf_op jit(solution)/shard_map/pallas_call | solution.py:31
  23.0 0.1 collective-permute-start.14
  23.2 0.1 collective-permute-start.10
  23.3 1.5 %collective-permute-start.11 = (f32[256,128]{1,0:T(8,128)S(1)}, f32[256,128]{1,0:T(8,128)S(1)}, u32[]{:S(2)}, u32[]{:S(2)}) collective-permute-start(f32[256,128]{1,0:T(8,128)S(1)} %get-tuple-element.45.te), channel_id=1, source_target_pairs={{0,1},{1,0},{2,3},{3,2},{4,5},{5,4},{6,7},{7,6},{8,9},{9,8},{10,11... | collective-permute-start | bytes 393224 | tf_op jit(solution)/shard_map/ppermute | solution.py:21
  24.8 2.3 %collective-permute-done.10.g = f32[256,128]{1,0:T(8,128)S(1)} collective-permute-done((f32[256,128]{1,0:T(8,128)S(1)}, f32[256,128]{1,0:T(8,128)S(1)}, u32[]{:S(2)}, u32[]{:S(2)}) %collective-permute-start.10) | collective-permute-done | bytes 131104 | tf_op jit(solution)/shard_map/ppermute | solution.py:21
  27.1 0.5 shard_map.85
  27.6 1.0 %collective-permute-start.12 = (f32[256,128]{1,0:T(8,128)S(1)}, f32[256,128]{1,0:T(8,128)S(1)}, u32[]{:S(2)}, u32[]{:S(2)}) collective-permute-start(f32[256,128]{1,0:T(8,128)S(1)} %get-tuple-element.46.ev.od), channel_id=1, source_target_pairs={{1,7},{3,5},{5,3},{7,1},{9,15},{11,13},{13,11},{15,9},{17,23},{19,... | collective-permute-start | bytes 393224 | tf_op jit(solution)/shard_map/ppermute | solution.py:21
  28.7 2.5 %collective-permute-start.13 = (f32[256,128]{1,0:T(8,128)S(1)}, f32[256,128]{1,0:T(8,128)S(1)}, u32[]{:S(2)}, u32[]{:S(2)}) collective-permute-start(f32[256,128]{1,0:T(8,128)S(1)} %get-tuple-element.48.go.te), channel_id=1, source_target_pairs={{0,1},{1,0},{2,3},{3,2},{4,5},{5,4},{6,7},{7,6},{8,9},{9,8},{10,11... | collective-permute-start | bytes 393224 | tf_op jit(solution)/shard_map/ppermute | solution.py:21
  31.2 0.0 collective-permute-done.14.se
  31.2 1.6 %collective-permute-done.12.g = f32[256,128]{1,0:T(8,128)S(1)} collective-permute-done((f32[256,128]{1,0:T(8,128)S(1)}, f32[256,128]{1,0:T(8,128)S(1)}, u32[]{:S(2)}, u32[]{:S(2)}) %collective-permute-start.12) | collective-permute-done | bytes 131104 | tf_op jit(solution)/shard_map/ppermute | solution.py:21
  32.8 0.0 collective-permute-done.13.th.ge.to
  32.8 0.5 shard_map.87
  33.3 0.8 %collective-permute-start.15 = (f32[256,128]{1,0:T(8,128)S(1)}, f32[256,128]{1,0:T(8,128)S(1)}, u32[]{:S(2)}, u32[]{:S(2)}) collective-permute-start(f32[256,128]{1,0:T(8,128)S(1)} %get-tuple-element.51.ev.od), channel_id=1, source_target_pairs={{1,9},{3,11},{5,13},{7,15},{9,1},{11,3},{13,5},{15,7},{17,25},{19,... | collective-permute-start | bytes 393224 | tf_op jit(solution)/shard_map/ppermute | solution.py:21
  34.1 3.9 %collective-permute-start.16 = (f32[256,128]{1,0:T(8,128)S(1)}, f32[256,128]{1,0:T(8,128)S(1)}, u32[]{:S(2)}, u32[]{:S(2)}) collective-permute-start(f32[256,128]{1,0:T(8,128)S(1)} %get-tuple-element.53.go.te), channel_id=1, source_target_pairs={{0,1},{1,0},{2,3},{3,2},{4,5},{5,4},{6,7},{7,6},{8,9},{9,8},{10,11... | collective-permute-start | bytes 393224 | tf_op jit(solution)/shard_map/ppermute | solution.py:21
  38.0 0.5 shard_map.88.refs_0_.s
  38.6 0.4 collective-permute-done.16.th.ge.to
  39.0 0.5 shard_map.89
  39.6 1.2 %collective-permute-start.17 = (f32[256,128]{1,0:T(8,128)S(1)}, f32[256,128]{1,0:T(8,128)S(1)}, u32[]{:S(2)}, u32[]{:S(2)}) collective-permute-start(f32[256,128]{1,0:T(8,128)S(1)} %get-tuple-element.54.ev.od), channel_id=1, source_target_pairs={{1,25},{3,27},{5,29},{7,31},{9,17},{11,19},{13,21},{15,23},{17,9},... | collective-permute-start | bytes 393224 | tf_op jit(solution)/shard_map/ppermute | solution.py:21
  40.8 2.3 %collective-permute-start.18 = (f32[256,128]{1,0:T(8,128)S(1)}, f32[256,128]{1,0:T(8,128)S(1)}, u32[]{:S(2)}, u32[]{:S(2)}) collective-permute-start(f32[256,128]{1,0:T(8,128)S(1)} %get-tuple-element.56.go.te), channel_id=1, source_target_pairs={{0,1},{1,0},{2,3},{3,2},{4,5},{5,4},{6,7},{7,6},{8,9},{9,8},{10,11... | collective-permute-start | bytes 393224 | tf_op jit(solution)/shard_map/ppermute | solution.py:21
  43.1 0.5 shard_map.90.refs_0_.s
  43.6 1.1 %collective-permute-done.17.g = f32[256,128]{1,0:T(8,128)S(1)} collective-permute-done((f32[256,128]{1,0:T(8,128)S(1)}, f32[256,128]{1,0:T(8,128)S(1)}, u32[]{:S(2)}, u32[]{:S(2)}) %collective-permute-start.17) | collective-permute-done | bytes 131104 | tf_op jit(solution)/shard_map/ppermute | solution.py:21
  44.7 0.5 shard_map.91
  45.2 1.0 %collective-permute-start.19 = (f32[256,128]{1,0:T(8,128)S(1)}, f32[256,128]{1,0:T(8,128)S(1)}, u32[]{:S(2)}, u32[]{:S(2)}) collective-permute-start(f32[256,128]{1,0:T(8,128)S(1)} %get-tuple-element.57.ev.od), channel_id=1, source_target_pairs={{1,33},{3,35},{5,37},{7,39},{9,41},{11,43},{13,45},{15,47},{17,49}... | collective-permute-start | bytes 393224 | tf_op jit(solution)/shard_map/ppermute | solution.py:21
  46.2 2.7 %collective-permute-start.20 = (f32[256,128]{1,0:T(8,128)S(1)}, f32[256,128]{1,0:T(8,128)S(1)}, u32[]{:S(2)}, u32[]{:S(2)}) collective-permute-start(f32[256,128]{1,0:T(8,128)S(1)} %get-tuple-element.59.go.te), channel_id=1, source_target_pairs={{0,1},{1,0},{2,3},{3,2},{4,5},{5,4},{6,7},{7,6},{8,9},{9,8},{10,11... | collective-permute-start | bytes 393224 | tf_op jit(solution)/shard_map/ppermute | solution.py:21
  49.0 0.5 shard_map.92.refs_0_.s
  49.5 0.4 collective-permute-done.20.th.ge.to
  49.9 0.5 shard_map.93
  50.5 3.9 %collective-permute-start.21 = (f32[256,128]{1,0:T(8,128)S(1)}, f32[256,128]{1,0:T(8,128)S(1)}, u32[]{:S(2)}, u32[]{:S(2)}) collective-permute-start(f32[256,128]{1,0:T(8,128)S(1)} %get-tuple-element.60.ev.od), channel_id=1, source_target_pairs={{1,65},{3,67},{5,69},{7,71},{9,73},{11,75},{13,77},{15,79},{17,81}... | collective-permute-start | bytes 393224 | tf_op jit(solution)/shard_map/ppermute | solution.py:21
  54.4 2.0 %collective-permute-start.22 = (f32[256,128]{1,0:T(8,128)S(1)}, f32[256,128]{1,0:T(8,128)S(1)}, u32[]{:S(2)}, u32[]{:S(2)}) collective-permute-start(f32[256,128]{1,0:T(8,128)S(1)} %get-tuple-element.62.go.te), channel_id=1, source_target_pairs={{0,1},{1,0},{2,3},{3,2},{4,5},{5,4},{6,7},{7,6},{8,9},{9,8},{10,11... | collective-permute-start | bytes 393224 | tf_op jit(solution)/shard_map/ppermute | solution.py:21
  56.4 0.5 shard_map.94.refs_0_.s
  56.9 1.5 %collective-permute-done.21.g = f32[256,128]{1,0:T(8,128)S(1)} collective-permute-done((f32[256,128]{1,0:T(8,128)S(1)}, f32[256,128]{1,0:T(8,128)S(1)}, u32[]{:S(2)}, u32[]{:S(2)}) %collective-permute-start.21) | collective-permute-done | bytes 131104 | tf_op jit(solution)/shard_map/ppermute | solution.py:21
  58.5 0.0 collective-permute-done.22.th.ge.to
  58.5 0.5 shard_map.95
  59.0 0.1 collective-permute-start.24
  59.1 0.1 collective-permute-start.23
  59.2 0.5 shard_map.96.s
  59.8 0.8 %collective-permute-done.24.ge.sw = f32[384,128]{1,0:T(8,128)S(1)} collective-permute-done((f32[384,128]{1,0:T(8,128)S(1)}, f32[384,128]{1,0:T(8,128)S(1)}, u32[]{:S(2)}, u32[]{:S(2)}) %collective-permute-start.24) | collective-permute-done | bytes 196640 | tf_op jit(solution)/shard_map/ppermute | solution.py:21
  60.5 0.5 shard_map.97.ar
  61.1 1.3 %shard_map.98.refs_0_.resp = f32[2,128,256]{2,1,0:T(8,128)S(1)} custom-call(f32[3,128,256]{2,1,0:T(8,128)S(1)} %shard_map.97.ar, f32[1,2,128,128]{3,2,1,0:T(8,128)S(1)} %get-tuple-element.34.inv.refs_2_, f32[1,2,128,128]{3,2,1,0:T(8,128)S(1)} %get-tuple-element.35.cou, f32[1024,128]{1,0:T(8,128)S(1)} %get-tuple-element.49.mi, ...), custom_call_target="tpu_custom_call" | custom-call | flops 100000000 | bytes 2097152 | tf_op jit(solution)/shard_map/pallas_call | solution.py:31
  62.4 2.1 %collective-permute-done.23.g = f32[128,128]{1,0:T(8,128)S(1)} collective-permute-done((f32[128,128]{1,0:T(8,128)S(1)}, f32[128,128]{1,0:T(8,128)S(1)}, u32[]{:S(2)}, u32[]{:S(2)}) %collective-permute-start.23) | collective-permute-done | bytes 65568 | tf_op jit(solution)/shard_map/ppermute | solution.py:21
  64.5 1.7 %collective-permute-start.25 = (f32[128,128]{1,0:T(8,128)S(1)}, f32[128,128]{1,0:T(8,128)S(1)}, u32[]{:S(2)}, u32[]{:S(2)}) collective-permute-start(f32[128,128]{1,0:T(8,128)S(1)} %shard_map.99.c), channel_id=1, source_target_pairs={{0,1},{1,0},{2,3},{3,2},{4,5},{5,4},{6,7},{7,6},{8,9},{9,8},{10,11... | collective-permute-start | bytes 196616 | tf_op jit(solution)/shard_map/ppermute | solution.py:21
  66.3 0.9 %collective-permute-done.25.sw = f32[128,128]{1,0:T(8,128)S(1)} collective-permute-done((f32[128,128]{1,0:T(8,128)S(1)}, f32[128,128]{1,0:T(8,128)S(1)}, u32[]{:S(2)}, u32[]{:S(2)}) %collective-permute-start.25) | collective-permute-done | bytes 65568 | tf_op jit(solution)/shard_map/ppermute | solution.py:21
  67.2 1.5 %shard_map.100 = (f32[16,16,128]{2,1,0:T(8,128)}, f32[3,16,16]{2,1,0:T(8,128)}) custom-call(f32[128,128]{1,0:T(8,128)S(1)} %shard_map.99.c, f32[128,128]{1,0:T(8,128)S(1)} %collective-permute-done.25.sw, f32[2,128,256]{2,1,0:T(8,128)S(1)} %shard_map.98.refs_0_.resp, f32[16,16,128]{2,1,0:T(8,128)S(1)} %get-tuple-element.37.odd.so.s, ...), custom_call_target="tpu_custom_call" | custom-call | flops 40000000 | bytes 1400000 | tf_op jit(solution)/shard_map/pallas_call | solution.py:360
  (18 shorter events, 0.1 us)
Async XLA Ops:
  1.7 5.0 %collective-permute-start.1 = (f32[16,16,128]{2,1,0:T(8,128)S(1)}, f32[16,16,128]{2,1,0:T(8,128)S(1)}, u32[]{:S(2)}, u32[]{:S(2)}) collective-permute-start(f32[16,16,128]{2,1,0:T(8,128)S(1)} %get-tuple-element.37.odd.so.s), channel_id=1, source_target_pairs={{0,1},{1,0},{2,3},{3,2},{4,5},{5,4},{6,7},{7,6},{8,9},{9,8},{10,11... | collective-permute-start | bytes 393224 | tf_op jit(solution)/shard_map/ppermute | solution.py:21
  6.0 4.7 %collective-permute-start = (f32[256,128]{1,0:T(8,128)S(1)}, f32[256,128]{1,0:T(8,128)S(1)}, u32[]{:S(2)}, u32[]{:S(2)}) collective-permute-start(f32[256,128]{1,0:T(8,128)S(1)} %get-tuple-element.36.t.refs_6_), channel_id=1, source_target_pairs={{0,1},{1,0},{2,3},{3,2},{4,5},{5,4},{6,7},{7,6},{8,9},{9,8},{10,11... | collective-permute-start | bytes 393224 | tf_op jit(solution)/shard_map/ppermute | solution.py:21
  6.1 8.0 %collective-permute-start.8 = (f32[1,2,128,128]{3,2,1,0:T(8,128)S(1)}, f32[1,2,128,128]{3,2,1,0:T(8,128)S(1)}, u32[]{:S(2)}, u32[]{:S(2)}) collective-permute-start(f32[1,2,128,128]{3,2,1,0:T(8,128)S(1)} %get-tuple-element.34.inv.refs_2_), channel_id=1, source_target_pairs={{0,1},{1,0},{2,3},{3,2},{4,5},{5,4},{6,7},{7,6},{8,9},{9,8},{10,11... | collective-permute-start | bytes 393224 | tf_op jit(solution)/shard_map/ppermute | solution.py:21
  6.6 8.7 %collective-permute-start.9 = (f32[2,128,128]{2,1,0:T(8,128)S(1)}, f32[2,128,128]{2,1,0:T(8,128)S(1)}, u32[]{:S(2)}, u32[]{:S(2)}) collective-permute-start(f32[2,128,128]{2,1,0:T(8,128)S(1)} %get-tuple-element.42.refs_4_.st), channel_id=1, source_target_pairs={{0,1},{1,0},{2,3},{3,2},{4,5},{5,4},{6,7},{7,6},{8,9},{9,8},{10,11... | collective-permute-start | bytes 393224 | tf_op jit(solution)/shard_map/ppermute | solution.py:21
  6.7 4.0 %copy-start = (f32[16,16]{1,0:T(8,128)S(1)}, f32[16,16]{1,0:T(8,128)}, u32[]{:S(2)}) copy-start(f32[16,16]{1,0:T(8,128)} %re.1) | copy-start | bytes 3076
  6.7 4.0 %copy-start.1 = (f32[16,16]{1,0:T(8,128)S(1)}, f32[16,16]{1,0:T(8,128)}, u32[]{:S(2)}) copy-start(f32[16,16]{1,0:T(8,128)} %wx.1) | copy-start | bytes 3076
  6.7 4.0 %copy-start.2 = (f32[16,16]{1,0:T(8,128)S(1)}, f32[16,16]{1,0:T(8,128)}, u32[]{:S(2)}) copy-start(f32[16,16]{1,0:T(8,128)} %wy.1) | copy-start | bytes 3076
  6.7 14.6 %collective-permute-start.4 = (f32[2,16,128]{2,1,0:T(8,128)S(1)}, f32[2,16,128]{2,1,0:T(8,128)S(1)}, u32[]{:S(2)}, u32[]{:S(2)}) collective-permute-start(f32[2,16,128]{2,1,0:T(8,128)S(1)} %get-tuple-element.39), channel_id=1, source_target_pairs={{32,64},{33,65},{34,66},{35,67},{36,68},{37,69},{38,70},{39,71},{4... | collective-permute-start | bytes 49160 | tf_op jit(solution)/shard_map/ppermute | solution.py:21
  10.6 10.6 %collective-permute-start.3 = (f32[2,16,128]{2,1,0:T(8,128)S(1)}, f32[2,16,128]{2,1,0:T(8,128)S(1)}, u32[]{:S(2)}, u32[]{:S(2)}) collective-permute-start(f32[2,16,128]{2,1,0:T(8,128)S(1)} %get-tuple-element.38.refs_0_), channel_id=1, source_target_pairs={{0,32},{1,33},{2,34},{3,35},{4,36},{5,37},{6,38},{7,39},{8,40},{9,... | collective-permute-start | bytes 49160 | tf_op jit(solution)/shard_map/ppermute | solution.py:21
  10.7 1.6 %collective-permute-start.7 = (f32[3,16,16]{2,1,0:T(8,128)S(1)}, f32[3,16,16]{2,1,0:T(8,128)S(1)}, u32[]{:S(2)}, u32[]{:S(2)}) collective-permute-start(f32[3,16,16]{2,1,0:T(8,128)S(1)} %shard_map.82.refs_0_), channel_id=1, source_target_pairs={{0,1},{1,0},{2,3},{3,2},{4,5},{5,4},{6,7},{7,6},{8,9},{9,8},{10,11... | collective-permute-start | bytes 9224 | tf_op jit(solution)/shard_map/ppermute | solution.py:21
  12.3 10.8 %collective-permute-start.2 = (f32[256,128]{1,0:T(8,128)S(1)}, f32[256,128]{1,0:T(8,128)S(1)}, u32[]{:S(2)}, u32[]{:S(2)}) collective-permute-start(f32[256,128]{1,0:T(8,128)S(1)} %shard_map.80.refs_8_.ev.ow), channel_id=1, source_target_pairs={{0,2},{2,0},{4,6},{6,4},{8,10},{10,8},{12,14},{14,12},{16,18},{18,... | collective-permute-start | bytes 393224 | tf_op jit(solution)/shard_map/ppermute | solution.py:21
  14.1 5.5 %collective-permute-start.5 = (f32[16,1,128]{2,1,0:T(1,128)S(1)}, f32[16,1,128]{2,1,0:T(1,128)S(1)}, u32[]{:S(2)}, u32[]{:S(2)}) collective-permute-start(f32[16,1,128]{2,1,0:T(1,128)S(1)} %get-tuple-element.40), channel_id=1, source_target_pairs={{0,2},{1,3},{2,0},{3,1},{4,6},{5,7},{6,4},{7,5},{8,10},{9,11},{10,... | collective-permute-start | bytes 24584 | tf_op jit(solution)/shard_map/ppermute | solution.py:21
  15.3 6.0 %collective-permute-start.6 = (f32[16,1,128]{2,1,0:T(1,128)S(1)}, f32[16,1,128]{2,1,0:T(1,128)S(1)}, u32[]{:S(2)}, u32[]{:S(2)}) collective-permute-start(f32[16,1,128]{2,1,0:T(1,128)S(1)} %get-tuple-element.41), channel_id=1, source_target_pairs={{2,4},{3,5},{6,8},{7,9},{10,12},{11,13},{14,16},{15,17},{18,20},{1... | collective-permute-start | bytes 24584 | tf_op jit(solution)/shard_map/ppermute | solution.py:21
  23.0 8.1 %collective-permute-start.14 = (f32[1024,128]{1,0:T(8,128)S(1)}, f32[1024,128]{1,0:T(8,128)S(1)}, u32[]{:S(2)}, u32[]{:S(2)}) collective-permute-start(f32[1024,128]{1,0:T(8,128)S(1)} %get-tuple-element.50), channel_id=1, source_target_pairs={{0,1},{1,0},{2,3},{3,2},{4,5},{5,4},{6,7},{7,6},{8,9},{9,8},{10,11... | collective-permute-start | bytes 1572872 | tf_op jit(solution)/shard_map/ppermute | solution.py:21
  23.2 3.9 %collective-permute-start.10 = (f32[256,128]{1,0:T(8,128)S(1)}, f32[256,128]{1,0:T(8,128)S(1)}, u32[]{:S(2)}, u32[]{:S(2)}) collective-permute-start(f32[256,128]{1,0:T(8,128)S(1)} %get-tuple-element.44.ev.od), channel_id=1, source_target_pairs={{1,3},{3,1},{5,7},{7,5},{9,11},{11,9},{13,15},{15,13},{17,19},{19,... | collective-permute-start | bytes 393224 | tf_op jit(solution)/shard_map/ppermute | solution.py:21
  23.3 3.8 %collective-permute-start.11 = (f32[256,128]{1,0:T(8,128)S(1)}, f32[256,128]{1,0:T(8,128)S(1)}, u32[]{:S(2)}, u32[]{:S(2)}) collective-permute-start(f32[256,128]{1,0:T(8,128)S(1)} %get-tuple-element.45.te), channel_id=1, source_target_pairs={{0,1},{1,0},{2,3},{3,2},{4,5},{5,4},{6,7},{7,6},{8,9},{9,8},{10,11... | collective-permute-start | bytes 393224 | tf_op jit(solution)/shard_map/ppermute | solution.py:21
  27.6 5.1 %collective-permute-start.12 = (f32[256,128]{1,0:T(8,128)S(1)}, f32[256,128]{1,0:T(8,128)S(1)}, u32[]{:S(2)}, u32[]{:S(2)}) collective-permute-start(f32[256,128]{1,0:T(8,128)S(1)} %get-tuple-element.46.ev.od), channel_id=1, source_target_pairs={{1,7},{3,5},{5,3},{7,1},{9,15},{11,13},{13,11},{15,9},{17,23},{19,... | collective-permute-start | bytes 393224 | tf_op jit(solution)/shard_map/ppermute | solution.py:21
  28.7 4.1 %collective-permute-start.13 = (f32[256,128]{1,0:T(8,128)S(1)}, f32[256,128]{1,0:T(8,128)S(1)}, u32[]{:S(2)}, u32[]{:S(2)}) collective-permute-start(f32[256,128]{1,0:T(8,128)S(1)} %get-tuple-element.48.go.te), channel_id=1, source_target_pairs={{0,1},{1,0},{2,3},{3,2},{4,5},{5,4},{6,7},{7,6},{8,9},{9,8},{10,11... | collective-permute-start | bytes 393224 | tf_op jit(solution)/shard_map/ppermute | solution.py:21
  33.3 5.3 %collective-permute-start.15 = (f32[256,128]{1,0:T(8,128)S(1)}, f32[256,128]{1,0:T(8,128)S(1)}, u32[]{:S(2)}, u32[]{:S(2)}) collective-permute-start(f32[256,128]{1,0:T(8,128)S(1)} %get-tuple-element.51.ev.od), channel_id=1, source_target_pairs={{1,9},{3,11},{5,13},{7,15},{9,1},{11,3},{13,5},{15,7},{17,25},{19,... | collective-permute-start | bytes 393224 | tf_op jit(solution)/shard_map/ppermute | solution.py:21
  34.1 4.9 %collective-permute-start.16 = (f32[256,128]{1,0:T(8,128)S(1)}, f32[256,128]{1,0:T(8,128)S(1)}, u32[]{:S(2)}, u32[]{:S(2)}) collective-permute-start(f32[256,128]{1,0:T(8,128)S(1)} %get-tuple-element.53.go.te), channel_id=1, source_target_pairs={{0,1},{1,0},{2,3},{3,2},{4,5},{5,4},{6,7},{7,6},{8,9},{9,8},{10,11... | collective-permute-start | bytes 393224 | tf_op jit(solution)/shard_map/ppermute | solution.py:21
  39.6 5.1 %collective-permute-start.17 = (f32[256,128]{1,0:T(8,128)S(1)}, f32[256,128]{1,0:T(8,128)S(1)}, u32[]{:S(2)}, u32[]{:S(2)}) collective-permute-start(f32[256,128]{1,0:T(8,128)S(1)} %get-tuple-element.54.ev.od), channel_id=1, source_target_pairs={{1,25},{3,27},{5,29},{7,31},{9,17},{11,19},{13,21},{15,23},{17,9},... | collective-permute-start | bytes 393224 | tf_op jit(solution)/shard_map/ppermute | solution.py:21
  40.8 3.9 %collective-permute-start.18 = (f32[256,128]{1,0:T(8,128)S(1)}, f32[256,128]{1,0:T(8,128)S(1)}, u32[]{:S(2)}, u32[]{:S(2)}) collective-permute-start(f32[256,128]{1,0:T(8,128)S(1)} %get-tuple-element.56.go.te), channel_id=1, source_target_pairs={{0,1},{1,0},{2,3},{3,2},{4,5},{5,4},{6,7},{7,6},{8,9},{9,8},{10,11... | collective-permute-start | bytes 393224 | tf_op jit(solution)/shard_map/ppermute | solution.py:21
  45.2 4.3 %collective-permute-start.19 = (f32[256,128]{1,0:T(8,128)S(1)}, f32[256,128]{1,0:T(8,128)S(1)}, u32[]{:S(2)}, u32[]{:S(2)}) collective-permute-start(f32[256,128]{1,0:T(8,128)S(1)} %get-tuple-element.57.ev.od), channel_id=1, source_target_pairs={{1,33},{3,35},{5,37},{7,39},{9,41},{11,43},{13,45},{15,47},{17,49}... | collective-permute-start | bytes 393224 | tf_op jit(solution)/shard_map/ppermute | solution.py:21
  46.2 3.7 %collective-permute-start.20 = (f32[256,128]{1,0:T(8,128)S(1)}, f32[256,128]{1,0:T(8,128)S(1)}, u32[]{:S(2)}, u32[]{:S(2)}) collective-permute-start(f32[256,128]{1,0:T(8,128)S(1)} %get-tuple-element.59.go.te), channel_id=1, source_target_pairs={{0,1},{1,0},{2,3},{3,2},{4,5},{5,4},{6,7},{7,6},{8,9},{9,8},{10,11... | collective-permute-start | bytes 393224 | tf_op jit(solution)/shard_map/ppermute | solution.py:21
  50.5 8.0 %collective-permute-start.21 = (f32[256,128]{1,0:T(8,128)S(1)}, f32[256,128]{1,0:T(8,128)S(1)}, u32[]{:S(2)}, u32[]{:S(2)}) collective-permute-start(f32[256,128]{1,0:T(8,128)S(1)} %get-tuple-element.60.ev.od), channel_id=1, source_target_pairs={{1,65},{3,67},{5,69},{7,71},{9,73},{11,75},{13,77},{15,79},{17,81}... | collective-permute-start | bytes 393224 | tf_op jit(solution)/shard_map/ppermute | solution.py:21
  54.4 4.1 %collective-permute-start.22 = (f32[256,128]{1,0:T(8,128)S(1)}, f32[256,128]{1,0:T(8,128)S(1)}, u32[]{:S(2)}, u32[]{:S(2)}) collective-permute-start(f32[256,128]{1,0:T(8,128)S(1)} %get-tuple-element.62.go.te), channel_id=1, source_target_pairs={{0,1},{1,0},{2,3},{3,2},{4,5},{5,4},{6,7},{7,6},{8,9},{9,8},{10,11... | collective-permute-start | bytes 393224 | tf_op jit(solution)/shard_map/ppermute | solution.py:21
  59.0 1.5 %collective-permute-start.24 = (f32[384,128]{1,0:T(8,128)S(1)}, f32[384,128]{1,0:T(8,128)S(1)}, u32[]{:S(2)}, u32[]{:S(2)}) collective-permute-start(f32[384,128]{1,0:T(8,128)S(1)} %get-tuple-element.64), channel_id=1, source_target_pairs={{0,1},{1,0},{2,3},{3,2},{4,5},{5,4},{6,7},{7,6},{8,9},{9,8},{10,11... | collective-permute-start | bytes 589832 | tf_op jit(solution)/shard_map/ppermute | solution.py:21
  59.1 5.4 %collective-permute-start.23 = (f32[128,128]{1,0:T(8,128)S(1)}, f32[128,128]{1,0:T(8,128)S(1)}, u32[]{:S(2)}, u32[]{:S(2)}) collective-permute-start(f32[128,128]{1,0:T(8,128)S(1)} %get-tuple-element.63), channel_id=1, source_target_pairs={{0,192},{1,193},{2,194},{3,195},{4,196},{5,197},{6,198},{7,199},{8... | collective-permute-start | bytes 196616 | tf_op jit(solution)/shard_map/ppermute | solution.py:21
  64.5 2.6 %collective-permute-start.25 = (f32[128,128]{1,0:T(8,128)S(1)}, f32[128,128]{1,0:T(8,128)S(1)}, u32[]{:S(2)}, u32[]{:S(2)}) collective-permute-start(f32[128,128]{1,0:T(8,128)S(1)} %shard_map.99.c), channel_id=1, source_target_pairs={{0,1},{1,0},{2,3},{3,2},{4,5},{5,4},{6,7},{7,6},{8,9},{9,8},{10,11... | collective-permute-start | bytes 196616 | tf_op jit(solution)/shard_map/ppermute | solution.py:21
